TPU v7x, 32 devices: a whole 2x2x4 slice. The times are simulated.
32 devices in a mesh: row: 8 (over y, x, core), col: 4 (over z).
Axes of the slice: x: 2, y: 2, z: 4, core: 2. Of those that a mesh axis runs over, the one named last changes fastest.
Arguments:
- tokens: bfloat16 [4, 4096, 1792], P(None, ('row', 'col')), may hold values from -12 to 12
- lengths: int32 [4, 8], replicated, may hold values from 1 to 1024, 4096 in all within a row
- permutation: int32 [4, 32], replicated, may hold values from 0 to 31, each once within a row
- cotangent: bfloat16 [4, 4096, 1792], P(None, ('row', 'col')), may hold values from -12 to 12
- norm1_gain: float32 [1792], replicated, may hold values from 0.5 to 1.5
- mixer_in: bfloat16 [1792, 1792], P('row', 'col'), may hold values from -0.125 to 0.125
- mixer_gate: bfloat16 [1792, 1792], P('row', 'col'), may hold values from -0.125 to 0.125
- conv_kernel: float32 [3, 1792], P(None, 'col'), may hold values from -2.5 to 2.5
- mixer_out: bfloat16 [1792, 1792], P('row', 'col'), may hold values from -0.125 to 0.125
- norm2_gain: float32 [1792], replicated, may hold values from 0.5 to 1.5
- ffn_gate: bfloat16 [1792, 4864], P('row', 'col'), may hold values from -0.125 to 0.125
- ffn_up: bfloat16 [1792, 4864], P('row', 'col'), may hold values from -0.125 to 0.125
- ffn_down: bfloat16 [1792, 4864], P('row', 'col'), may hold values from -0.078125 to 0.078125
Outputs:
- output: bfloat16 [4, 4096, 1792], P(None, ('row', 'col'))
- input_grad: float32 [4, 4096, 1792], P(None, ('row', 'col'))
- norm1_gain_grad: float32 [1792], P(('row', 'col'))
- mixer_in_grad: float32 [1792, 1792], P('row', 'col')
- mixer_gate_grad: float32 [1792, 1792], P('row', 'col')
- conv_kernel_grad: float32 [3, 1792], P(None, ('col', 'row'))
- mixer_out_grad: float32 [1792, 1792], P('row', 'col')
- norm2_gain_grad: float32 [1792], P(('row', 'col'))
- ffn_gate_grad: float32 [1792, 4864], P('row', 'col')
- ffn_up_grad: float32 [1792, 4864], P('row', 'col')
- ffn_down_grad: float32 [1792, 4864], P('row', 'col')
Inputs may be any that keep to these rules, and one draw needn't show every extreme that they name: Each row of lengths sums to 4096, and its largest entry is exactly 1024. `permutation`: each row holds every number of 0 to 31 once.
All inputs are finite; a program needn't handle non-finite values.
Results may differ from a plain program's by a relative error of at most 0.0083.
Values may be sent and summed in bfloat16 or wider, within the bound.
No kernel may reach another device: no remote copies, remote signals or barrier semaphores. Data moves between devices by JAX's collectives and lax.ppermute only.
A program may use at most 160 MiB of HBM per device.

v0:
```python
import functools

import jax
import jax.numpy as jnp
from jax import lax
from jax.experimental import pallas as pl
from jax.experimental.pallas import tpu as pltpu
from jax.sharding import Mesh
from jax.sharding import PartitionSpec as P

BLOCK = 128
EPSILON = 1e-05
F32 = jnp.float32
BF16 = jnp.bfloat16
EVERY = ("a", "b", "c", "z")


def dot_nn(left, right):
    return lax.dot_general(left, right, (((1,), (0,)), ((), ())), preferred_element_type=F32)


def dot_nt(left, right):
    return lax.dot_general(left, right, (((1,), (1,)), ((), ())), preferred_element_type=F32)


def dot_tn(left, right):
    return lax.dot_general(left, right, (((0,), (0,)), ((), ())), preferred_element_type=F32)


def shift_by(value, axis, amount):
    size = lax.axis_size(axis)
    return lax.ppermute(value, axis, [(i, (i + amount) % size) for i in range(size)])


def pieces_of(value, axis):
    return [value] + [shift_by(value, axis, s) for s in range(1, lax.axis_size(axis))]


def near_pieces(value, axis):
    return shift_by(value, axis, 1), shift_by(value, axis, -1)


def far_pieces(value, near, axis):
    size = lax.axis_size(axis)
    pieces = [value] + [None] * (size - 1)
    pieces[1], pieces[size - 1] = near
    for s in range(2, size // 2 + 1):
        pieces[s] = shift_by(pieces[s - 1], axis, 1)
    for s in range(2, (size - 1) // 2 + 1):
        pieces[size - s] = shift_by(pieces[size - s + 1], axis, -1)
    return pieces


def phase(*values):
    return lax.optimization_barrier(values)


def after(value, *earlier):
    return lax.optimization_barrier((value, earlier))[0]


def in_order(pieces, axis, dim):
    size, index = len(pieces), lax.axis_index(axis)
    if size == 2:
        first = index == 0
        return jnp.stack(
            [jnp.where(first, pieces[0], pieces[1]), jnp.where(first, pieces[1], pieces[0])], axis=dim
        )
    return jnp.stack(
        [lax.select_n((index - j) % size, *pieces) for j in range(size)], axis=dim
    )


def slices_of(terms, i, dim):
    return [lax.dynamic_index_in_dim(t, i, dim, keepdims=False) for t in terms]


def parted(terms, axis, dim, kind=BF16):
    size, index = lax.axis_size(axis), lax.axis_index(axis)
    return terms, [
        shift_by(joined(slices_of(terms, (index - s) % size, dim)).astype(kind), axis, -s) for s in range(1, size)
    ]


def settled(parts, axis, dim):
    terms, arrived = parts
    return slices_of(terms, lax.axis_index(axis), dim) + arrived


def joined(terms):
    total = terms[0].astype(F32)
    for value in terms[1:]:
        total = total + value.astype(F32)
    return total


def columns_home(terms):
    count = lax.axis_size("z")
    local = terms[0].shape[1] // count

    def columns(s):
        return joined([t[:, s * local : (s + 1) * local] for t in terms])

    return [columns(0)] + [shift_by(columns(s).astype(BF16), "z", -s) for s in range(1, count)]


def home(block):
    count, size = lax.axis_size("z"), lax.axis_size("b")
    moves = []
    for t in range(count):
        for z in range(count):
            team = (z % size) * 2 + z // size
            moves.append((team * count + t, t * count + z))
    return lax.ppermute(block, ("b", "c", "z"), moves)


def partner(value, bit):
    count = lax.axis_size(EVERY)
    return lax.ppermute(value, EVERY, [(i, i ^ bit) for i in range(count)])


def exchange_order():
    bits = [1 << i for i in range(lax.axis_size(EVERY).bit_length() - 1)]
    core = lax.axis_size("z")
    return [b for b in bits if b < core] + [b for b in bits[::-1] if b > core] + [core]


def entry_of(difference):
    return sum(((difference & bit) // bit) << i for i, bit in enumerate(exchange_order()))


def told(value, bits):
    for bit in bits:
        value = jnp.concatenate([value, partner(value, bit)], axis=0)
    return value


def first_kernel(steps, *refs):
    near_hidden, far_hidden, w_gate, w_up = refs[:4]
    gates, ups, activated = refs[-3:]
    near = pl.program_id(0) < steps
    hidden = jnp.where(near, near_hidden[...], far_hidden[...])
    gate = dot_nn(hidden, w_gate[...])
    up = dot_nn(hidden, w_up[...])
    gates[...] = gate.astype(BF16)
    ups[...] = up.astype(BF16)
    activated[...] = (gate * (1.0 / (1.0 + jnp.exp(-gate))) * up).astype(BF16)


def second_kernel(steps, *refs):
    near_cot, far_cot, gates, ups, activated, w_gate, w_up, w_down = refs[:8]
    grads, near_back, far_back, near_out, far_out = refs[-5:]
    units = w_down.shape[1]
    near = pl.program_id(0) < steps
    cot = jnp.where(near, near_cot[...], far_cot[...])
    grad = dot_nn(cot, w_down[...])
    gate, up = gates[...].astype(F32), ups[...].astype(F32)
    sigmoid = 1.0 / (1.0 + jnp.exp(-gate))
    to_gate = (grad * up * (sigmoid * (1.0 + gate * (1.0 - sigmoid)))).astype(BF16)
    to_up = (grad * (gate * sigmoid)).astype(BF16)
    grads[:, :units] = to_gate
    grads[:, units:] = to_up
    back = (dot_nt(to_gate, w_gate[...]) + dot_nt(to_up, w_up[...])).astype(BF16)
    out = dot_nt(activated[...], w_down[...]).astype(BF16)

    @pl.when(near)
    def _():
        near_back[...] = back
        near_out[...] = out

    @pl.when(jnp.logical_not(near))
    def _():
        far_back[...] = back
        far_out[...] = out


def feed_forward(second, part, parts, tokens, whole, weights, held):
    rows, width = tokens[0].shape
    units = weights[0].shape[1]
    tile = min(rows, 256)
    steps = rows // tile
    near = pl.BlockSpec((tile, width), lambda i: (jnp.minimum(i, steps - 1), 0))
    far = pl.BlockSpec((tile, width), lambda i: (jnp.maximum(i - steps, 0), 0))
    weight = pl.BlockSpec((width, units), lambda i: (0, 0), pipeline_mode=pl.Buffered(1))

    def of_whole(columns):
        return pl.BlockSpec((tile, columns), lambda i: (part * 2 * steps + i, 0))

    kept = (2 * units,) if second else (units,) * 3
    first_held = 2 + len(whole) + len(weights)
    products = 8 if second else 4
    return pl.pallas_call(
        functools.partial(second_kernel if second else first_kernel, steps),
        grid=(2 * steps,),
        in_specs=[near, far]
        + [of_whole(units)] * len(whole)
        + [weight] * len(weights)
        + [pl.BlockSpec(memory_space=pl.ANY)] * len(held),
        out_specs=[of_whole(n) for n in kept] + ([near, far] * 2 if second else []),
        out_shape=[jax.ShapeDtypeStruct((parts * 2 * rows, n), BF16) for n in kept]
        + [jax.ShapeDtypeStruct((rows, width), BF16)] * (4 if second else 0),
        input_output_aliases={first_held + i: i for i in range(len(held))},
        compiler_params=pltpu.CompilerParams(vmem_limit_bytes=58 * 2**20),
        cost_estimate=pl.CostEstimate(
            flops=2 * products * 2 * rows * width * units,
            bytes_accessed=2 * (2 * rows * width + len(weights) * width * units + 10 * rows * units),
            transcendentals=2 * rows * units,
        ),
        name="second_half" if second else "first_half",
    )(*tokens, *whole, *weights, *held)


def gradient_kernel(*refs, count, extra):
    side, tokens, right, result = refs[0], refs[1 : 1 + count], refs[1 + count], refs[-1]
    del side
    rows = tokens[0].shape[0]
    total = refs[2 + count][...].astype(F32) if extra else None
    for i in range(count):
        term = lax.dot_general(
            tokens[i][...], right[i * rows : (i + 1) * rows, :], (((0,), (0,)), ((), ())), preferred_element_type=F32
        )
        total = term if total is None else total + term
    result[...] = total.astype(BF16)


def gradient_half(side, tokens, right, units, column=0, extra=()):
    rows, width = tokens[0].shape
    count, half = len(tokens), width // 2
    tile = 256 if units % 256 == 0 else 128
    steps = units // tile
    out = pl.BlockSpec((half, tile), lambda j, side: (0, j))
    return pl.pallas_call(
        functools.partial(gradient_kernel, count=count, extra=len(extra)),
        grid_spec=pltpu.PrefetchScalarGridSpec(
            num_scalar_prefetch=1,
            grid=(steps,),
            in_specs=[
                pl.BlockSpec((rows, half), lambda j, side: (0, side[0]), pipeline_mode=pl.Buffered(1))
            ]
            * count
            + [pl.BlockSpec((count * rows, tile), lambda j, side: (0, column * steps + j))]
            + [out] * len(extra),
            out_specs=out,
        ),
        out_shape=jax.ShapeDtypeStruct((half, units), BF16),
        compiler_params=pltpu.CompilerParams(vmem_limit_bytes=40 * 2**20),
        cost_estimate=pl.CostEstimate(
            flops=2 * count * rows * half * units,
            bytes_accessed=2 * (count * rows * (half + units) + half * units),
            transcendentals=0,
        ),
        name="gradient_half",
    )(side.reshape(1).astype(jnp.int32), *tokens, right, *extra)


def split_kernel(core, left, right, kept, leaving):
    total = lax.dot_general(left[...], right[...], (((0,), (0,)), ((), ())), preferred_element_type=F32)
    groups, _, rows, _ = (kept.shape[0], 2, *kept.shape[1:])
    total = total.astype(BF16).reshape(groups, 2, rows, -1)
    first = core[0] == 0
    kept[...] = jnp.where(first, total[:, 0], total[:, 1])
    leaving[...] = jnp.where(first, total[:, 1], total[:, 0])


def split_gradient(core, left, right, groups):
    count, width = left.shape
    columns = right.shape[1]
    tile = 256
    rows = width // (2 * groups)
    out = pl.BlockSpec((groups, rows, tile), lambda j, core: (0, 0, j))
    return pl.pallas_call(
        split_kernel,
        grid_spec=pltpu.PrefetchScalarGridSpec(
            num_scalar_prefetch=1,
            grid=(columns // tile,),
            in_specs=[
                pl.BlockSpec((count, width), lambda j, core: (0, 0), pipeline_mode=pl.Buffered(1)),
                pl.BlockSpec((count, tile), lambda j, core: (0, j)),
            ],
            out_specs=[out, out],
        ),
        out_shape=[jax.ShapeDtypeStruct((groups, rows, columns), BF16)] * 2,
        compiler_params=pltpu.CompilerParams(vmem_limit_bytes=40 * 2**20),
        cost_estimate=pl.CostEstimate(
            flops=2 * count * width * columns,
            bytes_accessed=2 * (count * (width + columns) + width * columns),
            transcendentals=0,
        ),
        name="split_gradient",
    )(core.reshape(1).astype(jnp.int32), left, right)


def per_device(
    tokens,
    lengths,
    permutation,
    cotangent,
    norm1_gain,
    mixer_in,
    mixer_gate,
    conv_kernel,
    mixer_out,
    norm2_gain,
    ffn_gate,
    ffn_up,
    ffn_down,
):
    micro, length, width = tokens.shape
    count_b, count_z = lax.axis_size("b"), lax.axis_size("z")
    ia, ib, ic, iz = (lax.axis_index(n) for n in EVERY)
    place = ((ia * count_b + ib) * 2 + ic) * count_z + iz
    per_block = BLOCK // length
    blocks = permutation.shape[1]
    local = conv_kernel.shape[1]
    rows = micro * length

    dealt = lax.dynamic_slice_in_dim(permutation, place // per_block, 1, axis=1)[:, 0]
    own = dealt * per_block + place % per_block
    spots = jnp.arange(blocks, dtype=jnp.int32)

    def holder(piece):
        at = jnp.sum(jnp.where(permutation == (piece // per_block)[:, None], spots[None, :], 0), axis=1)
        return at * per_block + piece % per_block

    before = holder(jnp.maximum(own - 1, 0))
    last = blocks * per_block - 1
    behind = holder(jnp.minimum(own + 1, last))
    order = jnp.arange(lengths.shape[1], dtype=jnp.int32)
    offsets = jnp.sum(jnp.where(order[None, None, :] < order[None, :, None], lengths[:, None, :], 0), axis=2)
    position = own[:, None] * length + jnp.arange(length, dtype=jnp.int32)[None, :]
    is_start = jnp.any(position[:, :, None] == offsets[:, None, :], axis=2)
    was_start = jnp.any(position[:, :, None] - 1 == offsets[:, None, :], axis=2)
    keep_one = jnp.where(is_start, 0.0, 1.0).astype(F32)[:, :, None]
    keep_two = jnp.where(is_start | was_start, 0.0, 1.0).astype(F32)[:, :, None]

    units = -(-ffn_gate.shape[1] // 128) * 128
    spare = ((0, 0), (0, units - ffn_gate.shape[1]))

    def rows_of(pieces):
        return lax.all_gather(jnp.concatenate(pieces, axis=1), ("a", "b", "c"), axis=0, tiled=True)

    def told_at_once(value):
        return lax.all_gather(lax.all_gather(value, "z", axis=0), ("a", "b", "c"), axis=0)

    def in_plane(value):
        value = value.reshape(2, count_b, *value.shape[1:])
        mine = lax.dynamic_index_in_dim(value, ic, 0, keepdims=False)
        far = shift_by(lax.dynamic_index_in_dim(value, 1 - ic, 0, keepdims=False), "c", 1)
        value = in_order([mine, far], "c", 1)
        pieces = [lax.dynamic_index_in_dim(value, ib, 0, keepdims=False)]
        for s in range(1, count_b):
            leaving = lax.dynamic_index_in_dim(value, (ib + s) % count_b, 0, keepdims=False)
            pieces.append(shift_by(leaving, "b", s))
        return pieces

    def plane_rows(pieces):
        value = in_order(pieces, "b", 0)
        return value.reshape(-1, *value.shape[2:])

    bits = exchange_order()
    tap_count = conv_kernel.size
    told_rows = jnp.concatenate(
        [
            tokens[:, length - 2 :, :].reshape(micro * 2, width).astype(F32),
            jnp.pad(conv_kernel.reshape(1, tap_count), ((0, 0), (0, width - tap_count))),
        ]
    )[None]
    pad_g, pad_u, pad_d = (jnp.pad(w, spare) for w in (ffn_gate, ffn_up, ffn_down))
    z_in = pieces_of(mixer_in, "z")
    told_rows = told(told_rows, bits[:-3])
    far_cotangent = pieces_of(cotangent.reshape(rows, width), "b")
    before_at = [entry_of(before[m] ^ place) for m in range(micro)]
    behind_at = [(behind[m] // count_z, behind[m] % count_z) for m in range(micro)]
    z_in, told_rows, far_cotangent, mixer_gate, mixer_out, pad_g, before_at, behind_at = phase(
        z_in, told_rows, far_cotangent, mixer_gate, mixer_out, pad_g, before_at, behind_at
    )
    w_in = rows_of(z_in)
    z_gate = pieces_of(mixer_gate, "z")
    near_g = near_pieces(pad_g, "z")
    z_gate, near_g, told_rows, mixer_out, pad_u, pad_d = phase(z_gate, near_g, told_rows, mixer_out, pad_u, pad_d)
    w_gate = rows_of(z_gate)
    z_out = pieces_of(mixer_out, "z")
    z_g = far_pieces(pad_g, near_g, "z")
    told_rows = told(told_rows, bits[-3:-2])
    z_out, z_g, told_rows, pad_u, pad_d, w_in = phase(z_out, z_g, told_rows, pad_u, pad_d, w_in)
    w_out = rows_of(z_out)
    plane_g = in_plane(in_order(z_g, "z", 0))
    z_u = pieces_of(pad_u, "z")
    told_rows = told(told_rows, bits[-2:])
    plane_g, z_u, told_rows, pad_d, w_gate = phase(plane_g, z_u, told_rows, pad_d, w_gate)
    y_g = pieces_of(plane_rows(plane_g), "a")
    plane_u = in_plane(in_order(z_u, "z", 0))
    z_d = pieces_of(pad_d, "z")
    kernel = jnp.concatenate(
        [
            lax.dynamic_slice(
                told_rows, (entry_of(place ^ (place - iz + (iz - s) % count_z)), micro * 2, 0), (1, 1, tap_count)
            ).reshape(3, local)
            for s in range(count_z)
        ],
        axis=1,
    )
    y_g, plane_u, z_d, w_out = phase(y_g, plane_u, z_d, w_out)
    y_u = pieces_of(plane_rows(plane_u), "a")
    plane_d = in_plane(in_order(z_d, "z", 0))
    ffn_g = in_order(y_g, "a", 0).reshape(-1, units)

    tail_in = jnp.concatenate(
        [
            lax.dynamic_slice(told_rows, (before_at[m], 2 * m, 0), (1, 2, width))[0]
            for m in range(micro)
        ]
    )
    local_in = tokens.reshape(rows, width).astype(F32)
    local_cot = cotangent.reshape(rows, width).astype(F32)
    scale_one = lax.rsqrt(jnp.mean(local_in * local_in, axis=1, keepdims=True) + EPSILON)
    normed_one = local_in * scale_one
    hidden_one = (normed_one * norm1_gain).astype(BF16)
    tail_scale = lax.rsqrt(jnp.mean(tail_in * tail_in, axis=1, keepdims=True) + EPSILON)
    tail_hidden = (tail_in * tail_scale * norm1_gain).astype(BF16)
    channels = kernel.shape[1]
    signal = dot_nn(hidden_one, w_in).reshape(micro, length, channels)
    tail_signal = dot_nn(tail_hidden, w_in).reshape(micro, 2, channels)
    gating = dot_nn(hidden_one, w_gate).reshape(micro, length, channels)
    extended = jnp.concatenate([tail_signal, signal], axis=1)
    shift_one = keep_one * extended[:, 1 : length + 1, :]
    shift_two = keep_two * extended[:, 0:length, :]
    mixed = kernel[0] * signal + kernel[1] * shift_one + kernel[2] * shift_two
    product = (mixed * gating).astype(BF16).reshape(rows, channels)
    residual = local_in + dot_nt(product, w_out)

    scale_two = lax.rsqrt(jnp.mean(residual * residual, axis=1, keepdims=True) + EPSILON)
    normed_two = residual * scale_two
    hidden_own = (normed_two * norm2_gain).astype(BF16)


    def with_core(pieces):
        return [v for piece in pieces for v in (piece, shift_by(piece, "c", 1))]

    plane_d, y_u, ffn_g, hidden_own = phase(plane_d, y_u, ffn_g, hidden_own)
    y_d = pieces_of(plane_rows(plane_d), "a")
    ffn_u = in_order(y_u, "a", 0).reshape(-1, units)
    far_hidden = pieces_of(hidden_own, "b")[1:]
    hidden_parts = with_core([hidden_own])
    kept = feed_forward(False, 0, count_b, hidden_parts, (), (ffn_g, ffn_u), ())
    y_d, far_hidden, kept = phase(y_d, far_hidden, kept)
    hidden_parts = hidden_parts + with_core(far_hidden)
    for s in range(1, count_b):
        kept = feed_forward(False, s, count_b, hidden_parts[2 * s : 2 * s + 2], (), (ffn_g, ffn_u), kept)
    gates, ups, activated = kept
    ffn_d = in_order(y_d, "a", 0).reshape(-1, units)
    cot_parts = with_core(far_cotangent)
    other = 1 - ia
    leaving_down = gradient_half(other, cot_parts, activated, units)
    leaving_down, cot_parts, hidden_parts = phase(leaving_down, cot_parts, hidden_parts)
    come_down = shift_by(leaving_down, "a", 1)
    held, backs, outs = (), [None] * count_b, [None] * count_b
    for s in reversed(range(count_b)):
        pair = cot_parts[2 * s : 2 * s + 2]
        *held, near_back, far_back, near_out, far_out = feed_forward(
            True, s, count_b, pair, (gates, ups, activated), (ffn_g, ffn_u, ffn_d), held
        )
        backs[s] = (near_back, shift_by(far_back, "c", 1))
        outs[s] = (near_out, shift_by(far_out, "c", 1))
    grads = held[0]

    def to_owners(sums):
        return [(near.astype(F32) + far.astype(F32)).astype(BF16) for near, far in sums]

    def passed(values):
        return [shift_by(v, "b", -1 - i) for i, v in enumerate(values)]

    def over_z(stay, come):
        return lax.psum_scatter(joined([stay, come]).astype(BF16), "z", scatter_dimension=0, tiled=True)

    leaving_gate = gradient_half(other, hidden_parts, grads, units)
    own_back, own_out = backs[0], outs[0]
    leaving_gate, come_down, far_backs, far_outs, hidden_parts, cot_parts = phase(
        leaving_gate, come_down, backs[1:], outs[1:], hidden_parts, cot_parts
    )
    come_gate, came_back = shift_by(leaving_gate, "a", 1), passed(to_owners(far_backs))
    leaving_up = gradient_half(other, hidden_parts, grads, units, 1)
    stay_down = gradient_half(ia, cot_parts, activated, units)
    stay_gate = gradient_half(ia, hidden_parts, grads, units)
    stay_up = gradient_half(ia, hidden_parts, grads, units, 1)
    leaving_out = to_owners(far_outs)
    scattered_down = over_z(stay_down, come_down)
    come_gate, came_back, leaving_up, stay_gate, stay_up, own_back, own_out, leaving_out = phase(
        come_gate, came_back, leaving_up, stay_gate, stay_up, own_back, own_out, leaving_out
    )
    come_up, came_out = shift_by(leaving_up, "a", 1), passed(leaving_out)
    scattered_gate = over_z(stay_gate, come_gate)
    grad_hidden_two = joined([*own_back, *came_back])

    grad_gain_two = jnp.sum(grad_hidden_two * normed_two, axis=0)
    grad_norm_two = grad_hidden_two * norm2_gain
    inner_two = jnp.mean(grad_norm_two * normed_two, axis=1, keepdims=True)
    grad_residual = local_cot + scale_two * (grad_norm_two - normed_two * inner_two)
    grad_branch = grad_residual.astype(BF16)
    grad_product = dot_nn(grad_branch, w_out).reshape(micro, length, channels)
    def over_c(split):
        kept, leaving = split
        shape = (2, count_b, *kept.shape[1:])
        return [kept.reshape(shape), shift_by(leaving, "c", 1).reshape(shape)]

    def split(left, right):
        return split_gradient(ic, left, right, 2 * count_b)

    out_split = split(grad_branch, product)
    grad_mixed = grad_product * gating
    grad_gating = (grad_product * mixed).astype(BF16).reshape(rows, channels)
    grad_kernel = jnp.stack(
        [
            jnp.sum(grad_mixed * signal, axis=(0, 1)),
            jnp.sum(grad_mixed * shift_one, axis=(0, 1)),
            jnp.sum(grad_mixed * shift_two, axis=(0, 1)),
        ]
    )
    into_one = kernel[1] * (keep_one * grad_mixed)
    into_two = kernel[2] * (keep_two * grad_mixed)
    leaving = jnp.stack([into_two[:, 0], into_one[:, 0] + into_two[:, 1]], axis=1)
    blocked = leaving.reshape(micro, 2, count_z, local)

    def turned(value, dim):
        picks = [
            lax.dynamic_index_in_dim(value, (iz - j) % count_z, dim, keepdims=False) for j in range(count_z)
        ]
        return jnp.concatenate(picks, axis=-1)

    blocked = turned(blocked, 2).reshape(micro * 2, channels).astype(BF16)
    gate_split = split(hidden_one, grad_gating)
    from_gating = dot_nt(grad_gating, w_gate)
    blocked, come_up, came_out, out_split, gate_split, grad_mixed, from_gating, scattered_down = phase(
        blocked, come_up, came_out, out_split, gate_split, grad_mixed, from_gating, scattered_down
    )
    everyone = told_at_once(blocked)
    out_c, gate_c = over_c(out_split), over_c(gate_split)
    everyone, out_c, gate_c, grad_mixed, scattered_gate, scattered_down, come_up = phase(
        everyone, out_c, gate_c, grad_mixed, scattered_gate, scattered_down, come_up
    )
    scattered_up = over_z(stay_up, come_up)
    out_b = parted(out_c, "b", 1)
    gate_a = parted(gate_c, "a", 0)
    down_home = home(scattered_down)
    into_one = kernel[1] * (keep_one * grad_mixed)
    into_two = kernel[2] * (keep_two * grad_mixed)
    arrived = jnp.stack(
        [
            lax.dynamic_slice(
                everyone, (*behind_at[m], 2 * m, 0), (1, 1, 2, channels)
            )[0, 0]
            for m in range(micro)
        ]
    )
    arrived = turned(arrived.reshape(micro, 2, count_z, local), 2).astype(F32)
    arrived = jnp.where((own == last)[:, None, None], 0.0, arrived)
    from_one = jnp.concatenate([into_one[:, 1:], arrived[:, 1:]], axis=1)
    from_two = jnp.concatenate([into_two[:, 2:], arrived[:, :1], jnp.zeros_like(arrived[:, :1])], axis=1)
    grad_signal = (kernel[0] * grad_mixed + from_one + from_two).astype(BF16).reshape(rows, channels)
    in_split = split(hidden_one, grad_signal)
    grad_hidden_one = dot_nt(grad_signal, w_in) + from_gating
    grad_gain_one = jnp.sum(grad_hidden_one * normed_one, axis=0)
    grad_norm_one = grad_hidden_one * norm1_gain
    inner_one = jnp.mean(grad_norm_one * normed_one, axis=1, keepdims=True)
    input_grad = grad_residual + scale_one * (grad_norm_one - normed_one * inner_one)
    out_b, gate_a, in_split, input_grad, down_home, scattered_gate, grad_gain_one, own_out = phase(
        out_b, gate_a, in_split, input_grad, down_home, scattered_gate, grad_gain_one, own_out
    )
    in_c = over_c(in_split)
    middle = channels // 128 * 5 // 7 * 128
    in_a = parted([t[..., :middle] for t in in_c], "a", 0)
    in_b = parted([t[..., middle:] for t in in_c], "b", 1)
    gate_b = parted(settled(gate_a, "a", 0), "b", 0)
    out_a = parted(settled(out_b, "b", 1), "a", 0)
    gate_home, up_home = home(scattered_gate), home(scattered_up)
    by_place = (2, count_b, 2, count_z, -1)
    both_gains = jnp.stack([g.reshape(by_place) for g in (grad_gain_one, grad_gain_two)], axis=3)
    kernel_parts = turned(grad_kernel.reshape(3, count_z, local), 1).reshape(3, count_z, 2, count_b, 2, -1)
    small = jnp.concatenate([both_gains, kernel_parts.transpose(2, 3, 4, 0, 1, 5)], axis=3)
    small = parted([small], "c", 2, F32)
    in_a, in_b, gate_b, out_a, gate_home, up_home, down_home, own_out, small = phase(
        in_a, in_b, gate_b, out_a, gate_home, up_home, down_home, own_out, small
    )
    small = parted(settled(small, "c", 2), "a", 0, F32)
    small = parted(settled(small, "a", 0), "b", 0, F32)
    in_a, in_b = parted(settled(in_a, "a", 0), "b", 0), parted(settled(in_b, "b", 1), "a", 0)
    two_z = columns_home([jnp.concatenate([joined(settled(out_a, "a", 0)), joined(settled(gate_b, "b", 0))], axis=0)])
    in_a, in_b, two_z, small, own_out = phase(in_a, in_b, two_z, small, own_out)
    output = (joined([*own_out, *came_out]) + residual).astype(BF16)
    small = joined(settled(small, "b", 0))
    share = small.shape[2]
    small = turned(jnp.pad(small, ((0, 3), (0, 0), (0, local - share))), 1)
    in_rows = jnp.concatenate([joined(settled(in_a, "b", 0)), joined(settled(in_b, "a", 0))], axis=1)
    in_z = columns_home([jnp.concatenate([in_rows, small], axis=0)])
    grad_out, grad_gate_w = jnp.split(joined(two_z), 2)
    in_z = joined(in_z)
    grad_in_w, small = in_z[: in_rows.shape[0]], in_z[in_rows.shape[0] :, :share]
    hidden_units = ffn_gate.shape[1]
    grad_ffg, grad_ffu, grad_down = (g[:, :hidden_units].astype(F32) for g in (gate_home, up_home, down_home))

    return (
        output.reshape(micro, length, width),
        input_grad.reshape(micro, length, width),
        small[0],
        grad_in_w,
        grad_gate_w,
        small[2:5],
        grad_out,
        small[1],
        grad_ffg,
        grad_ffu,
        grad_down,
    )


def solution(mesh):
    row, col = mesh.shape["row"], mesh.shape["col"]
    fine = Mesh(mesh.devices.reshape(2, row // 4, 2, col), EVERY)
    by_rows = ("a", "b", "c")
    matrix = P(by_rows, "z")
    token = P(None, EVERY, None)
    return jax.shard_map(
        per_device,
        mesh=fine,
        in_specs=(
            token,
            P(),
            P(),
            token,
            P(),
            matrix,
            matrix,
            P(None, "z"),
            matrix,
            P(),
            matrix,
            matrix,
            matrix,
        ),
        out_specs=(
            token,
            token,
            P(EVERY),
            matrix,
            matrix,
            P(None, ("z", *by_rows)),
            matrix,
            P(EVERY),
            matrix,
            matrix,
            matrix,
        ),
        check_vma=False,
    )
```

profile of v0, /device:TPU:30, one launch (start us, length us, event | category | flops | bytes accessed | tf_op | source)
XLA Modules:
  0.0 839.3 jit_solution(12893578967549526197)
XLA Ops:
  15.7 9.6 %collective-permute-done.3 = f32[1,9,1792]{2,1,0:T(8,128)S(1)} collective-permute-done((f32[1,9,1792]{2,1,0:T(8,128)S(1)}, f32[1,9,1792]{2,1,0:T(8,128)S(1)}, u32[]{:S(2)}, u32[]{:S(2)}) %collective-permute-start.3) | collective-permute-done | bytes 64544 | tf_op jit(solution)/shard_map/ppermute | solution.py:119
  43.2 6.2 collective-permute-done.5.refs_3_.refs_0_
  57.9 25.4 %collective-permute-done.6 = bf16[224,448]{1,0:T(8,128)(2,1)S(1)} collective-permute-done((bf16[224,448]{1,0:T(8,128)(2,1)S(1)}, bf16[224,448]{1,0:T(8,128)(2,1)S(1)}, u32[]{:S(2)}, u32[]{:S(2)}) %collective-permute-start.6) | collective-permute-done | bytes 200736 | tf_op jit(solution)/shard_map/ppermute | solution.py:32
  83.4 13.9 %collective-permute-done.7 = bf16[224,448]{1,0:T(8,128)(2,1)S(1)} collective-permute-done((bf16[224,448]{1,0:T(8,128)(2,1)S(1)}, bf16[224,448]{1,0:T(8,128)(2,1)S(1)}, u32[]{:S(2)}, u32[]{:S(2)}) %collective-permute-start.7) | collective-permute-done | bytes 200736 | tf_op jit(solution)/shard_map/ppermute | solution.py:32
  104.3 6.6 collective-permute-done.15
  111.0 7.8 collective-permute-done.11
  118.9 15.6 %collective-permute-done.12 = bf16[224,448]{1,0:T(8,128)(2,1)} collective-permute-done((bf16[224,448]{1,0:T(8,128)(2,1)}, bf16[224,448]{1,0:T(8,128)(2,1)}, u32[]{:S(2)}, u32[]{:S(2)}) %collective-permute-start.12) | collective-permute-done | bytes 200736 | tf_op jit(solution)/shard_map/ppermute | solution.py:32
  145.8 10.8 %collective-permute-done.21 = f32[8,9,1792]{2,0,1:T(8,128)} collective-permute-done((f32[8,9,1792]{2,0,1:T(8,128)S(1)}, f32[8,9,1792]{2,0,1:T(8,128)}, u32[]{:S(2)}, u32[]{:S(2)}) %collective-permute-start.21) | collective-permute-done | bytes 516128 | tf_op jit(solution)/shard_map/ppermute | solution.py:119
  164.0 8.2 fusion.2
  174.8 18.8 %collective-permute-done.19 = bf16[224,1280]{1,0:T(8,128)(2,1)} collective-permute-done((bf16[224,1280]{1,0:T(8,128)(2,1)}, bf16[224,1280]{1,0:T(8,128)(2,1)}, u32[]{:S(2)}, u32[]{:S(2)}) %collective-permute-start.19) | collective-permute-done | bytes 573472 | tf_op jit(solution)/shard_map/ppermute | solution.py:32
  193.7 13.2 %collective-permute-done.17 = bf16[2,224,1280]{2,1,0:T(8,128)(2,1)} collective-permute-done((bf16[2,224,1280]{2,1,0:T(8,128)(2,1)}, bf16[2,224,1280]{2,1,0:T(8,128)(2,1)}, u32[]{:S(2)}, u32[]{:S(2)}) %collective-permute-start.17) | collective-permute-done | bytes 1146912 | tf_op jit(solution)/shard_map/ppermute | solution.py:32
  224.2 9.0 %multiply_convert_fusion.2 = (bf16[4,128,1792]{2,1,0:T(8,128)(2,1)S(1)}, f32[4,128,1792]{2,1,0:T(8,128)}, f32[4,128,1792]{2,1,0:T(8,128)}) fusion(f32[4,128,1792]{2,1,0:T(8,128)S(1)} %copy-done.43, f32[4,2,1792]{2,1,0:T(2,128)S(1)} %reshape.405, f32[4,128]{1,0:T(4,128)S(1)} %get-tuple-element.521, f32[1792]{0:T(1024)S(1)} %get-tuple-element.426, ...), kind=kOutput, calls=%fused_computation.57 | convolution fusion | flops 3302096896 | bytes 21194752 | tf_op jit(solution)/shard_map/dot_general | solution.py:19
  233.3 24.5 %collective-permute-done.27 = bf16[224,1280]{1,0:T(8,128)(2,1)} collective-permute-done((bf16[224,1280]{1,0:T(8,128)(2,1)}, bf16[224,1280]{1,0:T(8,128)(2,1)}, u32[]{:S(2)}, u32[]{:S(2)}) %collective-permute-start.27) | collective-permute-done | bytes 573472 | tf_op jit(solution)/shard_map/ppermute | solution.py:32
  257.8 11.8 %collective-permute-done.23 = bf16[4,224,1280]{2,1,0:T(8,128)(2,1)} collective-permute-done((bf16[4,224,1280]{2,1,0:T(8,128)(2,1)}, bf16[4,224,1280]{2,1,0:T(8,128)(2,1)}, u32[]{:S(2)}, u32[]{:S(2)}) %collective-permute-start.23) | collective-permute-done | bytes 2293792 | tf_op jit(solution)/shard_map/ppermute | solution.py:32
  275.1 3.7 multiply_reduce_fusion.5
  278.8 4.0 select_bitcast_fusion.5
  287.5 23.2 %collective-permute-done.32 = bf16[2,224,1280]{2,1,0:T(8,128)(2,1)S(1)} collective-permute-done((bf16[2,224,1280]{2,1,0:T(8,128)(2,1)S(1)}, bf16[2,224,1280]{2,1,0:T(8,128)(2,1)S(1)}, u32[]{:S(2)}, u32[]{:S(2)}) %collective-permute-start.32) | collective-permute-done | bytes 1146912 | tf_op jit(solution)/shard_map/ppermute | solution.py:32
  310.6 15.3 %collective-permute-done.33 = bf16[4,224,1280]{2,1,0:T(8,128)(2,1)S(1)} collective-permute-done((bf16[4,224,1280]{2,1,0:T(8,128)(2,1)S(1)}, bf16[4,224,1280]{2,1,0:T(8,128)(2,1)S(1)}, u32[]{:S(2)}, u32[]{:S(2)}) %collective-permute-start.33) | collective-permute-done | bytes 2293792 | tf_op jit(solution)/shard_map/ppermute | solution.py:32
  332.9 15.5 %first_half.2 = (bf16[2048,1280]{1,0:T(8,128)(2,1)}, bf16[2048,1280]{1,0:T(8,128)(2,1)}, bf16[2048,1280]{1,0:T(8,128)(2,1)}) custom-call(bf16[512,1792]{1,0:T(8,128)(2,1)} %copy-done, bf16[512,1792]{1,0:T(8,128)(2,1)} %copy-done.2, bf16[1792,1280]{1,0:T(8,128)(2,1)} %bitcast.340, bf16[1792,1280]{1,0:T(8,128)(2,1)} %bitcast.344), custom_call_target="tpu_custom_call" | custom-call | flops 18790481920 | bytes 25952256 | tf_op jit(solution)/shard_map/first_half/pallas_call | solution.py:192
  348.5 19.0 %collective-permute-done.35.refs_0_.refs_3_ = bf16[512,1792]{1,0:T(8,128)(2,1)} collective-permute-done((bf16[512,1792]{1,0:T(8,128)(2,1)S(1)}, bf16[512,1792]{1,0:T(8,128)(2,1)}, u32[]{:S(2)}, u32[]{:S(2)}) %collective-permute-start.35) | collective-permute-done | bytes 1835040 | tf_op jit(solution)/shard_map/ppermute | solution.py:32
  367.5 12.7 %collective-permute-done.34 = bf16[4,224,1280]{2,1,0:T(8,128)(2,1)} collective-permute-done((bf16[4,224,1280]{2,1,0:T(8,128)(2,1)S(1)}, bf16[4,224,1280]{2,1,0:T(8,128)(2,1)}, u32[]{:S(2)}, u32[]{:S(2)}) %collective-permute-start.34) | collective-permute-done | bytes 2293792 | tf_op jit(solution)/shard_map/ppermute | solution.py:32
  380.2 3.5 fusion.15.left
  390.6 16.0 %first_half.3 = (bf16[2048,1280]{1,0:T(8,128)(2,1)}, bf16[2048,1280]{1,0:T(8,128)(2,1)}, bf16[2048,1280]{1,0:T(8,128)(2,1)}) custom-call(bf16[512,1792]{1,0:T(8,128)(2,1)} %collective-permute-done.35.refs_0_.refs_3_, bf16[512,1792]{1,0:T(8,128)(2,1)} %copy-done.5, ...), custom_call_target="tpu_custom_call", output_to_operand_aliasing={{0}: (4, {}), {1}: (5, {}), {2}: (6, {})} | custom-call | flops 18790481920 | bytes 25952256 | tf_op jit(solution)/shard_map/first_half/pallas_call | solution.py:192
  406.6 9.3 %gradient_half.6 = bf16[896,1280]{1,0:T(8,128)(2,1)} custom-call(s32[1]{0:T(128)} %bitcast.39.refs_0_, bf16[512,1792]{1,0:T(8,128)(2,1)S(1)} %bitcast.318, bf16[512,1792]{1,0:T(8,128)(2,1)} %collective-permute-done.29.refs_2_.refs_1_, bf16[512,1792]{1,0:T(8,128)(2,1)} %collective-permute-done.5.refs_3_.refs_0_, ...), custom_call_target="tpu_custom_call" | custom-call | flops 4697620480 | bytes 11206656 | tf_op jit(solution)/shard_map/gradient_half/pallas_call | solution.py:232
  416.5 29.8 %second_half.2 = (bf16[2048,2560]{1,0:T(8,128)(2,1)}, bf16[512,1792]{1,0:T(8,128)(2,1)}, bf16[512,1792]{1,0:T(8,128)(2,1)}, bf16[512,1792]{1,0:T(8,128)(2,1)}, bf16[512,1792]{1,0:T(8,128)(2,1)}) custom-call(bf16[512,1792]{1,0:T(8,128)(2,1)} %collective-permute-done.5.refs_3_.refs_0_, bf16[512,1792]{1,0:T(8,128)(2,1)} %collective-permute-done.30.refs_4_.refs_1_, ...), custom_call_target="tpu_custom_call" | custom-call | flops 37580963840 | bytes 30539776 | tf_op jit(solution)/shard_map/second_half/pallas_call | solution.py:192
  446.8 30.2 %second_half.3 = (bf16[2048,2560]{1,0:T(8,128)(2,1)}, bf16[512,1792]{1,0:T(8,128)(2,1)}, bf16[512,1792]{1,0:T(8,128)(2,1)}, bf16[512,1792]{1,0:T(8,128)(2,1)}, bf16[512,1792]{1,0:T(8,128)(2,1)}) custom-call(bf16[512,1792]{1,0:T(8,128)(2,1)} %bitcast.316, bf16[512,1792]{1,0:T(8,128)(2,1)} %collective-permute-done.29.refs_2_.refs_1_, ...), custom_call_target="tpu_custom_call", output_to_operand_aliasing={{0}: (8, {})} | custom-call | flops 37580963840 | bytes 30539776 | tf_op jit(solution)/shard_map/second_half/pallas_call | solution.py:192
  479.0 8.8 %gradient_half.7 = bf16[896,1280]{1,0:T(8,128)(2,1)} custom-call(s32[1]{0:T(128)} %bitcast.39.refs_0_, bf16[512,1792]{1,0:T(8,128)(2,1)S(1)} %copy-done.1, bf16[512,1792]{1,0:T(8,128)(2,1)S(1)} %copy-done.3, bf16[512,1792]{1,0:T(8,128)(2,1)} %collective-permute-done.35.refs_0_.refs_3_, bf16[512,1792]{1,0:T(8,128)(2,1)S(1)} %copy-done.6, ...), custom_call_target="tpu_custom_call" | custom-call | flops 4697620480 | bytes 11206656 | tf_op jit(solution)/shard_map/gradient_half/pallas_call | solution.py:232
  489.3 3.1 add_convert_fusion.5
  493.1 8.1 gradient_half.11
  501.2 3.6 add_convert_fusion.2
  507.9 8.9 %gradient_half.8 = bf16[896,1280]{1,0:T(8,128)(2,1)} custom-call(s32[1]{0:T(128)} %bitcast.39.refs_0_, bf16[512,1792]{1,0:T(8,128)(2,1)S(1)} %copy-done.1, bf16[512,1792]{1,0:T(8,128)(2,1)S(1)} %copy-done.4, bf16[512,1792]{1,0:T(8,128)(2,1)} %collective-permute-done.35.refs_0_.refs_3_, bf16[512,1792]{1,0:T(8,128)(2,1)S(1)} %copy-done.7, ...), custom_call_target="tpu_custom_call" | custom-call | flops 4697620480 | bytes 11206656 | tf_op jit(solution)/shard_map/gradient_half/pallas_call | solution.py:232
  516.8 7.7 gradient_half.9
  524.5 7.8 gradient_half.10
  532.3 4.1 add_convert_fusion.4
  536.4 3.7 collective-permute-done.41
  542.2 3.6 multiply_reduce_fusion.3
  545.8 3.7 add_convert_fusion.1
  549.5 6.0 fusion.87
  555.5 7.0 fusion.94
  562.6 3.8 multiply_reduce_fusion
  572.1 5.4 split_gradient.3
  579.3 5.5 split_gradient.4
  584.8 5.4 fusion.95
  592.6 15.1 %all-gather = bf16[32,1792]{1,0:T(8,128)(2,1)S(1)} all-gather(bf16[8,1792]{1,0:T(8,128)(2,1)S(1)} %concatenate.106), channel_id=2, replica_groups=mesh['a'=2,'b'=2,'c'=2,'z'=4] {'z'}, dimensions={0}, use_global_device_ids=true | all-gather | bytes 143360 | tf_op jit(solution)/shard_map/all_gather | solution.py:343
  607.7 11.0 %all-gather.1 = bf16[32,8,1792]{2,1,0:T(8,128)(2,1)} all-gather(bf16[4,8,1792]{2,1,0:T(8,128)(2,1)S(1)} %bitcast.353), channel_id=3, replica_groups=mesh['a'=2,'b'=2,'c'=2,'z'=4] {'a','b','c'}, dimensions={0}, use_global_device_ids=true | all-gather | bytes 1032192 | tf_op jit(solution)/shard_map/all_gather | solution.py:343
  618.7 3.1 fusion.25
  628.6 4.7 fusion.7
  637.9 3.7 add_convert_fusion
  642.3 5.2 fusion.10
  649.4 4.0 fusion.20
  653.3 6.2 split_gradient.5
  662.3 19.2 %collective-permute-done.51 = bf16[224,1280]{1,0:T(8,128)(2,1)} collective-permute-done((bf16[224,1280]{1,0:T(8,128)(2,1)}, bf16[224,1280]{1,0:T(8,128)(2,1)}, u32[]{:S(2)}, u32[]{:S(2)}) %collective-permute-start.51) | collective-permute-done | bytes 573472 | tf_op jit(solution)/shard_map/ppermute | solution.py:114
  689.6 3.6 collective-permute-start.56
  693.2 3.3 collective-permute-start.57
  721.2 8.8 %collective-permute-done.55 = bf16[224,1792]{1,0:T(8,128)(2,1)} collective-permute-done((bf16[224,1792]{1,0:T(8,128)(2,1)}, bf16[224,1792]{1,0:T(8,128)(2,1)}, u32[]{:S(2)}, u32[]{:S(2)}) %collective-permute-start.55) | collective-permute-done | bytes 802848 | tf_op jit(solution)/shard_map/ppermute | solution.py:32
  730.0 5.1 collective-permute-done.58
  735.1 4.4 collective-permute-done.54
  751.7 3.6 collective-permute-start.65
  765.8 3.5 collective-permute-done.66
  769.4 5.9 collective-permute-done.61
  776.3 18.0 %collective-permute-done.63 = bf16[448,448]{1,0:T(8,128)(2,1)S(1)} collective-permute-done((bf16[448,448]{1,0:T(8,128)(2,1)S(1)}, bf16[448,448]{1,0:T(8,128)(2,1)S(1)}, u32[]{:S(2)}, u32[]{:S(2)}) %collective-permute-start.63) | collective-permute-done | bytes 401440 | tf_op jit(solution)/shard_map/ppermute | solution.py:32
  799.4 7.7 collective-permute-start.69
  810.2 4.4 add_convert_fusion.3
  815.9 14.3 %collective-permute-done.68 = bf16[232,448]{1,0:T(8,128)(2,1)S(1)} collective-permute-done((bf16[232,448]{1,0:T(8,128)(2,1)S(1)}, bf16[232,448]{1,0:T(8,128)(2,1)S(1)}, u32[]{:S(2)}, u32[]{:S(2)}) %collective-permute-start.68) | collective-permute-done | bytes 207904 | tf_op jit(solution)/shard_map/ppermute | solution.py:32
  (517 shorter events, 194.8 us)
Async XLA Ops:
  7.2 127.3 %all-gather.6.cloned.1.call-start = ((), (), s32[]{:S(2)}) async-start(), calls=%async_computation.3 | async-start | bytes 7225344 | tf_op jit(solution)/shard_map/all_gather | solution.py:340
  7.2 42.1 %collective-permute-start.5 = (bf16[512,1792]{1,0:T(8,128)(2,1)}, bf16[512,1792]{1,0:T(8,128)(2,1)}, u32[]{:S(2)}, u32[]{:S(2)}) collective-permute-start(bf16[512,1792]{1,0:T(8,128)(2,1)} %bitcast.315), channel_id=1, source_target_pairs={{0,8},{8,0},{1,9},{9,1},{2,10},{10,2},{3,11},{11,3},{4,12},{12,4},... | collective-permute-start | bytes 5505032 | tf_op jit(solution)/shard_map/ppermute | solution.py:32
  7.8 35.3 %collective-permute-start = (bf16[224,448]{1,0:T(8,128)(2,1)}, bf16[224,448]{1,0:T(8,128)(2,1)S(1)}, u32[]{:S(2)}, u32[]{:S(2)}) collective-permute-start(bf16[224,448]{1,0:T(8,128)(2,1)} %param.18), channel_id=1, source_target_pairs={{0,1},{1,2},{2,3},{3,0},{4,5},{5,6},{6,7},{7,4},{8,9},{9,10},{10,1... | collective-permute-start | bytes 602120 | tf_op jit(solution)/shard_map/ppermute | solution.py:32
  8.1 35.1 %collective-permute-start.1 = (bf16[224,448]{1,0:T(8,128)(2,1)}, bf16[224,448]{1,0:T(8,128)(2,1)}, u32[]{:S(2)}, u32[]{:S(2)}) collective-permute-start(bf16[224,448]{1,0:T(8,128)(2,1)} %param.18), channel_id=1, source_target_pairs={{0,2},{1,3},{2,0},{3,1},{4,6},{5,7},{6,4},{7,5},{8,10},{9,11},{10,... | collective-permute-start | bytes 602120 | tf_op jit(solution)/shard_map/ppermute | solution.py:32
  9.7 33.4 %collective-permute-start.2 = (bf16[224,448]{1,0:T(8,128)(2,1)}, bf16[224,448]{1,0:T(8,128)(2,1)}, u32[]{:S(2)}, u32[]{:S(2)}) collective-permute-start(bf16[224,448]{1,0:T(8,128)(2,1)} %param.18), channel_id=1, source_target_pairs={{0,3},{1,0},{2,1},{3,2},{4,7},{5,4},{6,5},{7,6},{8,11},{9,8},{10,9... | collective-permute-start | bytes 602120 | tf_op jit(solution)/shard_map/ppermute | solution.py:32
  25.3 17.8 %collective-permute-start.4 = (f32[2,9,1792]{2,1,0:T(8,128)S(1)}, f32[2,9,1792]{2,1,0:T(8,128)S(1)}, u32[]{:S(2)}, u32[]{:S(2)}) collective-permute-start(f32[2,9,1792]{2,1,0:T(8,128)S(1)} %pad_maximum_fusion.16), channel_id=1, source_target_pairs={{0,2},{1,3},{2,0},{3,1},{4,6},{5,7},{6,4},{7,5},{8,10},{9,11},{10,... | collective-permute-start | bytes 387080 | tf_op jit(solution)/shard_map/ppermute | solution.py:119
  51.5 142.2 %all-gather.8.cloned.1.call-start = ((), (), s32[]{:S(2)}) async-start(), calls=%async_computation.4 | async-start | bytes 7225344 | tf_op jit(solution)/shard_map/all_gather | solution.py:340
  51.6 45.7 %collective-permute-start.9 = (bf16[224,1280]{1,0:T(8,128)(2,1)S(1)}, bf16[224,1280]{1,0:T(8,128)(2,1)S(1)}, u32[]{:S(2)}, u32[]{:S(2)}) collective-permute-start(bf16[224,1280]{1,0:T(8,128)(2,1)S(1)} %pad.19), channel_id=1, source_target_pairs={{0,1},{1,2},{2,3},{3,0},{4,5},{5,6},{6,7},{7,4},{8,9},{9,10},{10,1... | collective-permute-start | bytes 1720328 | tf_op jit(solution)/shard_map/ppermute | solution.py:32
  51.8 46.2 %collective-permute-start.10 = (bf16[224,1280]{1,0:T(8,128)(2,1)S(1)}, bf16[224,1280]{1,0:T(8,128)(2,1)S(1)}, u32[]{:S(2)}, u32[]{:S(2)}) collective-permute-start(bf16[224,1280]{1,0:T(8,128)(2,1)S(1)} %pad.19), channel_id=1, source_target_pairs={{0,3},{1,0},{2,1},{3,2},{4,7},{5,4},{6,5},{7,6},{8,11},{9,8},{10,9... | collective-permute-start | bytes 1720328 | tf_op jit(solution)/shard_map/ppermute | solution.py:32
  53.6 29.7 %collective-permute-start.6 = (bf16[224,448]{1,0:T(8,128)(2,1)S(1)}, bf16[224,448]{1,0:T(8,128)(2,1)S(1)}, u32[]{:S(2)}, u32[]{:S(2)}) collective-permute-start(bf16[224,448]{1,0:T(8,128)(2,1)S(1)} %copy-done.67), channel_id=1, source_target_pairs={{0,1},{1,2},{2,3},{3,0},{4,5},{5,6},{6,7},{7,4},{8,9},{9,10},{10,1... | collective-permute-start | bytes 602120 | tf_op jit(solution)/shard_map/ppermute | solution.py:32
  55.7 41.6 %collective-permute-start.7 = (bf16[224,448]{1,0:T(8,128)(2,1)S(1)}, bf16[224,448]{1,0:T(8,128)(2,1)S(1)}, u32[]{:S(2)}, u32[]{:S(2)}) collective-permute-start(bf16[224,448]{1,0:T(8,128)(2,1)S(1)} %copy-done.67), channel_id=1, source_target_pairs={{0,2},{1,3},{2,0},{3,1},{4,6},{5,7},{6,4},{7,5},{8,10},{9,11},{10,... | collective-permute-start | bytes 602120 | tf_op jit(solution)/shard_map/ppermute | solution.py:32
  55.7 41.6 %collective-permute-start.8 = (bf16[224,448]{1,0:T(8,128)(2,1)S(1)}, bf16[224,448]{1,0:T(8,128)(2,1)S(1)}, u32[]{:S(2)}, u32[]{:S(2)}) collective-permute-start(bf16[224,448]{1,0:T(8,128)(2,1)S(1)} %copy-done.67), channel_id=1, source_target_pairs={{0,3},{1,0},{2,1},{3,2},{4,7},{5,4},{6,5},{7,6},{8,11},{9,8},{10,9... | collective-permute-start | bytes 602120 | tf_op jit(solution)/shard_map/ppermute | solution.py:32
  100.2 169.3 %all-gather.10.cloned.1.call-start = ((), (), s32[]{:S(2)}) async-start(), calls=%async_computation.5 | async-start | bytes 7225344 | tf_op jit(solution)/shard_map/all_gather | solution.py:340
  100.3 34.2 %collective-permute-start.14 = (bf16[224,1280]{1,0:T(8,128)(2,1)S(1)}, bf16[224,1280]{1,0:T(8,128)(2,1)}, u32[]{:S(2)}, u32[]{:S(2)}) collective-permute-start(bf16[224,1280]{1,0:T(8,128)(2,1)S(1)} %collective-permute-done.9), channel_id=1, source_target_pairs={{0,1},{1,2},{2,3},{3,0},{4,5},{5,6},{6,7},{7,4},{8,9},{9,10},{10,1... | collective-permute-start | bytes 1720328 | tf_op jit(solution)/shard_map/ppermute | solution.py:32
  100.9 18.0 %collective-permute-start.11 = (bf16[224,448]{1,0:T(8,128)(2,1)}, bf16[224,448]{1,0:T(8,128)(2,1)S(1)}, u32[]{:S(2)}, u32[]{:S(2)}) collective-permute-start(bf16[224,448]{1,0:T(8,128)(2,1)} %param.21), channel_id=1, source_target_pairs={{0,1},{1,2},{2,3},{3,0},{4,5},{5,6},{6,7},{7,4},{8,9},{9,10},{10,1... | collective-permute-start | bytes 602120 | tf_op jit(solution)/shard_map/ppermute | solution.py:32
  103.5 31.0 %collective-permute-start.12 = (bf16[224,448]{1,0:T(8,128)(2,1)}, bf16[224,448]{1,0:T(8,128)(2,1)}, u32[]{:S(2)}, u32[]{:S(2)}) collective-permute-start(bf16[224,448]{1,0:T(8,128)(2,1)} %param.21), channel_id=1, source_target_pairs={{0,2},{1,3},{2,0},{3,1},{4,6},{5,7},{6,4},{7,5},{8,10},{9,11},{10,... | collective-permute-start | bytes 602120 | tf_op jit(solution)/shard_map/ppermute | solution.py:32
  104.3 30.2 %collective-permute-start.13 = (bf16[224,448]{1,0:T(8,128)(2,1)}, bf16[224,448]{1,0:T(8,128)(2,1)}, u32[]{:S(2)}, u32[]{:S(2)}) collective-permute-start(bf16[224,448]{1,0:T(8,128)(2,1)} %param.21), channel_id=1, source_target_pairs={{0,3},{1,0},{2,1},{3,2},{4,7},{5,4},{6,5},{7,6},{8,11},{9,8},{10,9... | collective-permute-start | bytes 602120 | tf_op jit(solution)/shard_map/ppermute | solution.py:32
  136.7 455.0 %reduce-scatter.4.cloned.1.call-start = ((), (), s32[]{:S(2)}) async-start(), calls=%async_computation.6 | async-start | bytes 2867200 | tf_op jit(solution)/shard_map/reduce_scatter | solution.py:474
  140.5 18.2 %collective-permute-start.16 = (bf16[2,224,1280]{2,1,0:T(8,128)(2,1)}, bf16[2,224,1280]{2,1,0:T(8,128)(2,1)}, u32[]{:S(2)}, u32[]{:S(2)}) collective-permute-start(bf16[2,224,1280]{2,1,0:T(8,128)(2,1)} %dynamic-slice_bitcast_fusion.8), channel_id=1, source_target_pairs={{0,4},{4,0},{1,5},{5,1},{2,6},{6,2},{3,7},{7,3},{8,12},{12,8},{9,1... | collective-permute-start | bytes 3440648 | tf_op jit(solution)/shard_map/ppermute | solution.py:32
  143.7 31.1 %collective-permute-start.18 = (bf16[224,1280]{1,0:T(8,128)(2,1)}, bf16[224,1280]{1,0:T(8,128)(2,1)}, u32[]{:S(2)}, u32[]{:S(2)}) collective-permute-start(bf16[224,1280]{1,0:T(8,128)(2,1)} %pad.20), channel_id=1, source_target_pairs={{0,1},{1,2},{2,3},{3,0},{4,5},{5,6},{6,7},{7,4},{8,9},{9,10},{10,1... | collective-permute-start | bytes 1720328 | tf_op jit(solution)/shard_map/ppermute | solution.py:32
  143.8 49.9 %collective-permute-start.19 = (bf16[224,1280]{1,0:T(8,128)(2,1)}, bf16[224,1280]{1,0:T(8,128)(2,1)}, u32[]{:S(2)}, u32[]{:S(2)}) collective-permute-start(bf16[224,1280]{1,0:T(8,128)(2,1)} %pad.20), channel_id=1, source_target_pairs={{0,2},{1,3},{2,0},{3,1},{4,6},{5,7},{6,4},{7,5},{8,10},{9,11},{10,... | collective-permute-start | bytes 1720328 | tf_op jit(solution)/shard_map/ppermute | solution.py:32
  143.9 49.8 %collective-permute-start.20 = (bf16[224,1280]{1,0:T(8,128)(2,1)}, bf16[224,1280]{1,0:T(8,128)(2,1)}, u32[]{:S(2)}, u32[]{:S(2)}) collective-permute-start(bf16[224,1280]{1,0:T(8,128)(2,1)} %pad.20), channel_id=1, source_target_pairs={{0,3},{1,0},{2,1},{3,2},{4,7},{5,4},{6,5},{7,6},{8,11},{9,8},{10,9... | collective-permute-start | bytes 1720328 | tf_op jit(solution)/shard_map/ppermute | solution.py:32
  162.4 44.5 %collective-permute-start.17 = (bf16[2,224,1280]{2,1,0:T(8,128)(2,1)}, bf16[2,224,1280]{2,1,0:T(8,128)(2,1)}, u32[]{:S(2)}, u32[]{:S(2)}) collective-permute-start(bf16[2,224,1280]{2,1,0:T(8,128)(2,1)} %get-tuple-element.476), channel_id=1, source_target_pairs={{0,8},{8,0},{1,9},{9,1},{2,10},{10,2},{3,11},{11,3},{4,12},{12,4},... | collective-permute-start | bytes 3440648 | tf_op jit(solution)/shard_map/ppermute | solution.py:32
  206.9 26.4 %collective-permute-start.26 = (bf16[224,1280]{1,0:T(8,128)(2,1)}, bf16[224,1280]{1,0:T(8,128)(2,1)}, u32[]{:S(2)}, u32[]{:S(2)}) collective-permute-start(bf16[224,1280]{1,0:T(8,128)(2,1)} %pad.21), channel_id=1, source_target_pairs={{0,1},{1,2},{2,3},{3,0},{4,5},{5,6},{6,7},{7,4},{8,9},{9,10},{10,1... | collective-permute-start | bytes 1720328 | tf_op jit(solution)/shard_map/ppermute | solution.py:32
  207.3 50.5 %collective-permute-start.27 = (bf16[224,1280]{1,0:T(8,128)(2,1)}, bf16[224,1280]{1,0:T(8,128)(2,1)}, u32[]{:S(2)}, u32[]{:S(2)}) collective-permute-start(bf16[224,1280]{1,0:T(8,128)(2,1)} %pad.21), channel_id=1, source_target_pairs={{0,2},{1,3},{2,0},{3,1},{4,6},{5,7},{6,4},{7,5},{8,10},{9,11},{10,... | collective-permute-start | bytes 1720328 | tf_op jit(solution)/shard_map/ppermute | solution.py:32
  208.8 49.0 %collective-permute-start.28 = (bf16[224,1280]{1,0:T(8,128)(2,1)}, bf16[224,1280]{1,0:T(8,128)(2,1)}, u32[]{:S(2)}, u32[]{:S(2)}) collective-permute-start(bf16[224,1280]{1,0:T(8,128)(2,1)} %pad.21), channel_id=1, source_target_pairs={{0,3},{1,0},{2,1},{3,2},{4,7},{5,4},{6,5},{7,6},{8,11},{9,8},{10,9... | collective-permute-start | bytes 1720328 | tf_op jit(solution)/shard_map/ppermute | solution.py:32
  217.6 52.0 %collective-permute-start.23 = (bf16[4,224,1280]{2,1,0:T(8,128)(2,1)}, bf16[4,224,1280]{2,1,0:T(8,128)(2,1)}, u32[]{:S(2)}, u32[]{:S(2)}) collective-permute-start(bf16[4,224,1280]{2,1,0:T(8,128)(2,1)} %bitcast.27), channel_id=1, source_target_pairs={{0,16},{16,0},{1,17},{17,1},{2,18},{18,2},{3,19},{19,3},{4,20},{20... | collective-permute-start | bytes 6881288 | tf_op jit(solution)/shard_map/ppermute | solution.py:32
  222.7 35.1 %collective-permute-start.25 = (bf16[2,224,1280]{2,1,0:T(8,128)(2,1)S(1)}, bf16[2,224,1280]{2,1,0:T(8,128)(2,1)}, u32[]{:S(2)}, u32[]{:S(2)}) collective-permute-start(bf16[2,224,1280]{2,1,0:T(8,128)(2,1)S(1)} %get-tuple-element.468), channel_id=1, source_target_pairs={{0,8},{8,0},{1,9},{9,1},{2,10},{10,2},{3,11},{11,3},{4,12},{12,4},... | collective-permute-start | bytes 3440648 | tf_op jit(solution)/shard_map/ppermute | solution.py:32
  273.7 52.2 %collective-permute-start.33 = (bf16[4,224,1280]{2,1,0:T(8,128)(2,1)S(1)}, bf16[4,224,1280]{2,1,0:T(8,128)(2,1)S(1)}, u32[]{:S(2)}, u32[]{:S(2)}) collective-permute-start(bf16[4,224,1280]{2,1,0:T(8,128)(2,1)S(1)} %bitcast.330), channel_id=1, source_target_pairs={{0,16},{16,0},{1,17},{17,1},{2,18},{18,2},{3,19},{19,3},{4,20},{20... | collective-permute-start | bytes 6881288 | tf_op jit(solution)/shard_map/ppermute | solution.py:32
  283.1 27.5 %collective-permute-start.32 = (bf16[2,224,1280]{2,1,0:T(8,128)(2,1)S(1)}, bf16[2,224,1280]{2,1,0:T(8,128)(2,1)S(1)}, u32[]{:S(2)}, u32[]{:S(2)}) collective-permute-start(bf16[2,224,1280]{2,1,0:T(8,128)(2,1)S(1)} %get-tuple-element.462), channel_id=1, source_target_pairs={{0,8},{8,0},{1,9},{9,1},{2,10},{10,2},{3,11},{11,3},{4,12},{12,4},... | collective-permute-start | bytes 3440648 | tf_op jit(solution)/shard_map/ppermute | solution.py:32
  325.9 41.6 %collective-permute-start.35 = (bf16[512,1792]{1,0:T(8,128)(2,1)S(1)}, bf16[512,1792]{1,0:T(8,128)(2,1)}, u32[]{:S(2)}, u32[]{:S(2)}) collective-permute-start(bf16[512,1792]{1,0:T(8,128)(2,1)S(1)} %multiply_convert_fusion.1.refs_0_.refs_1_), channel_id=1, source_target_pairs={{0,8},{8,0},{1,9},{9,1},{2,10},{10,2},{3,11},{11,3},{4,12},{12,4},... | collective-permute-start | bytes 5505032 | tf_op jit(solution)/shard_map/ppermute | solution.py:32
  327.8 52.4 %collective-permute-start.34 = (bf16[4,224,1280]{2,1,0:T(8,128)(2,1)S(1)}, bf16[4,224,1280]{2,1,0:T(8,128)(2,1)}, u32[]{:S(2)}, u32[]{:S(2)}) collective-permute-start(bf16[4,224,1280]{2,1,0:T(8,128)(2,1)S(1)} %bitcast.332), channel_id=1, source_target_pairs={{0,16},{16,0},{1,17},{17,1},{2,18},{18,2},{3,19},{19,3},{4,20},{20... | collective-permute-start | bytes 6881288 | tf_op jit(solution)/shard_map/ppermute | solution.py:32
  383.7 22.9 %collective-permute-start.29 = (bf16[512,1792]{1,0:T(8,128)(2,1)S(1)}, bf16[512,1792]{1,0:T(8,128)(2,1)}, u32[]{:S(2)}, u32[]{:S(2)}) collective-permute-start(bf16[512,1792]{1,0:T(8,128)(2,1)S(1)} %bitcast.317), channel_id=1, source_target_pairs={{0,4},{4,0},{1,5},{5,1},{2,6},{6,2},{3,7},{7,3},{8,12},{12,8},{9,1... | collective-permute-start | bytes 5505032 | tf_op jit(solution)/shard_map/ppermute | solution.py:32
  384.2 22.4 %collective-permute-start.30 = (bf16[512,1792]{1,0:T(8,128)(2,1)}, bf16[512,1792]{1,0:T(8,128)(2,1)}, u32[]{:S(2)}, u32[]{:S(2)}) collective-permute-start(bf16[512,1792]{1,0:T(8,128)(2,1)} %collective-permute-done.5.refs_3_.refs_0_), channel_id=1, source_target_pairs={{0,4},{4,0},{1,5},{5,1},{2,6},{6,2},{3,7},{7,3},{8,12},{12,8},{9,1... | collective-permute-start | bytes 5505032 | tf_op jit(solution)/shard_map/ppermute | solution.py:32
  415.9 71.8 %collective-permute-start.38 = (bf16[896,1280]{1,0:T(8,128)(2,1)}, bf16[896,1280]{1,0:T(8,128)(2,1)}, u32[]{:S(2)}, u32[]{:S(2)}) collective-permute-start(bf16[896,1280]{1,0:T(8,128)(2,1)} %gradient_half.6), channel_id=1, source_target_pairs={{0,16},{16,0},{1,17},{17,1},{2,18},{18,2},{3,19},{19,3},{4,20},{20... | collective-permute-start | bytes 6881288 | tf_op jit(solution)/shard_map/ppermute | solution.py:32
  446.3 41.5 %collective-permute-start.39 = (bf16[512,1792]{1,0:T(8,128)(2,1)}, bf16[512,1792]{1,0:T(8,128)(2,1)}, u32[]{:S(2)}, u32[]{:S(2)}) collective-permute-start(bf16[512,1792]{1,0:T(8,128)(2,1)} %get-tuple-element.296), channel_id=1, source_target_pairs={{0,4},{4,0},{1,5},{5,1},{2,6},{6,2},{3,7},{7,3},{8,12},{12,8},{9,1... | collective-permute-start | bytes 5505032 | tf_op jit(solution)/shard_map/ppermute | solution.py:32
  446.5 41.3 %collective-permute-start.40 = (bf16[512,1792]{1,0:T(8,128)(2,1)}, bf16[512,1792]{1,0:T(8,128)(2,1)}, u32[]{:S(2)}, u32[]{:S(2)}) collective-permute-start(bf16[512,1792]{1,0:T(8,128)(2,1)} %get-tuple-element.298), channel_id=1, source_target_pairs={{0,4},{4,0},{1,5},{5,1},{2,6},{6,2},{3,7},{7,3},{8,12},{12,8},{9,1... | collective-permute-start | bytes 5505032 | tf_op jit(solution)/shard_map/ppermute | solution.py:32
  477.0 59.5 %collective-permute-start.43 = (bf16[512,1792]{1,0:T(8,128)(2,1)}, bf16[512,1792]{1,0:T(8,128)(2,1)}, u32[]{:S(2)}, u32[]{:S(2)}) collective-permute-start(bf16[512,1792]{1,0:T(8,128)(2,1)} %get-tuple-element.307), channel_id=1, source_target_pairs={{0,4},{4,0},{1,5},{5,1},{2,6},{6,2},{3,7},{7,3},{8,12},{12,8},{9,1... | collective-permute-start | bytes 5505032 | tf_op jit(solution)/shard_map/ppermute | solution.py:32
  477.2 59.2 %collective-permute-start.44 = (bf16[512,1792]{1,0:T(8,128)(2,1)}, bf16[512,1792]{1,0:T(8,128)(2,1)}, u32[]{:S(2)}, u32[]{:S(2)}) collective-permute-start(bf16[512,1792]{1,0:T(8,128)(2,1)} %get-tuple-element.309), channel_id=1, source_target_pairs={{0,4},{4,0},{1,5},{5,1},{2,6},{6,2},{3,7},{7,3},{8,12},{12,8},{9,1... | collective-permute-start | bytes 5505032 | tf_op jit(solution)/shard_map/ppermute | solution.py:32
  487.8 52.4 %collective-permute-start.41 = (bf16[896,1280]{1,0:T(8,128)(2,1)}, bf16[896,1280]{1,0:T(8,128)(2,1)}, u32[]{:S(2)}, u32[]{:S(2)}) collective-permute-start(bf16[896,1280]{1,0:T(8,128)(2,1)} %gradient_half.7), channel_id=1, source_target_pairs={{0,16},{16,0},{1,17},{17,1},{2,18},{18,2},{3,19},{19,3},{4,20},{20... | collective-permute-start | bytes 6881288 | tf_op jit(solution)/shard_map/ppermute | solution.py:32
  492.5 44.0 %collective-permute-start.42 = (bf16[512,1792]{1,0:T(8,128)(2,1)}, bf16[512,1792]{1,0:T(8,128)(2,1)}, u32[]{:S(2)}, u32[]{:S(2)}) collective-permute-start(bf16[512,1792]{1,0:T(8,128)(2,1)} %add_convert_fusion.5), channel_id=1, source_target_pairs={{0,8},{8,0},{1,9},{9,1},{2,10},{10,2},{3,11},{11,3},{4,12},{12,4},... | collective-permute-start | bytes 5505032 | tf_op jit(solution)/shard_map/ppermute | solution.py:32
  504.9 113.8 %reduce-scatter.6.cloned.1.call-start = ((), (), s32[]{:S(2)}) async-start(), calls=%async_computation.7 | async-start | bytes 2867200 | tf_op jit(solution)/shard_map/reduce_scatter | solution.py:474
  540.1 51.5 %collective-permute-start.45 = (bf16[896,1280]{1,0:T(8,128)(2,1)}, bf16[896,1280]{1,0:T(8,128)(2,1)}, u32[]{:S(2)}, u32[]{:S(2)}) collective-permute-start(bf16[896,1280]{1,0:T(8,128)(2,1)} %gradient_half.8), channel_id=1, source_target_pairs={{0,16},{16,0},{1,17},{17,1},{2,18},{18,2},{3,19},{19,3},{4,20},{20... | collective-permute-start | bytes 6881288 | tf_op jit(solution)/shard_map/ppermute | solution.py:32
  541.6 48.5 %collective-permute-start.46 = (bf16[512,1792]{1,0:T(8,128)(2,1)}, bf16[512,1792]{1,0:T(8,128)(2,1)}, u32[]{:S(2)}, u32[]{:S(2)}) collective-permute-start(bf16[512,1792]{1,0:T(8,128)(2,1)} %add_convert_fusion.4), channel_id=1, source_target_pairs={{0,8},{8,0},{1,9},{9,1},{2,10},{10,2},{3,11},{11,3},{4,12},{12,4},... | collective-permute-start | bytes 5505032 | tf_op jit(solution)/shard_map/ppermute | solution.py:32
  569.0 141.7 %reduce-scatter.8.cloned.1.call-start = ((), (), s32[]{:S(2)}) async-start(), calls=%async_computation.8 | async-start | bytes 2867200 | tf_op jit(solution)/shard_map/reduce_scatter | solution.py:474
  591.6 27.1 %collective-permute-start.47 = (bf16[4,224,1792]{2,1,0:T(8,128)(2,1)}, bf16[4,224,1792]{2,1,0:T(8,128)(2,1)}, u32[]{:S(2)}, u32[]{:S(2)}) collective-permute-start(bf16[4,224,1792]{2,1,0:T(8,128)(2,1)} %copy-done.21), channel_id=1, source_target_pairs={{0,4},{4,0},{1,5},{5,1},{2,6},{6,2},{3,7},{7,3},{8,12},{12,8},{9,1... | collective-permute-start | bytes 9633800 | tf_op jit(solution)/shard_map/ppermute | solution.py:32
  591.6 27.1 %collective-permute-start.48 = (bf16[4,224,1792]{2,1,0:T(8,128)(2,1)}, bf16[4,224,1792]{2,1,0:T(8,128)(2,1)}, u32[]{:S(2)}, u32[]{:S(2)}) collective-permute-start(bf16[4,224,1792]{2,1,0:T(8,128)(2,1)} %copy-done.22), channel_id=1, source_target_pairs={{0,4},{4,0},{1,5},{5,1},{2,6},{6,2},{3,7},{7,3},{8,12},{12,8},{9,1... | collective-permute-start | bytes 9633800 | tf_op jit(solution)/shard_map/ppermute | solution.py:32
  621.8 59.7 %collective-permute-start.49 = (bf16[2,224,1792]{2,1,0:T(8,128)(2,1)}, bf16[2,224,1792]{2,1,0:T(8,128)(2,1)}, u32[]{:S(2)}, u32[]{:S(2)}) collective-permute-start(bf16[2,224,1792]{2,1,0:T(8,128)(2,1)} %fusion.25), channel_id=1, source_target_pairs={{0,8},{8,0},{1,9},{9,1},{2,10},{10,2},{3,11},{11,3},{4,12},{12,4},... | collective-permute-start | bytes 4816904 | tf_op jit(solution)/shard_map/ppermute | solution.py:32
  626.0 55.5 %collective-permute-start.50 = (bf16[2,224,1792]{2,1,0:T(8,128)(2,1)}, bf16[2,224,1792]{2,1,0:T(8,128)(2,1)}, u32[]{:S(2)}, u32[]{:S(2)}) collective-permute-start(bf16[2,224,1792]{2,1,0:T(8,128)(2,1)} %fusion.26), channel_id=1, source_target_pairs={{0,16},{16,0},{1,17},{17,1},{2,18},{18,2},{3,19},{19,3},{4,20},{20... | collective-permute-start | bytes 4816904 | tf_op jit(solution)/shard_map/ppermute | solution.py:32
  635.8 45.8 %collective-permute-start.51 = (bf16[224,1280]{1,0:T(8,128)(2,1)}, bf16[224,1280]{1,0:T(8,128)(2,1)}, u32[]{:S(2)}, u32[]{:S(2)}) collective-permute-start(bf16[224,1280]{1,0:T(8,128)(2,1)} %reduce-scatter.4.cloned.1.call-done), channel_id=1, source_target_pairs={{0,0},{8,1},{4,2},{12,3},{1,4},{9,5},{5,6},{13,7},{2,8},{10,9},{6,... | collective-permute-start | bytes 1720328 | tf_op jit(solution)/shard_map/ppermute | solution.py:114
  681.6 18.0 %collective-permute-start.52 = (bf16[4,224,1792]{2,1,0:T(8,128)(2,1)}, bf16[4,224,1792]{2,1,0:T(8,128)(2,1)}, u32[]{:S(2)}, u32[]{:S(2)}) collective-permute-start(bf16[4,224,1792]{2,1,0:T(8,128)(2,1)} %get-tuple-element.358), channel_id=1, source_target_pairs={{0,4},{4,0},{1,5},{5,1},{2,6},{6,2},{3,7},{7,3},{8,12},{12,8},{9,1... | collective-permute-start | bytes 9633800 | tf_op jit(solution)/shard_map/ppermute | solution.py:32
  686.8 43.2 %collective-permute-start.55 = (bf16[224,1792]{1,0:T(8,128)(2,1)}, bf16[224,1792]{1,0:T(8,128)(2,1)}, u32[]{:S(2)}, u32[]{:S(2)}) collective-permute-start(bf16[224,1792]{1,0:T(8,128)(2,1)} %fusion.28), channel_id=1, source_target_pairs={{0,8},{8,0},{1,9},{9,1},{2,10},{10,2},{3,11},{11,3},{4,12},{12,4},... | collective-permute-start | bytes 2408456 | tf_op jit(solution)/shard_map/ppermute | solution.py:32
  689.6 40.4 %collective-permute-start.56 = (bf16[224,1792]{1,0:T(8,128)(2,1)}, bf16[224,1792]{1,0:T(8,128)(2,1)}, u32[]{:S(2)}, u32[]{:S(2)}) collective-permute-start(bf16[224,1792]{1,0:T(8,128)(2,1)} %fusion.27), channel_id=1, source_target_pairs={{0,16},{16,0},{1,17},{17,1},{2,18},{18,2},{3,19},{19,3},{4,20},{20... | collective-permute-start | bytes 2408456 | tf_op jit(solution)/shard_map/ppermute | solution.py:32
  693.2 23.6 %collective-permute-start.57 = (bf16[224,1280]{1,0:T(8,128)(2,1)}, bf16[224,1280]{1,0:T(8,128)(2,1)}, u32[]{:S(2)}, u32[]{:S(2)}) collective-permute-start(bf16[224,1280]{1,0:T(8,128)(2,1)} %reduce-scatter.6.cloned.1.call-done), channel_id=1, source_target_pairs={{0,0},{8,1},{4,2},{12,3},{1,4},{9,5},{5,6},{13,7},{2,8},{10,9},{6,... | collective-permute-start | bytes 1720328 | tf_op jit(solution)/shard_map/ppermute | solution.py:114
  704.1 35.4 %collective-permute-start.53 = (bf16[2,224,1280]{2,1,0:T(8,128)(2,1)}, bf16[2,224,1280]{2,1,0:T(8,128)(2,1)}, u32[]{:S(2)}, u32[]{:S(2)}) collective-permute-start(bf16[2,224,1280]{2,1,0:T(8,128)(2,1)} %fusion.31), channel_id=1, source_target_pairs={{0,16},{16,0},{1,17},{17,1},{2,18},{18,2},{3,19},{19,3},{4,20},{20... | collective-permute-start | bytes 3440648 | tf_op jit(solution)/shard_map/ppermute | solution.py:32
  710.7 24.4 %collective-permute-start.58 = (bf16[224,1280]{1,0:T(8,128)(2,1)}, bf16[224,1280]{1,0:T(8,128)(2,1)S(1)}, u32[]{:S(2)}, u32[]{:S(2)}) collective-permute-start(bf16[224,1280]{1,0:T(8,128)(2,1)} %reduce-scatter.8.cloned.1.call-done), channel_id=1, source_target_pairs={{0,0},{8,1},{4,2},{12,3},{1,4},{9,5},{5,6},{13,7},{2,8},{10,9},{6,... | collective-permute-start | bytes 1720328 | tf_op jit(solution)/shard_map/ppermute | solution.py:114
  716.8 22.7 %collective-permute-start.54 = (bf16[2,224,512]{2,1,0:T(8,128)(2,1)S(1)}, bf16[2,224,512]{2,1,0:T(8,128)(2,1)S(1)}, u32[]{:S(2)}, u32[]{:S(2)}) collective-permute-start(bf16[2,224,512]{2,1,0:T(8,128)(2,1)S(1)} %fusion.54), channel_id=1, source_target_pairs={{0,8},{8,0},{1,9},{9,1},{2,10},{10,2},{3,11},{11,3},{4,12},{12,4},... | collective-permute-start | bytes 1376264 | tf_op jit(solution)/shard_map/ppermute | solution.py:32
  747.1 47.2 %collective-permute-start.60 = (bf16[224,1280]{1,0:T(8,128)(2,1)S(1)}, bf16[224,1280]{1,0:T(8,128)(2,1)}, u32[]{:S(2)}, u32[]{:S(2)}) collective-permute-start(bf16[224,1280]{1,0:T(8,128)(2,1)S(1)} %fusion.44), channel_id=1, source_target_pairs={{0,8},{8,0},{1,9},{9,1},{2,10},{10,2},{3,11},{11,3},{4,12},{12,4},... | collective-permute-start | bytes 1720328 | tf_op jit(solution)/shard_map/ppermute | solution.py:32
  760.7 15.6 %collective-permute-start.62 = (bf16[448,448]{1,0:T(8,128)(2,1)S(1)}, bf16[448,448]{1,0:T(8,128)(2,1)S(1)}, u32[]{:S(2)}, u32[]{:S(2)}) collective-permute-start(bf16[448,448]{1,0:T(8,128)(2,1)S(1)} %get-tuple-element.488), channel_id=1, source_target_pairs={{0,3},{1,0},{2,1},{3,2},{4,7},{5,4},{6,5},{7,6},{8,11},{9,8},{10,9... | collective-permute-start | bytes 1204232 | tf_op jit(solution)/shard_map/ppermute | solution.py:32
  761.0 33.4 %collective-permute-start.63 = (bf16[448,448]{1,0:T(8,128)(2,1)S(1)}, bf16[448,448]{1,0:T(8,128)(2,1)S(1)}, u32[]{:S(2)}, u32[]{:S(2)}) collective-permute-start(bf16[448,448]{1,0:T(8,128)(2,1)S(1)} %get-tuple-element.487), channel_id=1, source_target_pairs={{0,2},{1,3},{2,0},{3,1},{4,6},{5,7},{6,4},{7,5},{8,10},{9,11},{10,... | collective-permute-start | bytes 1204232 | tf_op jit(solution)/shard_map/ppermute | solution.py:32
  763.0 31.4 %collective-permute-start.64 = (bf16[448,448]{1,0:T(8,128)(2,1)S(1)}, bf16[448,448]{1,0:T(8,128)(2,1)S(1)}, u32[]{:S(2)}, u32[]{:S(2)}) collective-permute-start(bf16[448,448]{1,0:T(8,128)(2,1)S(1)} %get-tuple-element.486), channel_id=1, source_target_pairs={{0,1},{1,2},{2,3},{3,0},{4,5},{5,6},{6,7},{7,4},{8,9},{9,10},{10,1... | collective-permute-start | bytes 1204232 | tf_op jit(solution)/shard_map/ppermute | solution.py:32
  799.4 16.5 %collective-permute-start.69 = (bf16[232,448]{1,0:T(8,128)(2,1)S(1)}, bf16[232,448]{1,0:T(8,128)(2,1)S(1)}, u32[]{:S(2)}, u32[]{:S(2)}) collective-permute-start(bf16[232,448]{1,0:T(8,128)(2,1)S(1)} %get-tuple-element.496), channel_id=1, source_target_pairs={{0,1},{1,2},{2,3},{3,0},{4,5},{5,6},{6,7},{7,4},{8,9},{9,10},{10,1... | collective-permute-start | bytes 623624 | tf_op jit(solution)/shard_map/ppermute | solution.py:32
  807.1 23.1 %collective-permute-start.68 = (bf16[232,448]{1,0:T(8,128)(2,1)S(1)}, bf16[232,448]{1,0:T(8,128)(2,1)S(1)}, u32[]{:S(2)}, u32[]{:S(2)}) collective-permute-start(bf16[232,448]{1,0:T(8,128)(2,1)S(1)} %get-tuple-element.497), channel_id=1, source_target_pairs={{0,2},{1,3},{2,0},{3,1},{4,6},{5,7},{6,4},{7,5},{8,10},{9,11},{10,... | collective-permute-start | bytes 623624 | tf_op jit(solution)/shard_map/ppermute | solution.py:32
  810.2 20.1 %collective-permute-start.67 = (bf16[232,448]{1,0:T(8,128)(2,1)S(1)}, bf16[232,448]{1,0:T(8,128)(2,1)S(1)}, u32[]{:S(2)}, u32[]{:S(2)}) collective-permute-start(bf16[232,448]{1,0:T(8,128)(2,1)S(1)} %get-tuple-element.495), channel_id=1, source_target_pairs={{0,3},{1,0},{2,1},{3,2},{4,7},{5,4},{6,5},{7,6},{8,11},{9,8},{10,9... | collective-permute-start | bytes 623624 | tf_op jit(solution)/shard_map/ppermute | solution.py:32
  (113 other events, 1361.0 us)
Sparse Core Ops, SparseCore 0:
  51.6 46.0 all-gather.5
  100.4 46.8 all-gather.7
  149.7 65.8 all-gather.9
  505.0 46.4 reduce-scatter.3
  569.1 48.2 reduce-scatter.5
  641.8 55.4 reduce-scatter.7
where the time goes:
time: 850 us; the launch traced here: 839 us
  waiting for transfers between devices  323 us (38%)
  Pallas kernels  159 us (19%)
  other arithmetic  123 us (14%)
  starting transfers between devices  73.5 us (9%)
  local copies, waits for them, and re-layouts  66.2 us (8%)
  matrix products  38.2 us (4%)
  between operations  29.9 us (4%)
  blocking collectives  26.1 us (3%)
    ppermute x62, waiting for transfers between devices, shift_by(): lax.ppermute(value, axis, [(i, (i + amount) % size) for i in range(size)])  269 us
    pallas_call x4, Pallas kernels, feed_forward(): pl.pallas_call(functools.partial(second_kernel if second else first_kerne...  91.5 us
    ppermute x62, starting transfers between devices, shift_by(): lax.ppermute(value, axis, [(i, (i + amount) % size) for i in range(size)])  60.8 us
    pallas_call x6, Pallas kernels, gradient_half(): pl.pallas_call(functools.partial(gradient_kernel, count=count, extra=len(...  50.6 us
    ppermute x3, waiting for transfers between devices, home(): return lax.ppermute(block, ('b', 'c', 'z'), moves)  27.4 us
    ppermute x5, waiting for transfers between devices, partner(): return lax.ppermute(value, EVERY, [(i, i ^ bit) for i in range(count)])  27 us
    dot_general x4, matrix products, dot_nn(): lax.dot_general(left, right, (((1,), (0,)), ((), ())), preferred_element_...  25.3 us
    unnamed x219, local copies, waits for them, and re-layouts  24.8 us
  transfers between devices with their start and end apart: 76, of which 28 were waited for; matrix products, arithmetic and copies ran while one was open for 22% of the time, Pallas kernels for 18%

commit v1 on v0

--- a/solution.py
+++ b/solution.py
@@ -358,21 +358,17 @@
         return value.reshape(-1, *value.shape[2:])
 
     bits = exchange_order()
-    tap_count = conv_kernel.size
-    told_rows = jnp.concatenate(
-        [
-            tokens[:, length - 2 :, :].reshape(micro * 2, width).astype(F32),
-            jnp.pad(conv_kernel.reshape(1, tap_count), ((0, 0), (0, width - tap_count))),
-        ]
-    )[None]
+    told_rows = tokens[:, length - 2 :, :].reshape(1, micro * 2, width)
     pad_g, pad_u, pad_d = (jnp.pad(w, spare) for w in (ffn_gate, ffn_up, ffn_down))
     z_in = pieces_of(mixer_in, "z")
-    told_rows = told(told_rows, bits[:-3])
+    z_bits = [b for b in bits if b < count_z]
+    told_rows = told(told_rows, z_bits)
+    taps = told(conv_kernel[None], z_bits)
     far_cotangent = pieces_of(cotangent.reshape(rows, width), "b")
     before_at = [entry_of(before[m] ^ place) for m in range(micro)]
     behind_at = [(behind[m] // count_z, behind[m] % count_z) for m in range(micro)]
-    z_in, told_rows, far_cotangent, mixer_gate, mixer_out, pad_g, before_at, behind_at = phase(
-        z_in, told_rows, far_cotangent, mixer_gate, mixer_out, pad_g, before_at, behind_at
+    z_in, told_rows, taps, far_cotangent, mixer_gate, mixer_out, pad_g, before_at, behind_at = phase(
+        z_in, told_rows, taps, far_cotangent, mixer_gate, mixer_out, pad_g, before_at, behind_at
     )
     w_in = rows_of(z_in)
     z_gate = pieces_of(mixer_gate, "z")
@@ -381,7 +377,7 @@
     w_gate = rows_of(z_gate)
     z_out = pieces_of(mixer_out, "z")
     z_g = far_pieces(pad_g, near_g, "z")
-    told_rows = told(told_rows, bits[-3:-2])
+    told_rows = told(told_rows, bits[len(z_bits) : -2])
     z_out, z_g, told_rows, pad_u, pad_d, w_in = phase(z_out, z_g, told_rows, pad_u, pad_d, w_in)
     w_out = rows_of(z_out)
     plane_g = in_plane(in_order(z_g, "z", 0))
@@ -393,9 +389,7 @@
     z_d = pieces_of(pad_d, "z")
     kernel = jnp.concatenate(
         [
-            lax.dynamic_slice(
-                told_rows, (entry_of(place ^ (place - iz + (iz - s) % count_z)), micro * 2, 0), (1, 1, tap_count)
-            ).reshape(3, local)
+            lax.dynamic_index_in_dim(taps, iz ^ ((iz - s) % count_z), 0, keepdims=False)
             for s in range(count_z)
         ],
         axis=1,
@@ -410,7 +404,7 @@
             lax.dynamic_slice(told_rows, (before_at[m], 2 * m, 0), (1, 2, width))[0]
             for m in range(micro)
         ]
-    )
+    ).astype(F32)
     local_in = tokens.reshape(rows, width).astype(F32)
     local_cot = cotangent.reshape(rows, width).astype(F32)
     scale_one = lax.rsqrt(jnp.mean(local_in * local_in, axis=1, keepdims=True) + EPSILON)

time: 850 us -> 839 us (0.987)
  waiting for transfers between devices: 323 us -> 312 us
    ppermute x5 -> x7, waiting for transfers between devices: 27 us -> 11.6 us  [partner(): return lax.ppermute(value, EVERY, [(i, i ^ bit) for i in range(count)])]
    ppermute x3, waiting for transfers between devices: 27.4 us -> 37.7 us  [home(): return lax.ppermute(block, ('b', 'c', 'z'), moves)]
    unnamed x219 -> x221, local copies, waits for them, and re-layouts: 24.8 us -> 25 us
  transfers between devices with their start and end apart: 76 -> 78, of which waited for: 28 -> 28; matrix products, arithmetic and copies ran while one was open for 22% -> 22% of each run, Pallas kernels for 18% -> 18%
where the time goes in v1:
time: 839 us; the launch traced here: 828 us
  waiting for transfers between devices  312 us (37%)
  Pallas kernels  159 us (19%)
  other arithmetic  120 us (14%)
  starting transfers between devices  78.5 us (9%)
  local copies, waits for them, and re-layouts  62.9 us (7%)
  matrix products  38.4 us (5%)
  between operations  29.7 us (4%)
  blocking collectives  26.4 us (3%)
    ppermute x62, waiting for transfers between devices, shift_by(): lax.ppermute(value, axis, [(i, (i + amount) % size) for i in range(size)])  263 us
    pallas_call x4, Pallas kernels, feed_forward(): pl.pallas_call(functools.partial(second_kernel if second else first_kerne...  91.7 us
    ppermute x62, starting transfers between devices, shift_by(): lax.ppermute(value, axis, [(i, (i + amount) % size) for i in range(size)])  63.9 us
    pallas_call x6, Pallas kernels, gradient_half(): pl.pallas_call(functools.partial(gradient_kernel, count=count, extra=len(...  50.6 us
    ppermute x3, waiting for transfers between devices, home(): return lax.ppermute(block, ('b', 'c', 'z'), moves)  37.7 us
    dot_general x4, matrix products, dot_nn(): lax.dot_general(left, right, (((1,), (0,)), ((), ())), preferred_element_...  25.4 us
    unnamed x221, local copies, waits for them, and re-layouts  25 us
    another operation x15, other arithmetic, in_order(): jnp.stack([jnp.where(first, pieces[0], pieces[1]), jnp.where(first, piece...  23.2 us
  transfers between devices with their start and end apart: 78, of which 28 were waited for; matrix products, arithmetic and copies ran while one was open for 22% of the time, Pallas kernels for 18%

profile of v1, /device:TPU:30, one launch (start us, length us, event | category | flops | bytes accessed | tf_op | source)
XLA Modules:
  0.0 827.9 jit_solution(14745234026168325618)
XLA Ops:
  43.9 5.5 collective-permute-done.7.refs_3_.refs_0_
  57.1 25.3 %collective-permute-done.8 = bf16[224,448]{1,0:T(8,128)(2,1)S(1)} collective-permute-done((bf16[224,448]{1,0:T(8,128)(2,1)S(1)}, bf16[224,448]{1,0:T(8,128)(2,1)S(1)}, u32[]{:S(2)}, u32[]{:S(2)}) %collective-permute-start.8) | collective-permute-done | bytes 200736 | tf_op jit(solution)/shard_map/ppermute | solution.py:32
  82.5 13.9 %collective-permute-done.9 = bf16[224,448]{1,0:T(8,128)(2,1)S(1)} collective-permute-done((bf16[224,448]{1,0:T(8,128)(2,1)S(1)}, bf16[224,448]{1,0:T(8,128)(2,1)S(1)}, u32[]{:S(2)}, u32[]{:S(2)}) %collective-permute-start.9) | collective-permute-done | bytes 200736 | tf_op jit(solution)/shard_map/ppermute | solution.py:32
  104.3 13.5 %collective-permute-done.13 = bf16[224,448]{1,0:T(8,128)(2,1)S(1)} collective-permute-done((bf16[224,448]{1,0:T(8,128)(2,1)S(1)}, bf16[224,448]{1,0:T(8,128)(2,1)S(1)}, u32[]{:S(2)}, u32[]{:S(2)}) %collective-permute-start.13) | collective-permute-done | bytes 200736 | tf_op jit(solution)/shard_map/ppermute | solution.py:32
  117.9 15.6 %collective-permute-done.14 = bf16[224,448]{1,0:T(8,128)(2,1)S(1)} collective-permute-done((bf16[224,448]{1,0:T(8,128)(2,1)S(1)}, bf16[224,448]{1,0:T(8,128)(2,1)S(1)}, u32[]{:S(2)}, u32[]{:S(2)}) %collective-permute-start.14) | collective-permute-done | bytes 200736 | tf_op jit(solution)/shard_map/ppermute | solution.py:32
  148.9 3.8 collective-permute-done.23
  152.8 8.2 fusion.2
  162.0 30.8 %collective-permute-done.21 = bf16[224,1280]{1,0:T(8,128)(2,1)} collective-permute-done((bf16[224,1280]{1,0:T(8,128)(2,1)}, bf16[224,1280]{1,0:T(8,128)(2,1)}, u32[]{:S(2)}, u32[]{:S(2)}) %collective-permute-start.21) | collective-permute-done | bytes 573472 | tf_op jit(solution)/shard_map/ppermute | solution.py:32
  193.0 3.1 collective-permute-start.29
  211.5 9.2 %multiply_convert_fusion.2 = (bf16[4,128,1792]{2,1,0:T(8,128)(2,1)S(1)}, f32[4,128,1792]{2,1,0:T(8,128)}, f32[4,128,1792]{2,1,0:T(8,128)}) fusion(f32[4,128,1792]{2,1,0:T(8,128)S(1)} %copy-done.42, f32[4,2,1792]{2,1,0:T(2,128)S(1)} %copy-done.62, f32[4,128]{1,0:T(4,128)S(1)} %copy-done.81, f32[1792]{0:T(1024)S(1)} %copy-done.75, ...), kind=kOutput, calls=%fused_computation.57 | convolution fusion | flops 3302096896 | bytes 21194752 | tf_op jit(solution)/shard_map/dot_general | solution.py:19
  220.7 25.7 %collective-permute-done.29 = bf16[224,1280]{1,0:T(8,128)(2,1)} collective-permute-done((bf16[224,1280]{1,0:T(8,128)(2,1)}, bf16[224,1280]{1,0:T(8,128)(2,1)}, u32[]{:S(2)}, u32[]{:S(2)}) %collective-permute-start.29) | collective-permute-done | bytes 573472 | tf_op jit(solution)/shard_map/ppermute | solution.py:32
  246.4 10.4 %collective-permute-done.25 = bf16[4,224,1280]{2,1,0:T(8,128)(2,1)} collective-permute-done((bf16[4,224,1280]{2,1,0:T(8,128)(2,1)}, bf16[4,224,1280]{2,1,0:T(8,128)(2,1)}, u32[]{:S(2)}, u32[]{:S(2)}) %collective-permute-start.25) | collective-permute-done | bytes 2293792 | tf_op jit(solution)/shard_map/ppermute | solution.py:32
  262.3 3.7 multiply_reduce_fusion.5
  265.9 4.0 select_bitcast_fusion.5
  273.7 24.1 %collective-permute-done.34 = bf16[2,224,1280]{2,1,0:T(8,128)(2,1)S(1)} collective-permute-done((bf16[2,224,1280]{2,1,0:T(8,128)(2,1)S(1)}, bf16[2,224,1280]{2,1,0:T(8,128)(2,1)S(1)}, u32[]{:S(2)}, u32[]{:S(2)}) %collective-permute-start.34) | collective-permute-done | bytes 1146912 | tf_op jit(solution)/shard_map/ppermute | solution.py:32
  297.8 15.3 %collective-permute-done.35 = bf16[4,224,1280]{2,1,0:T(8,128)(2,1)S(1)} collective-permute-done((bf16[4,224,1280]{2,1,0:T(8,128)(2,1)S(1)}, bf16[4,224,1280]{2,1,0:T(8,128)(2,1)S(1)}, u32[]{:S(2)}, u32[]{:S(2)}) %collective-permute-start.35) | collective-permute-done | bytes 2293792 | tf_op jit(solution)/shard_map/ppermute | solution.py:32
  319.2 15.6 %first_half.2 = (bf16[2048,1280]{1,0:T(8,128)(2,1)}, bf16[2048,1280]{1,0:T(8,128)(2,1)}, bf16[2048,1280]{1,0:T(8,128)(2,1)}) custom-call(bf16[512,1792]{1,0:T(8,128)(2,1)} %copy-done, bf16[512,1792]{1,0:T(8,128)(2,1)} %copy-done.2, bf16[1792,1280]{1,0:T(8,128)(2,1)} %bitcast.343, bf16[1792,1280]{1,0:T(8,128)(2,1)} %bitcast.347), custom_call_target="tpu_custom_call" | custom-call | flops 18790481920 | bytes 25952256 | tf_op jit(solution)/shard_map/first_half/pallas_call | solution.py:192
  334.8 19.9 %collective-permute-done.37.refs_0_.refs_3_ = bf16[512,1792]{1,0:T(8,128)(2,1)} collective-permute-done((bf16[512,1792]{1,0:T(8,128)(2,1)S(1)}, bf16[512,1792]{1,0:T(8,128)(2,1)}, u32[]{:S(2)}, u32[]{:S(2)}) %collective-permute-start.37) | collective-permute-done | bytes 1835040 | tf_op jit(solution)/shard_map/ppermute | solution.py:32
  354.6 11.8 %collective-permute-done.36 = bf16[4,224,1280]{2,1,0:T(8,128)(2,1)} collective-permute-done((bf16[4,224,1280]{2,1,0:T(8,128)(2,1)S(1)}, bf16[4,224,1280]{2,1,0:T(8,128)(2,1)}, u32[]{:S(2)}, u32[]{:S(2)}) %collective-permute-start.36) | collective-permute-done | bytes 2293792 | tf_op jit(solution)/shard_map/ppermute | solution.py:32
  366.5 3.5 fusion.15.left
  376.8 16.0 %first_half.3 = (bf16[2048,1280]{1,0:T(8,128)(2,1)}, bf16[2048,1280]{1,0:T(8,128)(2,1)}, bf16[2048,1280]{1,0:T(8,128)(2,1)}) custom-call(bf16[512,1792]{1,0:T(8,128)(2,1)} %collective-permute-done.37.refs_0_.refs_3_, bf16[512,1792]{1,0:T(8,128)(2,1)} %copy-done.5, ...), custom_call_target="tpu_custom_call", output_to_operand_aliasing={{0}: (4, {}), {1}: (5, {}), {2}: (6, {})} | custom-call | flops 18790481920 | bytes 25952256 | tf_op jit(solution)/shard_map/first_half/pallas_call | solution.py:192
  392.8 9.3 %gradient_half.6 = bf16[896,1280]{1,0:T(8,128)(2,1)} custom-call(s32[1]{0:T(128)} %bitcast.47.refs_0_, bf16[512,1792]{1,0:T(8,128)(2,1)S(1)} %bitcast.321, bf16[512,1792]{1,0:T(8,128)(2,1)} %collective-permute-done.31.refs_2_.refs_1_, bf16[512,1792]{1,0:T(8,128)(2,1)} %collective-permute-done.7.refs_3_.refs_0_, ...), custom_call_target="tpu_custom_call" | custom-call | flops 4697620480 | bytes 11206656 | tf_op jit(solution)/shard_map/gradient_half/pallas_call | solution.py:232
  402.7 29.9 %second_half.2 = (bf16[2048,2560]{1,0:T(8,128)(2,1)}, bf16[512,1792]{1,0:T(8,128)(2,1)}, bf16[512,1792]{1,0:T(8,128)(2,1)}, bf16[512,1792]{1,0:T(8,128)(2,1)}, bf16[512,1792]{1,0:T(8,128)(2,1)}) custom-call(bf16[512,1792]{1,0:T(8,128)(2,1)} %collective-permute-done.7.refs_3_.refs_0_, bf16[512,1792]{1,0:T(8,128)(2,1)} %collective-permute-done.32.refs_4_.refs_1_, ...), custom_call_target="tpu_custom_call" | custom-call | flops 37580963840 | bytes 30539776 | tf_op jit(solution)/shard_map/second_half/pallas_call | solution.py:192
  433.1 30.2 %second_half.3 = (bf16[2048,2560]{1,0:T(8,128)(2,1)}, bf16[512,1792]{1,0:T(8,128)(2,1)}, bf16[512,1792]{1,0:T(8,128)(2,1)}, bf16[512,1792]{1,0:T(8,128)(2,1)}, bf16[512,1792]{1,0:T(8,128)(2,1)}) custom-call(bf16[512,1792]{1,0:T(8,128)(2,1)} %bitcast.319, bf16[512,1792]{1,0:T(8,128)(2,1)} %collective-permute-done.31.refs_2_.refs_1_, ...), custom_call_target="tpu_custom_call", output_to_operand_aliasing={{0}: (8, {})} | custom-call | flops 37580963840 | bytes 30539776 | tf_op jit(solution)/shard_map/second_half/pallas_call | solution.py:192
  465.3 8.8 %gradient_half.7 = bf16[896,1280]{1,0:T(8,128)(2,1)} custom-call(s32[1]{0:T(128)} %bitcast.47.refs_0_, bf16[512,1792]{1,0:T(8,128)(2,1)S(1)} %copy-done.1, bf16[512,1792]{1,0:T(8,128)(2,1)S(1)} %copy-done.3, bf16[512,1792]{1,0:T(8,128)(2,1)} %collective-permute-done.37.refs_0_.refs_3_, bf16[512,1792]{1,0:T(8,128)(2,1)S(1)} %copy-done.6, ...), custom_call_target="tpu_custom_call" | custom-call | flops 4697620480 | bytes 11206656 | tf_op jit(solution)/shard_map/gradient_half/pallas_call | solution.py:232
  475.6 3.1 add_convert_fusion.5
  480.3 8.1 gradient_half.11
  488.4 3.6 add_convert_fusion.2
  495.1 9.0 %gradient_half.8 = bf16[896,1280]{1,0:T(8,128)(2,1)} custom-call(s32[1]{0:T(128)} %bitcast.47.refs_0_, bf16[512,1792]{1,0:T(8,128)(2,1)S(1)} %copy-done.1, bf16[512,1792]{1,0:T(8,128)(2,1)S(1)} %copy-done.4, bf16[512,1792]{1,0:T(8,128)(2,1)} %collective-permute-done.37.refs_0_.refs_3_, bf16[512,1792]{1,0:T(8,128)(2,1)S(1)} %copy-done.7, ...), custom_call_target="tpu_custom_call" | custom-call | flops 4697620480 | bytes 11206656 | tf_op jit(solution)/shard_map/gradient_half/pallas_call | solution.py:232
  504.1 7.7 gradient_half.9
  511.8 7.8 gradient_half.10
  519.6 4.1 add_convert_fusion.4
  529.4 3.6 multiply_reduce_fusion.3
  533.0 3.7 add_convert_fusion.1
  536.7 5.9 fusion.94
  542.7 7.0 fusion.101
  549.7 3.8 multiply_reduce_fusion
  559.2 5.4 split_gradient.3
  566.4 5.5 split_gradient.4
  571.9 5.4 fusion.102
  579.0 14.7 %all-gather = bf16[32,1792]{1,0:T(8,128)(2,1)S(1)} all-gather(bf16[8,1792]{1,0:T(8,128)(2,1)S(1)} %concatenate.111), channel_id=2, replica_groups=mesh['a'=2,'b'=2,'c'=2,'z'=4] {'z'}, dimensions={0}, use_global_device_ids=true | all-gather | bytes 143360 | tf_op jit(solution)/shard_map/all_gather | solution.py:343
  593.6 11.7 %all-gather.1 = bf16[32,8,1792]{2,1,0:T(8,128)(2,1)} all-gather(bf16[4,8,1792]{2,1,0:T(8,128)(2,1)S(1)} %bitcast.356), channel_id=3, replica_groups=mesh['a'=2,'b'=2,'c'=2,'z'=4] {'a','b','c'}, dimensions={0}, use_global_device_ids=true | all-gather | bytes 1032192 | tf_op jit(solution)/shard_map/all_gather | solution.py:343
  605.4 3.1 fusion.25
  609.8 3.0 fusion.26
  615.2 4.7 fusion.7
  624.6 3.7 add_convert_fusion
  629.0 5.2 fusion.10
  636.0 4.0 fusion.20
  640.0 6.2 split_gradient.5
  649.0 20.7 %collective-permute-done.53 = bf16[224,1280]{1,0:T(8,128)(2,1)} collective-permute-done((bf16[224,1280]{1,0:T(8,128)(2,1)}, bf16[224,1280]{1,0:T(8,128)(2,1)}, u32[]{:S(2)}, u32[]{:S(2)}) %collective-permute-start.53) | collective-permute-done | bytes 573472 | tf_op jit(solution)/shard_map/ppermute | solution.py:114
  674.9 2.8 fusion.27
  677.8 4.1 collective-permute-start.58
  691.3 4.2 collective-permute-start.61
  702.3 15.4 %collective-permute-done.59 = bf16[224,1280]{1,0:T(8,128)(2,1)} collective-permute-done((bf16[224,1280]{1,0:T(8,128)(2,1)}, bf16[224,1280]{1,0:T(8,128)(2,1)}, u32[]{:S(2)}, u32[]{:S(2)}) %collective-permute-start.59) | collective-permute-done | bytes 573472 | tf_op jit(solution)/shard_map/ppermute | solution.py:114
  723.8 3.8 collective-permute-done.56
  739.8 4.1 collective-permute-start.67
  749.7 3.7 collective-permute-start.66
  753.7 3.5 collective-permute-done.68
  757.3 5.9 collective-permute-done.63
  764.9 18.0 %collective-permute-done.65 = bf16[448,448]{1,0:T(8,128)(2,1)S(1)} collective-permute-done((bf16[448,448]{1,0:T(8,128)(2,1)S(1)}, bf16[448,448]{1,0:T(8,128)(2,1)S(1)}, u32[]{:S(2)}, u32[]{:S(2)}) %collective-permute-start.65) | collective-permute-done | bytes 401440 | tf_op jit(solution)/shard_map/ppermute | solution.py:32
  788.0 6.1 collective-permute-start.71
  794.1 4.7 collective-permute-start.70
  798.8 4.4 add_convert_fusion.3
  804.5 14.3 %collective-permute-done.70 = bf16[232,448]{1,0:T(8,128)(2,1)S(1)} collective-permute-done((bf16[232,448]{1,0:T(8,128)(2,1)S(1)}, bf16[232,448]{1,0:T(8,128)(2,1)S(1)}, u32[]{:S(2)}, u32[]{:S(2)}) %collective-permute-start.70) | collective-permute-done | bytes 207904 | tf_op jit(solution)/shard_map/ppermute | solution.py:32
  (516 shorter events, 185.4 us)
Async XLA Ops:
  7.2 127.0 %all-gather.6.cloned.1.call-start = ((), (), s32[]{:S(2)}) async-start(), calls=%async_computation.3 | async-start | bytes 7225344 | tf_op jit(solution)/shard_map/all_gather | solution.py:340
  7.2 42.1 %collective-permute-start.7 = (bf16[512,1792]{1,0:T(8,128)(2,1)}, bf16[512,1792]{1,0:T(8,128)(2,1)}, u32[]{:S(2)}, u32[]{:S(2)}) collective-permute-start(bf16[512,1792]{1,0:T(8,128)(2,1)} %bitcast.318), channel_id=1, source_target_pairs={{0,8},{8,0},{1,9},{9,1},{2,10},{10,2},{3,11},{11,3},{4,12},{12,4},... | collective-permute-start | bytes 5505032 | tf_op jit(solution)/shard_map/ppermute | solution.py:32
  7.8 36.0 %collective-permute-start = (bf16[224,448]{1,0:T(8,128)(2,1)}, bf16[224,448]{1,0:T(8,128)(2,1)S(1)}, u32[]{:S(2)}, u32[]{:S(2)}) collective-permute-start(bf16[224,448]{1,0:T(8,128)(2,1)} %param.18), channel_id=1, source_target_pairs={{0,1},{1,2},{2,3},{3,0},{4,5},{5,6},{6,7},{7,4},{8,9},{9,10},{10,1... | collective-permute-start | bytes 602120 | tf_op jit(solution)/shard_map/ppermute | solution.py:32
  8.1 35.8 %collective-permute-start.1 = (bf16[224,448]{1,0:T(8,128)(2,1)}, bf16[224,448]{1,0:T(8,128)(2,1)S(1)}, u32[]{:S(2)}, u32[]{:S(2)}) collective-permute-start(bf16[224,448]{1,0:T(8,128)(2,1)} %param.18), channel_id=1, source_target_pairs={{0,2},{1,3},{2,0},{3,1},{4,6},{5,7},{6,4},{7,5},{8,10},{9,11},{10,... | collective-permute-start | bytes 602120 | tf_op jit(solution)/shard_map/ppermute | solution.py:32
  9.7 34.2 %collective-permute-start.2 = (bf16[224,448]{1,0:T(8,128)(2,1)}, bf16[224,448]{1,0:T(8,128)(2,1)S(1)}, u32[]{:S(2)}, u32[]{:S(2)}) collective-permute-start(bf16[224,448]{1,0:T(8,128)(2,1)} %param.18), channel_id=1, source_target_pairs={{0,3},{1,0},{2,1},{3,2},{4,7},{5,4},{6,5},{7,6},{8,11},{9,8},{10,9... | collective-permute-start | bytes 602120 | tf_op jit(solution)/shard_map/ppermute | solution.py:32
  10.2 19.4 %collective-permute-start.5 = (f32[1,3,448]{2,1,0:T(4,128)}, f32[1,3,448]{2,1,0:T(4,128)S(1)}, u32[]{:S(2)}, u32[]{:S(2)}) collective-permute-start(f32[1,3,448]{2,1,0:T(4,128)} %bitcast.371), channel_id=1, source_target_pairs={{0,1},{1,0},{2,3},{3,2},{4,5},{5,4},{6,7},{7,6},{8,9},{9,8},{10,11... | collective-permute-start | bytes 16136 | tf_op jit(solution)/shard_map/ppermute | solution.py:119
  50.6 142.3 %all-gather.8.cloned.1.call-start = ((), (), s32[]{:S(2)}) async-start(), calls=%async_computation.4 | async-start | bytes 7225344 | tf_op jit(solution)/shard_map/all_gather | solution.py:340
  50.7 45.7 %collective-permute-start.11 = (bf16[224,1280]{1,0:T(8,128)(2,1)S(1)}, bf16[224,1280]{1,0:T(8,128)(2,1)S(1)}, u32[]{:S(2)}, u32[]{:S(2)}) collective-permute-start(bf16[224,1280]{1,0:T(8,128)(2,1)S(1)} %pad.14), channel_id=1, source_target_pairs={{0,1},{1,2},{2,3},{3,0},{4,5},{5,6},{6,7},{7,4},{8,9},{9,10},{10,1... | collective-permute-start | bytes 1720328 | tf_op jit(solution)/shard_map/ppermute | solution.py:32
  50.9 46.2 %collective-permute-start.12 = (bf16[224,1280]{1,0:T(8,128)(2,1)S(1)}, bf16[224,1280]{1,0:T(8,128)(2,1)S(1)}, u32[]{:S(2)}, u32[]{:S(2)}) collective-permute-start(bf16[224,1280]{1,0:T(8,128)(2,1)S(1)} %pad.14), channel_id=1, source_target_pairs={{0,3},{1,0},{2,1},{3,2},{4,7},{5,4},{6,5},{7,6},{8,11},{9,8},{10,9... | collective-permute-start | bytes 1720328 | tf_op jit(solution)/shard_map/ppermute | solution.py:32
  52.8 29.7 %collective-permute-start.8 = (bf16[224,448]{1,0:T(8,128)(2,1)S(1)}, bf16[224,448]{1,0:T(8,128)(2,1)S(1)}, u32[]{:S(2)}, u32[]{:S(2)}) collective-permute-start(bf16[224,448]{1,0:T(8,128)(2,1)S(1)} %copy-done.65), channel_id=1, source_target_pairs={{0,1},{1,2},{2,3},{3,0},{4,5},{5,6},{6,7},{7,4},{8,9},{9,10},{10,1... | collective-permute-start | bytes 602120 | tf_op jit(solution)/shard_map/ppermute | solution.py:32
  54.8 41.6 %collective-permute-start.9 = (bf16[224,448]{1,0:T(8,128)(2,1)S(1)}, bf16[224,448]{1,0:T(8,128)(2,1)S(1)}, u32[]{:S(2)}, u32[]{:S(2)}) collective-permute-start(bf16[224,448]{1,0:T(8,128)(2,1)S(1)} %copy-done.65), channel_id=1, source_target_pairs={{0,2},{1,3},{2,0},{3,1},{4,6},{5,7},{6,4},{7,5},{8,10},{9,11},{10,... | collective-permute-start | bytes 602120 | tf_op jit(solution)/shard_map/ppermute | solution.py:32
  54.8 41.6 %collective-permute-start.10 = (bf16[224,448]{1,0:T(8,128)(2,1)S(1)}, bf16[224,448]{1,0:T(8,128)(2,1)S(1)}, u32[]{:S(2)}, u32[]{:S(2)}) collective-permute-start(bf16[224,448]{1,0:T(8,128)(2,1)S(1)} %copy-done.65), channel_id=1, source_target_pairs={{0,3},{1,0},{2,1},{3,2},{4,7},{5,4},{6,5},{7,6},{8,11},{9,8},{10,9... | collective-permute-start | bytes 602120 | tf_op jit(solution)/shard_map/ppermute | solution.py:32
  99.4 157.5 %all-gather.10.cloned.1.call-start = ((), (), s32[]{:S(2)}) async-start(), calls=%async_computation.5 | async-start | bytes 7225344 | tf_op jit(solution)/shard_map/all_gather | solution.py:340
  99.4 34.8 %collective-permute-start.16 = (bf16[224,1280]{1,0:T(8,128)(2,1)S(1)}, bf16[224,1280]{1,0:T(8,128)(2,1)S(1)}, u32[]{:S(2)}, u32[]{:S(2)}) collective-permute-start(bf16[224,1280]{1,0:T(8,128)(2,1)S(1)} %collective-permute-done.11), channel_id=1, source_target_pairs={{0,1},{1,2},{2,3},{3,0},{4,5},{5,6},{6,7},{7,4},{8,9},{9,10},{10,1... | collective-permute-start | bytes 1720328 | tf_op jit(solution)/shard_map/ppermute | solution.py:32
  100.0 17.9 %collective-permute-start.13 = (bf16[224,448]{1,0:T(8,128)(2,1)S(1)}, bf16[224,448]{1,0:T(8,128)(2,1)S(1)}, u32[]{:S(2)}, u32[]{:S(2)}) collective-permute-start(bf16[224,448]{1,0:T(8,128)(2,1)S(1)} %copy-done.66), channel_id=1, source_target_pairs={{0,1},{1,2},{2,3},{3,0},{4,5},{5,6},{6,7},{7,4},{8,9},{9,10},{10,1... | collective-permute-start | bytes 602120 | tf_op jit(solution)/shard_map/ppermute | solution.py:32
  102.6 30.8 %collective-permute-start.14 = (bf16[224,448]{1,0:T(8,128)(2,1)S(1)}, bf16[224,448]{1,0:T(8,128)(2,1)S(1)}, u32[]{:S(2)}, u32[]{:S(2)}) collective-permute-start(bf16[224,448]{1,0:T(8,128)(2,1)S(1)} %copy-done.66), channel_id=1, source_target_pairs={{0,2},{1,3},{2,0},{3,1},{4,6},{5,7},{6,4},{7,5},{8,10},{9,11},{10,... | collective-permute-start | bytes 602120 | tf_op jit(solution)/shard_map/ppermute | solution.py:32
  103.5 30.0 %collective-permute-start.15 = (bf16[224,448]{1,0:T(8,128)(2,1)S(1)}, bf16[224,448]{1,0:T(8,128)(2,1)S(1)}, u32[]{:S(2)}, u32[]{:S(2)}) collective-permute-start(bf16[224,448]{1,0:T(8,128)(2,1)S(1)} %copy-done.66), channel_id=1, source_target_pairs={{0,3},{1,0},{2,1},{3,2},{4,7},{5,4},{6,5},{7,6},{8,11},{9,8},{10,9... | collective-permute-start | bytes 602120 | tf_op jit(solution)/shard_map/ppermute | solution.py:32
  136.3 441.7 %reduce-scatter.4.cloned.1.call-start = ((), (), s32[]{:S(2)}) async-start(), calls=%async_computation.6 | async-start | bytes 2867200 | tf_op jit(solution)/shard_map/reduce_scatter | solution.py:468
  142.2 19.9 %collective-permute-start.20 = (bf16[224,1280]{1,0:T(8,128)(2,1)}, bf16[224,1280]{1,0:T(8,128)(2,1)}, u32[]{:S(2)}, u32[]{:S(2)}) collective-permute-start(bf16[224,1280]{1,0:T(8,128)(2,1)} %pad.15), channel_id=1, source_target_pairs={{0,1},{1,2},{2,3},{3,0},{4,5},{5,6},{6,7},{7,4},{8,9},{9,10},{10,1... | collective-permute-start | bytes 1720328 | tf_op jit(solution)/shard_map/ppermute | solution.py:32
  142.2 50.7 %collective-permute-start.21 = (bf16[224,1280]{1,0:T(8,128)(2,1)}, bf16[224,1280]{1,0:T(8,128)(2,1)}, u32[]{:S(2)}, u32[]{:S(2)}) collective-permute-start(bf16[224,1280]{1,0:T(8,128)(2,1)} %pad.15), channel_id=1, source_target_pairs={{0,2},{1,3},{2,0},{3,1},{4,6},{5,7},{6,4},{7,5},{8,10},{9,11},{10,... | collective-permute-start | bytes 1720328 | tf_op jit(solution)/shard_map/ppermute | solution.py:32
  142.2 50.7 %collective-permute-start.22 = (bf16[224,1280]{1,0:T(8,128)(2,1)}, bf16[224,1280]{1,0:T(8,128)(2,1)}, u32[]{:S(2)}, u32[]{:S(2)}) collective-permute-start(bf16[224,1280]{1,0:T(8,128)(2,1)} %pad.15), channel_id=1, source_target_pairs={{0,3},{1,0},{2,1},{3,2},{4,7},{5,4},{6,5},{7,6},{8,11},{9,8},{10,9... | collective-permute-start | bytes 1720328 | tf_op jit(solution)/shard_map/ppermute | solution.py:32
  147.4 45.5 %collective-permute-start.19 = (bf16[2,224,1280]{2,1,0:T(8,128)(2,1)}, bf16[2,224,1280]{2,1,0:T(8,128)(2,1)}, u32[]{:S(2)}, u32[]{:S(2)}) collective-permute-start(bf16[2,224,1280]{2,1,0:T(8,128)(2,1)} %get-tuple-element.474), channel_id=1, source_target_pairs={{0,8},{8,0},{1,9},{9,1},{2,10},{10,2},{3,11},{11,3},{4,12},{12,4},... | collective-permute-start | bytes 3440648 | tf_op jit(solution)/shard_map/ppermute | solution.py:32
  192.9 27.8 %collective-permute-start.28 = (bf16[224,1280]{1,0:T(8,128)(2,1)}, bf16[224,1280]{1,0:T(8,128)(2,1)}, u32[]{:S(2)}, u32[]{:S(2)}) collective-permute-start(bf16[224,1280]{1,0:T(8,128)(2,1)} %pad.16), channel_id=1, source_target_pairs={{0,1},{1,2},{2,3},{3,0},{4,5},{5,6},{6,7},{7,4},{8,9},{9,10},{10,1... | collective-permute-start | bytes 1720328 | tf_op jit(solution)/shard_map/ppermute | solution.py:32
  193.0 53.4 %collective-permute-start.29 = (bf16[224,1280]{1,0:T(8,128)(2,1)}, bf16[224,1280]{1,0:T(8,128)(2,1)}, u32[]{:S(2)}, u32[]{:S(2)}) collective-permute-start(bf16[224,1280]{1,0:T(8,128)(2,1)} %pad.16), channel_id=1, source_target_pairs={{0,2},{1,3},{2,0},{3,1},{4,6},{5,7},{6,4},{7,5},{8,10},{9,11},{10,... | collective-permute-start | bytes 1720328 | tf_op jit(solution)/shard_map/ppermute | solution.py:32
  196.1 50.3 %collective-permute-start.30 = (bf16[224,1280]{1,0:T(8,128)(2,1)}, bf16[224,1280]{1,0:T(8,128)(2,1)}, u32[]{:S(2)}, u32[]{:S(2)}) collective-permute-start(bf16[224,1280]{1,0:T(8,128)(2,1)} %pad.16), channel_id=1, source_target_pairs={{0,3},{1,0},{2,1},{3,2},{4,7},{5,4},{6,5},{7,6},{8,11},{9,8},{10,9... | collective-permute-start | bytes 1720328 | tf_op jit(solution)/shard_map/ppermute | solution.py:32
  204.9 51.9 %collective-permute-start.25 = (bf16[4,224,1280]{2,1,0:T(8,128)(2,1)}, bf16[4,224,1280]{2,1,0:T(8,128)(2,1)}, u32[]{:S(2)}, u32[]{:S(2)}) collective-permute-start(bf16[4,224,1280]{2,1,0:T(8,128)(2,1)} %bitcast.35), channel_id=1, source_target_pairs={{0,16},{16,0},{1,17},{17,1},{2,18},{18,2},{3,19},{19,3},{4,20},{20... | collective-permute-start | bytes 6881288 | tf_op jit(solution)/shard_map/ppermute | solution.py:32
  210.0 36.4 %collective-permute-start.27 = (bf16[2,224,1280]{2,1,0:T(8,128)(2,1)S(1)}, bf16[2,224,1280]{2,1,0:T(8,128)(2,1)}, u32[]{:S(2)}, u32[]{:S(2)}) collective-permute-start(bf16[2,224,1280]{2,1,0:T(8,128)(2,1)S(1)} %get-tuple-element.466), channel_id=1, source_target_pairs={{0,8},{8,0},{1,9},{9,1},{2,10},{10,2},{3,11},{11,3},{4,12},{12,4},... | collective-permute-start | bytes 3440648 | tf_op jit(solution)/shard_map/ppermute | solution.py:32
  259.0 10.9 %collective-permute-start.33 = (bf16[2,224,1280]{2,1,0:T(8,128)(2,1)S(1)}, bf16[2,224,1280]{2,1,0:T(8,128)(2,1)S(1)}, u32[]{:S(2)}, u32[]{:S(2)}) collective-permute-start(bf16[2,224,1280]{2,1,0:T(8,128)(2,1)S(1)} %dynamic-slice_bitcast_fusion.6), channel_id=1, source_target_pairs={{0,4},{4,0},{1,5},{5,1},{2,6},{6,2},{3,7},{7,3},{8,12},{12,8},{9,1... | collective-permute-start | bytes 3440648 | tf_op jit(solution)/shard_map/ppermute | solution.py:32
  260.9 52.2 %collective-permute-start.35 = (bf16[4,224,1280]{2,1,0:T(8,128)(2,1)S(1)}, bf16[4,224,1280]{2,1,0:T(8,128)(2,1)S(1)}, u32[]{:S(2)}, u32[]{:S(2)}) collective-permute-start(bf16[4,224,1280]{2,1,0:T(8,128)(2,1)S(1)} %bitcast.331), channel_id=1, source_target_pairs={{0,16},{16,0},{1,17},{17,1},{2,18},{18,2},{3,19},{19,3},{4,20},{20... | collective-permute-start | bytes 6881288 | tf_op jit(solution)/shard_map/ppermute | solution.py:32
  270.3 27.5 %collective-permute-start.34 = (bf16[2,224,1280]{2,1,0:T(8,128)(2,1)S(1)}, bf16[2,224,1280]{2,1,0:T(8,128)(2,1)S(1)}, u32[]{:S(2)}, u32[]{:S(2)}) collective-permute-start(bf16[2,224,1280]{2,1,0:T(8,128)(2,1)S(1)} %get-tuple-element.460), channel_id=1, source_target_pairs={{0,8},{8,0},{1,9},{9,1},{2,10},{10,2},{3,11},{11,3},{4,12},{12,4},... | collective-permute-start | bytes 3440648 | tf_op jit(solution)/shard_map/ppermute | solution.py:32
  313.1 41.6 %collective-permute-start.37 = (bf16[512,1792]{1,0:T(8,128)(2,1)S(1)}, bf16[512,1792]{1,0:T(8,128)(2,1)}, u32[]{:S(2)}, u32[]{:S(2)}) collective-permute-start(bf16[512,1792]{1,0:T(8,128)(2,1)S(1)} %multiply_convert_fusion.1.refs_0_.refs_1_), channel_id=1, source_target_pairs={{0,8},{8,0},{1,9},{9,1},{2,10},{10,2},{3,11},{11,3},{4,12},{12,4},... | collective-permute-start | bytes 5505032 | tf_op jit(solution)/shard_map/ppermute | solution.py:32
  314.0 52.4 %collective-permute-start.36 = (bf16[4,224,1280]{2,1,0:T(8,128)(2,1)S(1)}, bf16[4,224,1280]{2,1,0:T(8,128)(2,1)}, u32[]{:S(2)}, u32[]{:S(2)}) collective-permute-start(bf16[4,224,1280]{2,1,0:T(8,128)(2,1)S(1)} %bitcast.333), channel_id=1, source_target_pairs={{0,16},{16,0},{1,17},{17,1},{2,18},{18,2},{3,19},{19,3},{4,20},{20... | collective-permute-start | bytes 6881288 | tf_op jit(solution)/shard_map/ppermute | solution.py:32
  369.9 22.9 %collective-permute-start.31 = (bf16[512,1792]{1,0:T(8,128)(2,1)S(1)}, bf16[512,1792]{1,0:T(8,128)(2,1)}, u32[]{:S(2)}, u32[]{:S(2)}) collective-permute-start(bf16[512,1792]{1,0:T(8,128)(2,1)S(1)} %bitcast.320), channel_id=1, source_target_pairs={{0,4},{4,0},{1,5},{5,1},{2,6},{6,2},{3,7},{7,3},{8,12},{12,8},{9,1... | collective-permute-start | bytes 5505032 | tf_op jit(solution)/shard_map/ppermute | solution.py:32
  370.4 22.4 %collective-permute-start.32 = (bf16[512,1792]{1,0:T(8,128)(2,1)}, bf16[512,1792]{1,0:T(8,128)(2,1)}, u32[]{:S(2)}, u32[]{:S(2)}) collective-permute-start(bf16[512,1792]{1,0:T(8,128)(2,1)} %collective-permute-done.7.refs_3_.refs_0_), channel_id=1, source_target_pairs={{0,4},{4,0},{1,5},{5,1},{2,6},{6,2},{3,7},{7,3},{8,12},{12,8},{9,1... | collective-permute-start | bytes 5505032 | tf_op jit(solution)/shard_map/ppermute | solution.py:32
  402.1 72.0 %collective-permute-start.40 = (bf16[896,1280]{1,0:T(8,128)(2,1)}, bf16[896,1280]{1,0:T(8,128)(2,1)}, u32[]{:S(2)}, u32[]{:S(2)}) collective-permute-start(bf16[896,1280]{1,0:T(8,128)(2,1)} %gradient_half.6), channel_id=1, source_target_pairs={{0,16},{16,0},{1,17},{17,1},{2,18},{18,2},{3,19},{19,3},{4,20},{20... | collective-permute-start | bytes 6881288 | tf_op jit(solution)/shard_map/ppermute | solution.py:32
  432.6 41.5 %collective-permute-start.41 = (bf16[512,1792]{1,0:T(8,128)(2,1)}, bf16[512,1792]{1,0:T(8,128)(2,1)}, u32[]{:S(2)}, u32[]{:S(2)}) collective-permute-start(bf16[512,1792]{1,0:T(8,128)(2,1)} %get-tuple-element.298), channel_id=1, source_target_pairs={{0,4},{4,0},{1,5},{5,1},{2,6},{6,2},{3,7},{7,3},{8,12},{12,8},{9,1... | collective-permute-start | bytes 5505032 | tf_op jit(solution)/shard_map/ppermute | solution.py:32
  432.8 41.3 %collective-permute-start.42 = (bf16[512,1792]{1,0:T(8,128)(2,1)}, bf16[512,1792]{1,0:T(8,128)(2,1)}, u32[]{:S(2)}, u32[]{:S(2)}) collective-permute-start(bf16[512,1792]{1,0:T(8,128)(2,1)} %get-tuple-element.300), channel_id=1, source_target_pairs={{0,4},{4,0},{1,5},{5,1},{2,6},{6,2},{3,7},{7,3},{8,12},{12,8},{9,1... | collective-permute-start | bytes 5505032 | tf_op jit(solution)/shard_map/ppermute | solution.py:32
  463.3 60.4 %collective-permute-start.45 = (bf16[512,1792]{1,0:T(8,128)(2,1)}, bf16[512,1792]{1,0:T(8,128)(2,1)}, u32[]{:S(2)}, u32[]{:S(2)}) collective-permute-start(bf16[512,1792]{1,0:T(8,128)(2,1)} %get-tuple-element.309), channel_id=1, source_target_pairs={{0,4},{4,0},{1,5},{5,1},{2,6},{6,2},{3,7},{7,3},{8,12},{12,8},{9,1... | collective-permute-start | bytes 5505032 | tf_op jit(solution)/shard_map/ppermute | solution.py:32
  463.5 60.2 %collective-permute-start.46 = (bf16[512,1792]{1,0:T(8,128)(2,1)}, bf16[512,1792]{1,0:T(8,128)(2,1)}, u32[]{:S(2)}, u32[]{:S(2)}) collective-permute-start(bf16[512,1792]{1,0:T(8,128)(2,1)} %get-tuple-element.311), channel_id=1, source_target_pairs={{0,4},{4,0},{1,5},{5,1},{2,6},{6,2},{3,7},{7,3},{8,12},{12,8},{9,1... | collective-permute-start | bytes 5505032 | tf_op jit(solution)/shard_map/ppermute | solution.py:32
  474.2 52.4 %collective-permute-start.43 = (bf16[896,1280]{1,0:T(8,128)(2,1)}, bf16[896,1280]{1,0:T(8,128)(2,1)}, u32[]{:S(2)}, u32[]{:S(2)}) collective-permute-start(bf16[896,1280]{1,0:T(8,128)(2,1)} %gradient_half.7), channel_id=1, source_target_pairs={{0,16},{16,0},{1,17},{17,1},{2,18},{18,2},{3,19},{19,3},{4,20},{20... | collective-permute-start | bytes 6881288 | tf_op jit(solution)/shard_map/ppermute | solution.py:32
  478.8 44.9 %collective-permute-start.44 = (bf16[512,1792]{1,0:T(8,128)(2,1)}, bf16[512,1792]{1,0:T(8,128)(2,1)}, u32[]{:S(2)}, u32[]{:S(2)}) collective-permute-start(bf16[512,1792]{1,0:T(8,128)(2,1)} %add_convert_fusion.5), channel_id=1, source_target_pairs={{0,8},{8,0},{1,9},{9,1},{2,10},{10,2},{3,11},{11,3},{4,12},{12,4},... | collective-permute-start | bytes 5505032 | tf_op jit(solution)/shard_map/ppermute | solution.py:32
  492.1 113.2 %reduce-scatter.6.cloned.1.call-start = ((), (), s32[]{:S(2)}) async-start(), calls=%async_computation.7 | async-start | bytes 2867200 | tf_op jit(solution)/shard_map/reduce_scatter | solution.py:468
  526.5 51.5 %collective-permute-start.47 = (bf16[896,1280]{1,0:T(8,128)(2,1)}, bf16[896,1280]{1,0:T(8,128)(2,1)}, u32[]{:S(2)}, u32[]{:S(2)}) collective-permute-start(bf16[896,1280]{1,0:T(8,128)(2,1)} %gradient_half.8), channel_id=1, source_target_pairs={{0,16},{16,0},{1,17},{17,1},{2,18},{18,2},{3,19},{19,3},{4,20},{20... | collective-permute-start | bytes 6881288 | tf_op jit(solution)/shard_map/ppermute | solution.py:32
  527.9 49.3 %collective-permute-start.48 = (bf16[512,1792]{1,0:T(8,128)(2,1)}, bf16[512,1792]{1,0:T(8,128)(2,1)}, u32[]{:S(2)}, u32[]{:S(2)}) collective-permute-start(bf16[512,1792]{1,0:T(8,128)(2,1)} %add_convert_fusion.4), channel_id=1, source_target_pairs={{0,8},{8,0},{1,9},{9,1},{2,10},{10,2},{3,11},{11,3},{4,12},{12,4},... | collective-permute-start | bytes 5505032 | tf_op jit(solution)/shard_map/ppermute | solution.py:32
  556.1 143.1 %reduce-scatter.8.cloned.1.call-start = ((), (), s32[]{:S(2)}) async-start(), calls=%async_computation.8 | async-start | bytes 2867200 | tf_op jit(solution)/shard_map/reduce_scatter | solution.py:468
  578.0 27.4 %collective-permute-start.49 = (bf16[4,224,1792]{2,1,0:T(8,128)(2,1)}, bf16[4,224,1792]{2,1,0:T(8,128)(2,1)}, u32[]{:S(2)}, u32[]{:S(2)}) collective-permute-start(bf16[4,224,1792]{2,1,0:T(8,128)(2,1)} %copy-done.21), channel_id=1, source_target_pairs={{0,4},{4,0},{1,5},{5,1},{2,6},{6,2},{3,7},{7,3},{8,12},{12,8},{9,1... | collective-permute-start | bytes 9633800 | tf_op jit(solution)/shard_map/ppermute | solution.py:32
  578.0 27.4 %collective-permute-start.50 = (bf16[4,224,1792]{2,1,0:T(8,128)(2,1)}, bf16[4,224,1792]{2,1,0:T(8,128)(2,1)}, u32[]{:S(2)}, u32[]{:S(2)}) collective-permute-start(bf16[4,224,1792]{2,1,0:T(8,128)(2,1)} %copy-done.22), channel_id=1, source_target_pairs={{0,4},{4,0},{1,5},{5,1},{2,6},{6,2},{3,7},{7,3},{8,12},{12,8},{9,1... | collective-permute-start | bytes 9633800 | tf_op jit(solution)/shard_map/ppermute | solution.py:32
  608.5 61.2 %collective-permute-start.51 = (bf16[2,224,1792]{2,1,0:T(8,128)(2,1)}, bf16[2,224,1792]{2,1,0:T(8,128)(2,1)}, u32[]{:S(2)}, u32[]{:S(2)}) collective-permute-start(bf16[2,224,1792]{2,1,0:T(8,128)(2,1)} %fusion.25), channel_id=1, source_target_pairs={{0,8},{8,0},{1,9},{9,1},{2,10},{10,2},{3,11},{11,3},{4,12},{12,4},... | collective-permute-start | bytes 4816904 | tf_op jit(solution)/shard_map/ppermute | solution.py:32
  612.8 56.9 %collective-permute-start.52 = (bf16[2,224,1792]{2,1,0:T(8,128)(2,1)}, bf16[2,224,1792]{2,1,0:T(8,128)(2,1)}, u32[]{:S(2)}, u32[]{:S(2)}) collective-permute-start(bf16[2,224,1792]{2,1,0:T(8,128)(2,1)} %fusion.26), channel_id=1, source_target_pairs={{0,16},{16,0},{1,17},{17,1},{2,18},{18,2},{3,19},{19,3},{4,20},{20... | collective-permute-start | bytes 4816904 | tf_op jit(solution)/shard_map/ppermute | solution.py:32
  622.4 47.2 %collective-permute-start.53 = (bf16[224,1280]{1,0:T(8,128)(2,1)}, bf16[224,1280]{1,0:T(8,128)(2,1)}, u32[]{:S(2)}, u32[]{:S(2)}) collective-permute-start(bf16[224,1280]{1,0:T(8,128)(2,1)} %reduce-scatter.4.cloned.1.call-done), channel_id=1, source_target_pairs={{0,0},{8,1},{4,2},{12,3},{1,4},{9,5},{5,6},{13,7},{2,8},{10,9},{6,... | collective-permute-start | bytes 1720328 | tf_op jit(solution)/shard_map/ppermute | solution.py:114
  669.7 16.9 %collective-permute-start.54 = (bf16[4,224,1792]{2,1,0:T(8,128)(2,1)}, bf16[4,224,1792]{2,1,0:T(8,128)(2,1)}, u32[]{:S(2)}, u32[]{:S(2)}) collective-permute-start(bf16[4,224,1792]{2,1,0:T(8,128)(2,1)} %get-tuple-element.360), channel_id=1, source_target_pairs={{0,4},{4,0},{1,5},{5,1},{2,6},{6,2},{3,7},{7,3},{8,12},{12,8},{9,1... | collective-permute-start | bytes 9633800 | tf_op jit(solution)/shard_map/ppermute | solution.py:32
  674.9 47.2 %collective-permute-start.57 = (bf16[224,1792]{1,0:T(8,128)(2,1)}, bf16[224,1792]{1,0:T(8,128)(2,1)}, u32[]{:S(2)}, u32[]{:S(2)}) collective-permute-start(bf16[224,1792]{1,0:T(8,128)(2,1)} %fusion.28), channel_id=1, source_target_pairs={{0,8},{8,0},{1,9},{9,1},{2,10},{10,2},{3,11},{11,3},{4,12},{12,4},... | collective-permute-start | bytes 2408456 | tf_op jit(solution)/shard_map/ppermute | solution.py:32
  677.8 44.4 %collective-permute-start.58 = (bf16[224,1792]{1,0:T(8,128)(2,1)}, bf16[224,1792]{1,0:T(8,128)(2,1)}, u32[]{:S(2)}, u32[]{:S(2)}) collective-permute-start(bf16[224,1792]{1,0:T(8,128)(2,1)} %fusion.27), channel_id=1, source_target_pairs={{0,16},{16,0},{1,17},{17,1},{2,18},{18,2},{3,19},{19,3},{4,20},{20... | collective-permute-start | bytes 2408456 | tf_op jit(solution)/shard_map/ppermute | solution.py:32
  681.8 35.9 %collective-permute-start.59 = (bf16[224,1280]{1,0:T(8,128)(2,1)}, bf16[224,1280]{1,0:T(8,128)(2,1)}, u32[]{:S(2)}, u32[]{:S(2)}) collective-permute-start(bf16[224,1280]{1,0:T(8,128)(2,1)} %reduce-scatter.6.cloned.1.call-done), channel_id=1, source_target_pairs={{0,0},{8,1},{4,2},{12,3},{1,4},{9,5},{5,6},{13,7},{2,8},{10,9},{6,... | collective-permute-start | bytes 1720328 | tf_op jit(solution)/shard_map/ppermute | solution.py:114
  691.2 36.4 %collective-permute-start.55 = (bf16[2,224,1280]{2,1,0:T(8,128)(2,1)}, bf16[2,224,1280]{2,1,0:T(8,128)(2,1)}, u32[]{:S(2)}, u32[]{:S(2)}) collective-permute-start(bf16[2,224,1280]{2,1,0:T(8,128)(2,1)} %fusion.31), channel_id=1, source_target_pairs={{0,16},{16,0},{1,17},{17,1},{2,18},{18,2},{3,19},{19,3},{4,20},{20... | collective-permute-start | bytes 3440648 | tf_op jit(solution)/shard_map/ppermute | solution.py:32
  699.2 24.5 %collective-permute-start.60 = (bf16[224,1280]{1,0:T(8,128)(2,1)}, bf16[224,1280]{1,0:T(8,128)(2,1)S(1)}, u32[]{:S(2)}, u32[]{:S(2)}) collective-permute-start(bf16[224,1280]{1,0:T(8,128)(2,1)} %reduce-scatter.8.cloned.1.call-done), channel_id=1, source_target_pairs={{0,0},{8,1},{4,2},{12,3},{1,4},{9,5},{5,6},{13,7},{2,8},{10,9},{6,... | collective-permute-start | bytes 1720328 | tf_op jit(solution)/shard_map/ppermute | solution.py:114
  735.3 47.7 %collective-permute-start.62 = (bf16[224,1280]{1,0:T(8,128)(2,1)S(1)}, bf16[224,1280]{1,0:T(8,128)(2,1)}, u32[]{:S(2)}, u32[]{:S(2)}) collective-permute-start(bf16[224,1280]{1,0:T(8,128)(2,1)S(1)} %fusion.44), channel_id=1, source_target_pairs={{0,8},{8,0},{1,9},{9,1},{2,10},{10,2},{3,11},{11,3},{4,12},{12,4},... | collective-permute-start | bytes 1720328 | tf_op jit(solution)/shard_map/ppermute | solution.py:32
  739.8 13.6 %collective-permute-start.67 = (f32[2,5,4,56]{3,2,1,0:T(4,128)S(1)}, f32[2,5,4,56]{3,2,1,0:T(4,128)S(1)}, u32[]{:S(2)}, u32[]{:S(2)}) collective-permute-start(f32[2,5,4,56]{3,2,1,0:T(4,128)S(1)} %bitcast_add_fusion.5), channel_id=1, source_target_pairs={{0,16},{16,0},{1,17},{17,1},{2,18},{18,2},{3,19},{19,3},{4,20},{20... | collective-permute-start | bytes 26888 | tf_op jit(solution)/shard_map/ppermute | solution.py:32
  749.3 15.6 %collective-permute-start.64 = (bf16[448,448]{1,0:T(8,128)(2,1)S(1)}, bf16[448,448]{1,0:T(8,128)(2,1)S(1)}, u32[]{:S(2)}, u32[]{:S(2)}) collective-permute-start(bf16[448,448]{1,0:T(8,128)(2,1)S(1)} %get-tuple-element.482), channel_id=1, source_target_pairs={{0,3},{1,0},{2,1},{3,2},{4,7},{5,4},{6,5},{7,6},{8,11},{9,8},{10,9... | collective-permute-start | bytes 1204232 | tf_op jit(solution)/shard_map/ppermute | solution.py:32
  749.6 33.4 %collective-permute-start.65 = (bf16[448,448]{1,0:T(8,128)(2,1)S(1)}, bf16[448,448]{1,0:T(8,128)(2,1)S(1)}, u32[]{:S(2)}, u32[]{:S(2)}) collective-permute-start(bf16[448,448]{1,0:T(8,128)(2,1)S(1)} %get-tuple-element.481), channel_id=1, source_target_pairs={{0,2},{1,3},{2,0},{3,1},{4,6},{5,7},{6,4},{7,5},{8,10},{9,11},{10,... | collective-permute-start | bytes 1204232 | tf_op jit(solution)/shard_map/ppermute | solution.py:32
  749.7 33.3 %collective-permute-start.66 = (bf16[448,448]{1,0:T(8,128)(2,1)S(1)}, bf16[448,448]{1,0:T(8,128)(2,1)S(1)}, u32[]{:S(2)}, u32[]{:S(2)}) collective-permute-start(bf16[448,448]{1,0:T(8,128)(2,1)S(1)} %get-tuple-element.480), channel_id=1, source_target_pairs={{0,1},{1,2},{2,3},{3,0},{4,5},{5,6},{6,7},{7,4},{8,9},{9,10},{10,1... | collective-permute-start | bytes 1204232 | tf_op jit(solution)/shard_map/ppermute | solution.py:32
  788.0 16.5 %collective-permute-start.71 = (bf16[232,448]{1,0:T(8,128)(2,1)S(1)}, bf16[232,448]{1,0:T(8,128)(2,1)S(1)}, u32[]{:S(2)}, u32[]{:S(2)}) collective-permute-start(bf16[232,448]{1,0:T(8,128)(2,1)S(1)} %get-tuple-element.494), channel_id=1, source_target_pairs={{0,1},{1,2},{2,3},{3,0},{4,5},{5,6},{6,7},{7,4},{8,9},{9,10},{10,1... | collective-permute-start | bytes 623624 | tf_op jit(solution)/shard_map/ppermute | solution.py:32
  794.1 24.7 %collective-permute-start.70 = (bf16[232,448]{1,0:T(8,128)(2,1)S(1)}, bf16[232,448]{1,0:T(8,128)(2,1)S(1)}, u32[]{:S(2)}, u32[]{:S(2)}) collective-permute-start(bf16[232,448]{1,0:T(8,128)(2,1)S(1)} %get-tuple-element.495), channel_id=1, source_target_pairs={{0,2},{1,3},{2,0},{3,1},{4,6},{5,7},{6,4},{7,5},{8,10},{9,11},{10,... | collective-permute-start | bytes 623624 | tf_op jit(solution)/shard_map/ppermute | solution.py:32
  798.8 20.1 %collective-permute-start.69 = (bf16[232,448]{1,0:T(8,128)(2,1)S(1)}, bf16[232,448]{1,0:T(8,128)(2,1)S(1)}, u32[]{:S(2)}, u32[]{:S(2)}) collective-permute-start(bf16[232,448]{1,0:T(8,128)(2,1)S(1)} %get-tuple-element.493), channel_id=1, source_target_pairs={{0,3},{1,0},{2,1},{3,2},{4,7},{5,4},{6,5},{7,6},{8,11},{9,8},{10,9... | collective-permute-start | bytes 623624 | tf_op jit(solution)/shard_map/ppermute | solution.py:32
  (118 other events, 1050.1 us)
Sparse Core Ops, SparseCore 0:
  50.7 46.0 all-gather.5
  99.5 46.0 all-gather.7
  148.0 56.2 all-gather.9
  492.2 46.3 reduce-scatter.3
  556.2 48.0 reduce-scatter.5
  628.4 55.4 reduce-scatter.7

commit v2 on v1

--- a/solution.py
+++ b/solution.py
@@ -394,9 +394,10 @@
         ],
         axis=1,
     )
-    y_g, plane_u, z_d, w_out = phase(y_g, plane_u, z_d, w_out)
-    y_u = pieces_of(plane_rows(plane_u), "a")
-    plane_d = in_plane(in_order(z_d, "z", 0))
+    rows_u, half_d = plane_rows(plane_u), in_order(z_d, "z", 0)
+    y_g, rows_u, half_d, w_out = phase(y_g, rows_u, half_d, w_out)
+    y_u = pieces_of(rows_u, "a")
+    plane_d = in_plane(half_d)
     ffn_g = in_order(y_g, "a", 0).reshape(-1, units)
 
     tail_in = jnp.concatenate(

time: 839 us -> 842 us (level)
    unnamed x221 -> x219, local copies, waits for them, and re-layouts: 25 us -> 26 us
  transfers between devices with their start and end apart: 78 -> 78, of which waited for: 28 -> 30; matrix products, arithmetic and copies ran while one was open for 22% -> 22% of each run, Pallas kernels for 18% -> 18%
where the time goes in v2:
time: 842 us; the launch traced here: 830 us
  waiting for transfers between devices  307 us (36%)
  Pallas kernels  159 us (19%)
  other arithmetic  119 us (14%)
  starting transfers between devices  79.7 us (9%)
  local copies, waits for them, and re-layouts  64.8 us (8%)
  matrix products  44.2 us (5%)
  between operations  29.7 us (4%)
  blocking collectives  26.3 us (3%)
    ppermute x62, waiting for transfers between devices, shift_by(): lax.ppermute(value, axis, [(i, (i + amount) % size) for i in range(size)])  258 us
    pallas_call x4, Pallas kernels, feed_forward(): pl.pallas_call(functools.partial(second_kernel if second else first_kerne...  91.5 us
    ppermute x62, starting transfers between devices, shift_by(): lax.ppermute(value, axis, [(i, (i + amount) % size) for i in range(size)])  65 us
    pallas_call x6, Pallas kernels, gradient_half(): pl.pallas_call(functools.partial(gradient_kernel, count=count, extra=len(...  50.6 us
    ppermute x3, waiting for transfers between devices, home(): return lax.ppermute(block, ('b', 'c', 'z'), moves)  37.7 us
    dot_general x4, matrix products, dot_nn(): lax.dot_general(left, right, (((1,), (0,)), ((), ())), preferred_element_...  28.2 us
    unnamed x219, local copies, waits for them, and re-layouts  26 us
    another operation x15, other arithmetic, in_order(): jnp.stack([jnp.where(first, pieces[0], pieces[1]), jnp.where(first, piece...  20.7 us
  transfers between devices with their start and end apart: 78, of which 30 were waited for; matrix products, arithmetic and copies ran while one was open for 22% of the time, Pallas kernels for 18%

profile of v2, /device:TPU:30, one launch (start us, length us, event | category | flops | bytes accessed | tf_op | source)
XLA Modules:
  0.0 830.2 jit_solution(16688406044444382474)
XLA Ops:
  43.9 5.5 collective-permute-done.7.refs_3_.refs_0_
  57.2 25.3 %collective-permute-done.8 = bf16[224,448]{1,0:T(8,128)(2,1)S(1)} collective-permute-done((bf16[224,448]{1,0:T(8,128)(2,1)S(1)}, bf16[224,448]{1,0:T(8,128)(2,1)S(1)}, u32[]{:S(2)}, u32[]{:S(2)}) %collective-permute-start.8) | collective-permute-done | bytes 200736 | tf_op jit(solution)/shard_map/ppermute | solution.py:32
  82.5 13.9 %collective-permute-done.9 = bf16[224,448]{1,0:T(8,128)(2,1)S(1)} collective-permute-done((bf16[224,448]{1,0:T(8,128)(2,1)S(1)}, bf16[224,448]{1,0:T(8,128)(2,1)S(1)}, u32[]{:S(2)}, u32[]{:S(2)}) %collective-permute-start.9) | collective-permute-done | bytes 200736 | tf_op jit(solution)/shard_map/ppermute | solution.py:32
  104.4 13.5 %collective-permute-done.13 = bf16[224,448]{1,0:T(8,128)(2,1)S(1)} collective-permute-done((bf16[224,448]{1,0:T(8,128)(2,1)S(1)}, bf16[224,448]{1,0:T(8,128)(2,1)S(1)}, u32[]{:S(2)}, u32[]{:S(2)}) %collective-permute-start.13) | collective-permute-done | bytes 200736 | tf_op jit(solution)/shard_map/ppermute | solution.py:32
  117.9 15.6 %collective-permute-done.14 = bf16[224,448]{1,0:T(8,128)(2,1)S(1)} collective-permute-done((bf16[224,448]{1,0:T(8,128)(2,1)S(1)}, bf16[224,448]{1,0:T(8,128)(2,1)S(1)}, u32[]{:S(2)}, u32[]{:S(2)}) %collective-permute-start.14) | collective-permute-done | bytes 200736 | tf_op jit(solution)/shard_map/ppermute | solution.py:32
  148.7 3.8 collective-permute-done.23
  152.7 8.2 fusion.2
  161.9 30.8 %collective-permute-done.21 = bf16[224,1280]{1,0:T(8,128)(2,1)} collective-permute-done((bf16[224,1280]{1,0:T(8,128)(2,1)}, bf16[224,1280]{1,0:T(8,128)(2,1)}, u32[]{:S(2)}, u32[]{:S(2)}) %collective-permute-start.21) | collective-permute-done | bytes 573472 | tf_op jit(solution)/shard_map/ppermute | solution.py:32
  192.7 3.1 collective-permute-start.29
  195.8 3.8 collective-permute-start.28
  203.9 3.8 fusion.59
  213.4 9.3 %multiply_convert_fusion.2 = (bf16[4,128,1792]{2,1,0:T(8,128)(2,1)S(1)}, f32[4,128,1792]{2,1,0:T(8,128)}, f32[4,128,1792]{2,1,0:T(8,128)}) fusion(f32[4,128,1792]{2,1,0:T(8,128)S(1)} %copy-done.46, f32[4,2,1792]{2,1,0:T(2,128)S(1)} %reshape.386, f32[4,128]{1,0:T(4,128)S(1)} %copy-done.84, f32[1792]{0:T(1024)S(1)} %copy-done.78, ...), kind=kOutput, calls=%fused_computation.57 | convolution fusion | flops 3302096896 | bytes 21194752 | tf_op jit(solution)/shard_map/dot_general | solution.py:19
  222.7 11.5 %collective-permute-done.29 = bf16[224,1280]{1,0:T(8,128)(2,1)} collective-permute-done((bf16[224,1280]{1,0:T(8,128)(2,1)}, bf16[224,1280]{1,0:T(8,128)(2,1)}, u32[]{:S(2)}, u32[]{:S(2)}) %collective-permute-start.29) | collective-permute-done | bytes 573472 | tf_op jit(solution)/shard_map/ppermute | solution.py:32
  241.5 20.4 %collective-permute-done.25 = bf16[4,224,1280]{2,1,0:T(8,128)(2,1)} collective-permute-done((bf16[4,224,1280]{2,1,0:T(8,128)(2,1)S(1)}, bf16[4,224,1280]{2,1,0:T(8,128)(2,1)}, u32[]{:S(2)}, u32[]{:S(2)}) %collective-permute-start.25) | collective-permute-done | bytes 2293792 | tf_op jit(solution)/shard_map/ppermute | solution.py:32
  264.0 6.6 multiply_reduce_fusion.5
  270.7 3.3 select_bitcast_fusion.5
  278.2 23.9 %collective-permute-done.34 = bf16[2,224,1280]{2,1,0:T(8,128)(2,1)S(1)} collective-permute-done((bf16[2,224,1280]{2,1,0:T(8,128)(2,1)S(1)}, bf16[2,224,1280]{2,1,0:T(8,128)(2,1)S(1)}, u32[]{:S(2)}, u32[]{:S(2)}) %collective-permute-start.34) | collective-permute-done | bytes 1146912 | tf_op jit(solution)/shard_map/ppermute | solution.py:32
  302.1 13.8 %collective-permute-done.35 = bf16[4,224,1280]{2,1,0:T(8,128)(2,1)S(1)} collective-permute-done((bf16[4,224,1280]{2,1,0:T(8,128)(2,1)}, bf16[4,224,1280]{2,1,0:T(8,128)(2,1)S(1)}, u32[]{:S(2)}, u32[]{:S(2)}) %collective-permute-start.35) | collective-permute-done | bytes 2293792 | tf_op jit(solution)/shard_map/ppermute | solution.py:32
  323.1 15.6 %first_half.2 = (bf16[2048,1280]{1,0:T(8,128)(2,1)}, bf16[2048,1280]{1,0:T(8,128)(2,1)}, bf16[2048,1280]{1,0:T(8,128)(2,1)}) custom-call(bf16[512,1792]{1,0:T(8,128)(2,1)} %copy-done, bf16[512,1792]{1,0:T(8,128)(2,1)} %copy-done.2, bf16[1792,1280]{1,0:T(8,128)(2,1)} %bitcast.347, bf16[1792,1280]{1,0:T(8,128)(2,1)} %bitcast.351), custom_call_target="tpu_custom_call" | custom-call | flops 18790481920 | bytes 25952256 | tf_op jit(solution)/shard_map/first_half/pallas_call | solution.py:192
  338.7 18.9 %collective-permute-done.37.refs_0_.refs_3_ = bf16[512,1792]{1,0:T(8,128)(2,1)} collective-permute-done((bf16[512,1792]{1,0:T(8,128)(2,1)S(1)}, bf16[512,1792]{1,0:T(8,128)(2,1)}, u32[]{:S(2)}, u32[]{:S(2)}) %collective-permute-start.37) | collective-permute-done | bytes 1835040 | tf_op jit(solution)/shard_map/ppermute | solution.py:32
  357.5 11.7 %collective-permute-done.36 = bf16[4,224,1280]{2,1,0:T(8,128)(2,1)} collective-permute-done((bf16[4,224,1280]{2,1,0:T(8,128)(2,1)S(1)}, bf16[4,224,1280]{2,1,0:T(8,128)(2,1)}, u32[]{:S(2)}, u32[]{:S(2)}) %collective-permute-start.36) | collective-permute-done | bytes 2293792 | tf_op jit(solution)/shard_map/ppermute | solution.py:32
  369.3 3.5 fusion.15.left
  379.6 16.0 %first_half.3 = (bf16[2048,1280]{1,0:T(8,128)(2,1)}, bf16[2048,1280]{1,0:T(8,128)(2,1)}, bf16[2048,1280]{1,0:T(8,128)(2,1)}) custom-call(bf16[512,1792]{1,0:T(8,128)(2,1)} %collective-permute-done.37.refs_0_.refs_3_, bf16[512,1792]{1,0:T(8,128)(2,1)} %copy-done.5, ...), custom_call_target="tpu_custom_call", output_to_operand_aliasing={{0}: (4, {}), {1}: (5, {}), {2}: (6, {})} | custom-call | flops 18790481920 | bytes 25952256 | tf_op jit(solution)/shard_map/first_half/pallas_call | solution.py:192
  395.7 9.3 %gradient_half.6 = bf16[896,1280]{1,0:T(8,128)(2,1)} custom-call(s32[1]{0:T(128)} %bitcast.54.refs_0_, bf16[512,1792]{1,0:T(8,128)(2,1)S(1)} %bitcast.325, bf16[512,1792]{1,0:T(8,128)(2,1)} %collective-permute-done.31.refs_2_.refs_1_, bf16[512,1792]{1,0:T(8,128)(2,1)} %collective-permute-done.7.refs_3_.refs_0_, ...), custom_call_target="tpu_custom_call" | custom-call | flops 4697620480 | bytes 11206656 | tf_op jit(solution)/shard_map/gradient_half/pallas_call | solution.py:232
  405.4 29.8 %second_half.2 = (bf16[2048,2560]{1,0:T(8,128)(2,1)}, bf16[512,1792]{1,0:T(8,128)(2,1)}, bf16[512,1792]{1,0:T(8,128)(2,1)}, bf16[512,1792]{1,0:T(8,128)(2,1)}, bf16[512,1792]{1,0:T(8,128)(2,1)}) custom-call(bf16[512,1792]{1,0:T(8,128)(2,1)} %collective-permute-done.7.refs_3_.refs_0_, bf16[512,1792]{1,0:T(8,128)(2,1)} %collective-permute-done.32.refs_4_.refs_1_, ...), custom_call_target="tpu_custom_call" | custom-call | flops 37580963840 | bytes 30539776 | tf_op jit(solution)/shard_map/second_half/pallas_call | solution.py:192
  435.8 30.2 %second_half.3 = (bf16[2048,2560]{1,0:T(8,128)(2,1)}, bf16[512,1792]{1,0:T(8,128)(2,1)}, bf16[512,1792]{1,0:T(8,128)(2,1)}, bf16[512,1792]{1,0:T(8,128)(2,1)}, bf16[512,1792]{1,0:T(8,128)(2,1)}) custom-call(bf16[512,1792]{1,0:T(8,128)(2,1)} %bitcast.323, bf16[512,1792]{1,0:T(8,128)(2,1)} %collective-permute-done.31.refs_2_.refs_1_, ...), custom_call_target="tpu_custom_call", output_to_operand_aliasing={{0}: (8, {})} | custom-call | flops 37580963840 | bytes 30539776 | tf_op jit(solution)/shard_map/second_half/pallas_call | solution.py:192
  468.0 8.8 %gradient_half.7 = bf16[896,1280]{1,0:T(8,128)(2,1)} custom-call(s32[1]{0:T(128)} %bitcast.54.refs_0_, bf16[512,1792]{1,0:T(8,128)(2,1)S(1)} %copy-done.1, bf16[512,1792]{1,0:T(8,128)(2,1)S(1)} %copy-done.3, bf16[512,1792]{1,0:T(8,128)(2,1)} %collective-permute-done.37.refs_0_.refs_3_, bf16[512,1792]{1,0:T(8,128)(2,1)S(1)} %copy-done.6, ...), custom_call_target="tpu_custom_call" | custom-call | flops 4697620480 | bytes 11206656 | tf_op jit(solution)/shard_map/gradient_half/pallas_call | solution.py:232
  478.3 3.1 add_convert_fusion.5
  482.9 8.1 gradient_half.11
  491.1 3.6 add_convert_fusion.2
  497.8 8.9 %gradient_half.8 = bf16[896,1280]{1,0:T(8,128)(2,1)} custom-call(s32[1]{0:T(128)} %bitcast.54.refs_0_, bf16[512,1792]{1,0:T(8,128)(2,1)S(1)} %copy-done.1, bf16[512,1792]{1,0:T(8,128)(2,1)S(1)} %copy-done.4, bf16[512,1792]{1,0:T(8,128)(2,1)} %collective-permute-done.37.refs_0_.refs_3_, bf16[512,1792]{1,0:T(8,128)(2,1)S(1)} %copy-done.7, ...), custom_call_target="tpu_custom_call" | custom-call | flops 4697620480 | bytes 11206656 | tf_op jit(solution)/shard_map/gradient_half/pallas_call | solution.py:232
  506.8 7.7 gradient_half.9
  514.4 7.8 gradient_half.10
  522.3 4.1 add_convert_fusion.4
  532.1 3.6 multiply_reduce_fusion.3
  535.7 3.7 add_convert_fusion.1
  539.4 5.8 fusion.94
  545.3 7.0 fusion.101
  552.4 3.8 multiply_reduce_fusion
  561.9 5.4 split_gradient.3
  569.1 5.5 split_gradient.4
  574.6 5.4 fusion.102
  581.6 14.9 %all-gather = bf16[32,1792]{1,0:T(8,128)(2,1)S(1)} all-gather(bf16[8,1792]{1,0:T(8,128)(2,1)S(1)} %concatenate.111), channel_id=2, replica_groups=mesh['a'=2,'b'=2,'c'=2,'z'=4] {'z'}, dimensions={0}, use_global_device_ids=true | all-gather | bytes 143360 | tf_op jit(solution)/shard_map/all_gather | solution.py:343
  596.4 11.4 %all-gather.1 = bf16[32,8,1792]{2,1,0:T(8,128)(2,1)} all-gather(bf16[4,8,1792]{2,1,0:T(8,128)(2,1)S(1)} %bitcast.360), channel_id=3, replica_groups=mesh['a'=2,'b'=2,'c'=2,'z'=4] {'a','b','c'}, dimensions={0}, use_global_device_ids=true | all-gather | bytes 1032192 | tf_op jit(solution)/shard_map/all_gather | solution.py:343
  607.9 3.1 fusion.25
  617.8 4.7 fusion.7
  627.2 3.7 add_convert_fusion
  631.6 5.2 fusion.10
  638.6 4.0 fusion.20
  642.6 6.2 split_gradient.5
  651.7 20.6 %collective-permute-done.53 = bf16[224,1280]{1,0:T(8,128)(2,1)} collective-permute-done((bf16[224,1280]{1,0:T(8,128)(2,1)}, bf16[224,1280]{1,0:T(8,128)(2,1)}, u32[]{:S(2)}, u32[]{:S(2)}) %collective-permute-start.53) | collective-permute-done | bytes 573472 | tf_op jit(solution)/shard_map/ppermute | solution.py:114
  680.3 3.8 collective-permute-start.58
  693.5 4.2 collective-permute-start.61
  704.5 15.5 %collective-permute-done.59 = bf16[224,1280]{1,0:T(8,128)(2,1)} collective-permute-done((bf16[224,1280]{1,0:T(8,128)(2,1)}, bf16[224,1280]{1,0:T(8,128)(2,1)}, u32[]{:S(2)}, u32[]{:S(2)}) %collective-permute-start.59) | collective-permute-done | bytes 573472 | tf_op jit(solution)/shard_map/ppermute | solution.py:114
  726.0 4.1 collective-permute-done.56
  742.4 3.8 collective-permute-start.67
  751.9 3.7 collective-permute-start.66
  755.9 3.5 collective-permute-done.68
  759.5 5.9 collective-permute-done.63
  767.2 18.0 %collective-permute-done.65 = bf16[448,448]{1,0:T(8,128)(2,1)S(1)} collective-permute-done((bf16[448,448]{1,0:T(8,128)(2,1)S(1)}, bf16[448,448]{1,0:T(8,128)(2,1)S(1)}, u32[]{:S(2)}, u32[]{:S(2)}) %collective-permute-start.65) | collective-permute-done | bytes 401440 | tf_op jit(solution)/shard_map/ppermute | solution.py:32
  790.3 4.5 collective-permute-start.71
  794.8 6.3 collective-permute-start.70
  801.1 4.4 add_convert_fusion.3
  806.8 14.3 %collective-permute-done.70 = bf16[232,448]{1,0:T(8,128)(2,1)S(1)} collective-permute-done((bf16[232,448]{1,0:T(8,128)(2,1)S(1)}, bf16[232,448]{1,0:T(8,128)(2,1)S(1)}, u32[]{:S(2)}, u32[]{:S(2)}) %collective-permute-start.70) | collective-permute-done | bytes 207904 | tf_op jit(solution)/shard_map/ppermute | solution.py:32
  (512 shorter events, 191.4 us)
Async XLA Ops:
  7.2 127.0 %all-gather.6.cloned.1.call-start = ((), (), s32[]{:S(2)}) async-start(), calls=%async_computation.3 | async-start | bytes 7225344 | tf_op jit(solution)/shard_map/all_gather | solution.py:340
  7.2 42.1 %collective-permute-start.7 = (bf16[512,1792]{1,0:T(8,128)(2,1)}, bf16[512,1792]{1,0:T(8,128)(2,1)}, u32[]{:S(2)}, u32[]{:S(2)}) collective-permute-start(bf16[512,1792]{1,0:T(8,128)(2,1)} %bitcast.322), channel_id=1, source_target_pairs={{0,8},{8,0},{1,9},{9,1},{2,10},{10,2},{3,11},{11,3},{4,12},{12,4},... | collective-permute-start | bytes 5505032 | tf_op jit(solution)/shard_map/ppermute | solution.py:32
  7.8 36.0 %collective-permute-start = (bf16[224,448]{1,0:T(8,128)(2,1)}, bf16[224,448]{1,0:T(8,128)(2,1)S(1)}, u32[]{:S(2)}, u32[]{:S(2)}) collective-permute-start(bf16[224,448]{1,0:T(8,128)(2,1)} %param.18), channel_id=1, source_target_pairs={{0,1},{1,2},{2,3},{3,0},{4,5},{5,6},{6,7},{7,4},{8,9},{9,10},{10,1... | collective-permute-start | bytes 602120 | tf_op jit(solution)/shard_map/ppermute | solution.py:32
  8.1 35.8 %collective-permute-start.1 = (bf16[224,448]{1,0:T(8,128)(2,1)}, bf16[224,448]{1,0:T(8,128)(2,1)S(1)}, u32[]{:S(2)}, u32[]{:S(2)}) collective-permute-start(bf16[224,448]{1,0:T(8,128)(2,1)} %param.18), channel_id=1, source_target_pairs={{0,2},{1,3},{2,0},{3,1},{4,6},{5,7},{6,4},{7,5},{8,10},{9,11},{10,... | collective-permute-start | bytes 602120 | tf_op jit(solution)/shard_map/ppermute | solution.py:32
  9.7 34.2 %collective-permute-start.2 = (bf16[224,448]{1,0:T(8,128)(2,1)}, bf16[224,448]{1,0:T(8,128)(2,1)S(1)}, u32[]{:S(2)}, u32[]{:S(2)}) collective-permute-start(bf16[224,448]{1,0:T(8,128)(2,1)} %param.18), channel_id=1, source_target_pairs={{0,3},{1,0},{2,1},{3,2},{4,7},{5,4},{6,5},{7,6},{8,11},{9,8},{10,9... | collective-permute-start | bytes 602120 | tf_op jit(solution)/shard_map/ppermute | solution.py:32
  10.2 19.4 %collective-permute-start.5 = (f32[1,3,448]{2,1,0:T(4,128)}, f32[1,3,448]{2,1,0:T(4,128)S(1)}, u32[]{:S(2)}, u32[]{:S(2)}) collective-permute-start(f32[1,3,448]{2,1,0:T(4,128)} %bitcast.375), channel_id=1, source_target_pairs={{0,1},{1,0},{2,3},{3,2},{4,5},{5,4},{6,7},{7,6},{8,9},{9,8},{10,11... | collective-permute-start | bytes 16136 | tf_op jit(solution)/shard_map/ppermute | solution.py:119
  50.6 142.1 %all-gather.8.cloned.1.call-start = ((), (), s32[]{:S(2)}) async-start(), calls=%async_computation.4 | async-start | bytes 7225344 | tf_op jit(solution)/shard_map/all_gather | solution.py:340
  50.7 45.7 %collective-permute-start.11 = (bf16[224,1280]{1,0:T(8,128)(2,1)S(1)}, bf16[224,1280]{1,0:T(8,128)(2,1)S(1)}, u32[]{:S(2)}, u32[]{:S(2)}) collective-permute-start(bf16[224,1280]{1,0:T(8,128)(2,1)S(1)} %pad.14), channel_id=1, source_target_pairs={{0,1},{1,2},{2,3},{3,0},{4,5},{5,6},{6,7},{7,4},{8,9},{9,10},{10,1... | collective-permute-start | bytes 1720328 | tf_op jit(solution)/shard_map/ppermute | solution.py:32
  50.9 46.2 %collective-permute-start.12 = (bf16[224,1280]{1,0:T(8,128)(2,1)S(1)}, bf16[224,1280]{1,0:T(8,128)(2,1)S(1)}, u32[]{:S(2)}, u32[]{:S(2)}) collective-permute-start(bf16[224,1280]{1,0:T(8,128)(2,1)S(1)} %pad.14), channel_id=1, source_target_pairs={{0,3},{1,0},{2,1},{3,2},{4,7},{5,4},{6,5},{7,6},{8,11},{9,8},{10,9... | collective-permute-start | bytes 1720328 | tf_op jit(solution)/shard_map/ppermute | solution.py:32
  52.8 29.7 %collective-permute-start.8 = (bf16[224,448]{1,0:T(8,128)(2,1)S(1)}, bf16[224,448]{1,0:T(8,128)(2,1)S(1)}, u32[]{:S(2)}, u32[]{:S(2)}) collective-permute-start(bf16[224,448]{1,0:T(8,128)(2,1)S(1)} %copy-done.69), channel_id=1, source_target_pairs={{0,1},{1,2},{2,3},{3,0},{4,5},{5,6},{6,7},{7,4},{8,9},{9,10},{10,1... | collective-permute-start | bytes 602120 | tf_op jit(solution)/shard_map/ppermute | solution.py:32
  54.8 41.6 %collective-permute-start.9 = (bf16[224,448]{1,0:T(8,128)(2,1)S(1)}, bf16[224,448]{1,0:T(8,128)(2,1)S(1)}, u32[]{:S(2)}, u32[]{:S(2)}) collective-permute-start(bf16[224,448]{1,0:T(8,128)(2,1)S(1)} %copy-done.69), channel_id=1, source_target_pairs={{0,2},{1,3},{2,0},{3,1},{4,6},{5,7},{6,4},{7,5},{8,10},{9,11},{10,... | collective-permute-start | bytes 602120 | tf_op jit(solution)/shard_map/ppermute | solution.py:32
  54.8 41.6 %collective-permute-start.10 = (bf16[224,448]{1,0:T(8,128)(2,1)S(1)}, bf16[224,448]{1,0:T(8,128)(2,1)S(1)}, u32[]{:S(2)}, u32[]{:S(2)}) collective-permute-start(bf16[224,448]{1,0:T(8,128)(2,1)S(1)} %copy-done.69), channel_id=1, source_target_pairs={{0,3},{1,0},{2,1},{3,2},{4,7},{5,4},{6,5},{7,6},{8,11},{9,8},{10,9... | collective-permute-start | bytes 602120 | tf_op jit(solution)/shard_map/ppermute | solution.py:32
  99.4 162.5 %all-gather.10.cloned.1.call-start = ((), (), s32[]{:S(2)}) async-start(), calls=%async_computation.5 | async-start | bytes 7225344 | tf_op jit(solution)/shard_map/all_gather | solution.py:340
  99.4 34.8 %collective-permute-start.16 = (bf16[224,1280]{1,0:T(8,128)(2,1)S(1)}, bf16[224,1280]{1,0:T(8,128)(2,1)S(1)}, u32[]{:S(2)}, u32[]{:S(2)}) collective-permute-start(bf16[224,1280]{1,0:T(8,128)(2,1)S(1)} %collective-permute-done.11), channel_id=1, source_target_pairs={{0,1},{1,2},{2,3},{3,0},{4,5},{5,6},{6,7},{7,4},{8,9},{9,10},{10,1... | collective-permute-start | bytes 1720328 | tf_op jit(solution)/shard_map/ppermute | solution.py:32
  100.2 17.7 %collective-permute-start.13 = (bf16[224,448]{1,0:T(8,128)(2,1)S(1)}, bf16[224,448]{1,0:T(8,128)(2,1)S(1)}, u32[]{:S(2)}, u32[]{:S(2)}) collective-permute-start(bf16[224,448]{1,0:T(8,128)(2,1)S(1)} %copy-done.70), channel_id=1, source_target_pairs={{0,1},{1,2},{2,3},{3,0},{4,5},{5,6},{6,7},{7,4},{8,9},{9,10},{10,1... | collective-permute-start | bytes 602120 | tf_op jit(solution)/shard_map/ppermute | solution.py:32
  102.7 30.8 %collective-permute-start.14 = (bf16[224,448]{1,0:T(8,128)(2,1)S(1)}, bf16[224,448]{1,0:T(8,128)(2,1)S(1)}, u32[]{:S(2)}, u32[]{:S(2)}) collective-permute-start(bf16[224,448]{1,0:T(8,128)(2,1)S(1)} %copy-done.70), channel_id=1, source_target_pairs={{0,2},{1,3},{2,0},{3,1},{4,6},{5,7},{6,4},{7,5},{8,10},{9,11},{10,... | collective-permute-start | bytes 602120 | tf_op jit(solution)/shard_map/ppermute | solution.py:32
  103.5 30.0 %collective-permute-start.15 = (bf16[224,448]{1,0:T(8,128)(2,1)S(1)}, bf16[224,448]{1,0:T(8,128)(2,1)S(1)}, u32[]{:S(2)}, u32[]{:S(2)}) collective-permute-start(bf16[224,448]{1,0:T(8,128)(2,1)S(1)} %copy-done.70), channel_id=1, source_target_pairs={{0,3},{1,0},{2,1},{3,2},{4,7},{5,4},{6,5},{7,6},{8,11},{9,8},{10,9... | collective-permute-start | bytes 602120 | tf_op jit(solution)/shard_map/ppermute | solution.py:32
  136.3 444.3 %reduce-scatter.4.cloned.1.call-start = ((), (), s32[]{:S(2)}) async-start(), calls=%async_computation.6 | async-start | bytes 2867200 | tf_op jit(solution)/shard_map/reduce_scatter | solution.py:469
  142.0 19.9 %collective-permute-start.20 = (bf16[224,1280]{1,0:T(8,128)(2,1)}, bf16[224,1280]{1,0:T(8,128)(2,1)}, u32[]{:S(2)}, u32[]{:S(2)}) collective-permute-start(bf16[224,1280]{1,0:T(8,128)(2,1)} %pad.15), channel_id=1, source_target_pairs={{0,1},{1,2},{2,3},{3,0},{4,5},{5,6},{6,7},{7,4},{8,9},{9,10},{10,1... | collective-permute-start | bytes 1720328 | tf_op jit(solution)/shard_map/ppermute | solution.py:32
  142.0 50.7 %collective-permute-start.21 = (bf16[224,1280]{1,0:T(8,128)(2,1)}, bf16[224,1280]{1,0:T(8,128)(2,1)}, u32[]{:S(2)}, u32[]{:S(2)}) collective-permute-start(bf16[224,1280]{1,0:T(8,128)(2,1)} %pad.15), channel_id=1, source_target_pairs={{0,2},{1,3},{2,0},{3,1},{4,6},{5,7},{6,4},{7,5},{8,10},{9,11},{10,... | collective-permute-start | bytes 1720328 | tf_op jit(solution)/shard_map/ppermute | solution.py:32
  142.0 50.7 %collective-permute-start.22 = (bf16[224,1280]{1,0:T(8,128)(2,1)}, bf16[224,1280]{1,0:T(8,128)(2,1)}, u32[]{:S(2)}, u32[]{:S(2)}) collective-permute-start(bf16[224,1280]{1,0:T(8,128)(2,1)} %pad.15), channel_id=1, source_target_pairs={{0,3},{1,0},{2,1},{3,2},{4,7},{5,4},{6,5},{7,6},{8,11},{9,8},{10,9... | collective-permute-start | bytes 1720328 | tf_op jit(solution)/shard_map/ppermute | solution.py:32
  147.2 45.5 %collective-permute-start.19 = (bf16[2,224,1280]{2,1,0:T(8,128)(2,1)}, bf16[2,224,1280]{2,1,0:T(8,128)(2,1)}, u32[]{:S(2)}, u32[]{:S(2)}) collective-permute-start(bf16[2,224,1280]{2,1,0:T(8,128)(2,1)} %get-tuple-element.464), channel_id=1, source_target_pairs={{0,8},{8,0},{1,9},{9,1},{2,10},{10,2},{3,11},{11,3},{4,12},{12,4},... | collective-permute-start | bytes 3440648 | tf_op jit(solution)/shard_map/ppermute | solution.py:32
  192.7 41.5 %collective-permute-start.29 = (bf16[224,1280]{1,0:T(8,128)(2,1)}, bf16[224,1280]{1,0:T(8,128)(2,1)}, u32[]{:S(2)}, u32[]{:S(2)}) collective-permute-start(bf16[224,1280]{1,0:T(8,128)(2,1)} %pad.16), channel_id=1, source_target_pairs={{0,2},{1,3},{2,0},{3,1},{4,6},{5,7},{6,4},{7,5},{8,10},{9,11},{10,... | collective-permute-start | bytes 1720328 | tf_op jit(solution)/shard_map/ppermute | solution.py:32
  195.8 38.4 %collective-permute-start.30 = (bf16[224,1280]{1,0:T(8,128)(2,1)}, bf16[224,1280]{1,0:T(8,128)(2,1)}, u32[]{:S(2)}, u32[]{:S(2)}) collective-permute-start(bf16[224,1280]{1,0:T(8,128)(2,1)} %pad.16), channel_id=1, source_target_pairs={{0,3},{1,0},{2,1},{3,2},{4,7},{5,4},{6,5},{7,6},{8,11},{9,8},{10,9... | collective-permute-start | bytes 1720328 | tf_op jit(solution)/shard_map/ppermute | solution.py:32
  195.8 39.3 %collective-permute-start.28 = (bf16[224,1280]{1,0:T(8,128)(2,1)}, bf16[224,1280]{1,0:T(8,128)(2,1)}, u32[]{:S(2)}, u32[]{:S(2)}) collective-permute-start(bf16[224,1280]{1,0:T(8,128)(2,1)} %pad.16), channel_id=1, source_target_pairs={{0,1},{1,2},{2,3},{3,0},{4,5},{5,6},{6,7},{7,4},{8,9},{9,10},{10,1... | collective-permute-start | bytes 1720328 | tf_op jit(solution)/shard_map/ppermute | solution.py:32
  209.4 52.4 %collective-permute-start.25 = (bf16[4,224,1280]{2,1,0:T(8,128)(2,1)S(1)}, bf16[4,224,1280]{2,1,0:T(8,128)(2,1)}, u32[]{:S(2)}, u32[]{:S(2)}) collective-permute-start(bf16[4,224,1280]{2,1,0:T(8,128)(2,1)S(1)} %bitcast.335), channel_id=1, source_target_pairs={{0,16},{16,0},{1,17},{17,1},{2,18},{18,2},{3,19},{19,3},{4,20},{20... | collective-permute-start | bytes 6881288 | tf_op jit(solution)/shard_map/ppermute | solution.py:32
  211.9 27.8 %collective-permute-start.27 = (bf16[2,224,1280]{2,1,0:T(8,128)(2,1)S(1)}, bf16[2,224,1280]{2,1,0:T(8,128)(2,1)S(1)}, u32[]{:S(2)}, u32[]{:S(2)}) collective-permute-start(bf16[2,224,1280]{2,1,0:T(8,128)(2,1)S(1)} %fusion.37), channel_id=1, source_target_pairs={{0,8},{8,0},{1,9},{9,1},{2,10},{10,2},{3,11},{11,3},{4,12},{12,4},... | collective-permute-start | bytes 3440648 | tf_op jit(solution)/shard_map/ppermute | solution.py:32
  263.3 10.7 %collective-permute-start.33 = (bf16[2,224,1280]{2,1,0:T(8,128)(2,1)S(1)}, bf16[2,224,1280]{2,1,0:T(8,128)(2,1)S(1)}, u32[]{:S(2)}, u32[]{:S(2)}) collective-permute-start(bf16[2,224,1280]{2,1,0:T(8,128)(2,1)S(1)} %dynamic-slice_bitcast_fusion.6), channel_id=1, source_target_pairs={{0,4},{4,0},{1,5},{5,1},{2,6},{6,2},{3,7},{7,3},{8,12},{12,8},{9,1... | collective-permute-start | bytes 3440648 | tf_op jit(solution)/shard_map/ppermute | solution.py:32
  263.4 52.5 %collective-permute-start.35 = (bf16[4,224,1280]{2,1,0:T(8,128)(2,1)}, bf16[4,224,1280]{2,1,0:T(8,128)(2,1)S(1)}, u32[]{:S(2)}, u32[]{:S(2)}) collective-permute-start(bf16[4,224,1280]{2,1,0:T(8,128)(2,1)} %bitcast.337), channel_id=1, source_target_pairs={{0,16},{16,0},{1,17},{17,1},{2,18},{18,2},{3,19},{19,3},{4,20},{20... | collective-permute-start | bytes 6881288 | tf_op jit(solution)/shard_map/ppermute | solution.py:32
  274.7 27.4 %collective-permute-start.34 = (bf16[2,224,1280]{2,1,0:T(8,128)(2,1)S(1)}, bf16[2,224,1280]{2,1,0:T(8,128)(2,1)S(1)}, u32[]{:S(2)}, u32[]{:S(2)}) collective-permute-start(bf16[2,224,1280]{2,1,0:T(8,128)(2,1)S(1)} %get-tuple-element.452), channel_id=1, source_target_pairs={{0,8},{8,0},{1,9},{9,1},{2,10},{10,2},{3,11},{11,3},{4,12},{12,4},... | collective-permute-start | bytes 3440648 | tf_op jit(solution)/shard_map/ppermute | solution.py:32
  315.9 41.7 %collective-permute-start.37 = (bf16[512,1792]{1,0:T(8,128)(2,1)S(1)}, bf16[512,1792]{1,0:T(8,128)(2,1)}, u32[]{:S(2)}, u32[]{:S(2)}) collective-permute-start(bf16[512,1792]{1,0:T(8,128)(2,1)S(1)} %multiply_convert_fusion.1.refs_0_.refs_1_), channel_id=1, source_target_pairs={{0,8},{8,0},{1,9},{9,1},{2,10},{10,2},{3,11},{11,3},{4,12},{12,4},... | collective-permute-start | bytes 5505032 | tf_op jit(solution)/shard_map/ppermute | solution.py:32
  316.8 52.4 %collective-permute-start.36 = (bf16[4,224,1280]{2,1,0:T(8,128)(2,1)S(1)}, bf16[4,224,1280]{2,1,0:T(8,128)(2,1)}, u32[]{:S(2)}, u32[]{:S(2)}) collective-permute-start(bf16[4,224,1280]{2,1,0:T(8,128)(2,1)S(1)} %bitcast.339), channel_id=1, source_target_pairs={{0,16},{16,0},{1,17},{17,1},{2,18},{18,2},{3,19},{19,3},{4,20},{20... | collective-permute-start | bytes 6881288 | tf_op jit(solution)/shard_map/ppermute | solution.py:32
  372.7 22.9 %collective-permute-start.31 = (bf16[512,1792]{1,0:T(8,128)(2,1)S(1)}, bf16[512,1792]{1,0:T(8,128)(2,1)}, u32[]{:S(2)}, u32[]{:S(2)}) collective-permute-start(bf16[512,1792]{1,0:T(8,128)(2,1)S(1)} %bitcast.324), channel_id=1, source_target_pairs={{0,4},{4,0},{1,5},{5,1},{2,6},{6,2},{3,7},{7,3},{8,12},{12,8},{9,1... | collective-permute-start | bytes 5505032 | tf_op jit(solution)/shard_map/ppermute | solution.py:32
  373.3 22.4 %collective-permute-start.32 = (bf16[512,1792]{1,0:T(8,128)(2,1)}, bf16[512,1792]{1,0:T(8,128)(2,1)}, u32[]{:S(2)}, u32[]{:S(2)}) collective-permute-start(bf16[512,1792]{1,0:T(8,128)(2,1)} %collective-permute-done.7.refs_3_.refs_0_), channel_id=1, source_target_pairs={{0,4},{4,0},{1,5},{5,1},{2,6},{6,2},{3,7},{7,3},{8,12},{12,8},{9,1... | collective-permute-start | bytes 5505032 | tf_op jit(solution)/shard_map/ppermute | solution.py:32
  404.9 71.8 %collective-permute-start.40 = (bf16[896,1280]{1,0:T(8,128)(2,1)}, bf16[896,1280]{1,0:T(8,128)(2,1)}, u32[]{:S(2)}, u32[]{:S(2)}) collective-permute-start(bf16[896,1280]{1,0:T(8,128)(2,1)} %gradient_half.6), channel_id=1, source_target_pairs={{0,16},{16,0},{1,17},{17,1},{2,18},{18,2},{3,19},{19,3},{4,20},{20... | collective-permute-start | bytes 6881288 | tf_op jit(solution)/shard_map/ppermute | solution.py:32
  435.3 41.5 %collective-permute-start.41 = (bf16[512,1792]{1,0:T(8,128)(2,1)}, bf16[512,1792]{1,0:T(8,128)(2,1)}, u32[]{:S(2)}, u32[]{:S(2)}) collective-permute-start(bf16[512,1792]{1,0:T(8,128)(2,1)} %get-tuple-element.290), channel_id=1, source_target_pairs={{0,4},{4,0},{1,5},{5,1},{2,6},{6,2},{3,7},{7,3},{8,12},{12,8},{9,1... | collective-permute-start | bytes 5505032 | tf_op jit(solution)/shard_map/ppermute | solution.py:32
  435.5 41.3 %collective-permute-start.42 = (bf16[512,1792]{1,0:T(8,128)(2,1)}, bf16[512,1792]{1,0:T(8,128)(2,1)}, u32[]{:S(2)}, u32[]{:S(2)}) collective-permute-start(bf16[512,1792]{1,0:T(8,128)(2,1)} %get-tuple-element.292), channel_id=1, source_target_pairs={{0,4},{4,0},{1,5},{5,1},{2,6},{6,2},{3,7},{7,3},{8,12},{12,8},{9,1... | collective-permute-start | bytes 5505032 | tf_op jit(solution)/shard_map/ppermute | solution.py:32
  465.9 60.4 %collective-permute-start.45 = (bf16[512,1792]{1,0:T(8,128)(2,1)}, bf16[512,1792]{1,0:T(8,128)(2,1)}, u32[]{:S(2)}, u32[]{:S(2)}) collective-permute-start(bf16[512,1792]{1,0:T(8,128)(2,1)} %get-tuple-element.301), channel_id=1, source_target_pairs={{0,4},{4,0},{1,5},{5,1},{2,6},{6,2},{3,7},{7,3},{8,12},{12,8},{9,1... | collective-permute-start | bytes 5505032 | tf_op jit(solution)/shard_map/ppermute | solution.py:32
  466.2 60.2 %collective-permute-start.46 = (bf16[512,1792]{1,0:T(8,128)(2,1)}, bf16[512,1792]{1,0:T(8,128)(2,1)}, u32[]{:S(2)}, u32[]{:S(2)}) collective-permute-start(bf16[512,1792]{1,0:T(8,128)(2,1)} %get-tuple-element.303), channel_id=1, source_target_pairs={{0,4},{4,0},{1,5},{5,1},{2,6},{6,2},{3,7},{7,3},{8,12},{12,8},{9,1... | collective-permute-start | bytes 5505032 | tf_op jit(solution)/shard_map/ppermute | solution.py:32
  476.8 52.4 %collective-permute-start.43 = (bf16[896,1280]{1,0:T(8,128)(2,1)}, bf16[896,1280]{1,0:T(8,128)(2,1)}, u32[]{:S(2)}, u32[]{:S(2)}) collective-permute-start(bf16[896,1280]{1,0:T(8,128)(2,1)} %gradient_half.7), channel_id=1, source_target_pairs={{0,16},{16,0},{1,17},{17,1},{2,18},{18,2},{3,19},{19,3},{4,20},{20... | collective-permute-start | bytes 6881288 | tf_op jit(solution)/shard_map/ppermute | solution.py:32
  481.5 44.9 %collective-permute-start.44 = (bf16[512,1792]{1,0:T(8,128)(2,1)}, bf16[512,1792]{1,0:T(8,128)(2,1)}, u32[]{:S(2)}, u32[]{:S(2)}) collective-permute-start(bf16[512,1792]{1,0:T(8,128)(2,1)} %add_convert_fusion.5), channel_id=1, source_target_pairs={{0,8},{8,0},{1,9},{9,1},{2,10},{10,2},{3,11},{11,3},{4,12},{12,4},... | collective-permute-start | bytes 5505032 | tf_op jit(solution)/shard_map/ppermute | solution.py:32
  494.8 113.1 %reduce-scatter.6.cloned.1.call-start = ((), (), s32[]{:S(2)}) async-start(), calls=%async_computation.7 | async-start | bytes 2867200 | tf_op jit(solution)/shard_map/reduce_scatter | solution.py:469
  529.1 51.5 %collective-permute-start.47 = (bf16[896,1280]{1,0:T(8,128)(2,1)}, bf16[896,1280]{1,0:T(8,128)(2,1)}, u32[]{:S(2)}, u32[]{:S(2)}) collective-permute-start(bf16[896,1280]{1,0:T(8,128)(2,1)} %gradient_half.8), channel_id=1, source_target_pairs={{0,16},{16,0},{1,17},{17,1},{2,18},{18,2},{3,19},{19,3},{4,20},{20... | collective-permute-start | bytes 6881288 | tf_op jit(solution)/shard_map/ppermute | solution.py:32
  530.6 49.3 %collective-permute-start.48 = (bf16[512,1792]{1,0:T(8,128)(2,1)}, bf16[512,1792]{1,0:T(8,128)(2,1)}, u32[]{:S(2)}, u32[]{:S(2)}) collective-permute-start(bf16[512,1792]{1,0:T(8,128)(2,1)} %add_convert_fusion.4), channel_id=1, source_target_pairs={{0,8},{8,0},{1,9},{9,1},{2,10},{10,2},{3,11},{11,3},{4,12},{12,4},... | collective-permute-start | bytes 5505032 | tf_op jit(solution)/shard_map/ppermute | solution.py:32
  558.8 142.7 %reduce-scatter.8.cloned.1.call-start = ((), (), s32[]{:S(2)}) async-start(), calls=%async_computation.8 | async-start | bytes 2867200 | tf_op jit(solution)/shard_map/reduce_scatter | solution.py:469
  580.6 27.3 %collective-permute-start.49 = (bf16[4,224,1792]{2,1,0:T(8,128)(2,1)}, bf16[4,224,1792]{2,1,0:T(8,128)(2,1)}, u32[]{:S(2)}, u32[]{:S(2)}) collective-permute-start(bf16[4,224,1792]{2,1,0:T(8,128)(2,1)} %copy-done.21), channel_id=1, source_target_pairs={{0,4},{4,0},{1,5},{5,1},{2,6},{6,2},{3,7},{7,3},{8,12},{12,8},{9,1... | collective-permute-start | bytes 9633800 | tf_op jit(solution)/shard_map/ppermute | solution.py:32
  580.6 27.3 %collective-permute-start.50 = (bf16[4,224,1792]{2,1,0:T(8,128)(2,1)}, bf16[4,224,1792]{2,1,0:T(8,128)(2,1)}, u32[]{:S(2)}, u32[]{:S(2)}) collective-permute-start(bf16[4,224,1792]{2,1,0:T(8,128)(2,1)} %copy-done.22), channel_id=1, source_target_pairs={{0,4},{4,0},{1,5},{5,1},{2,6},{6,2},{3,7},{7,3},{8,12},{12,8},{9,1... | collective-permute-start | bytes 9633800 | tf_op jit(solution)/shard_map/ppermute | solution.py:32
  611.0 61.2 %collective-permute-start.51 = (bf16[2,224,1792]{2,1,0:T(8,128)(2,1)}, bf16[2,224,1792]{2,1,0:T(8,128)(2,1)}, u32[]{:S(2)}, u32[]{:S(2)}) collective-permute-start(bf16[2,224,1792]{2,1,0:T(8,128)(2,1)} %fusion.25), channel_id=1, source_target_pairs={{0,8},{8,0},{1,9},{9,1},{2,10},{10,2},{3,11},{11,3},{4,12},{12,4},... | collective-permute-start | bytes 4816904 | tf_op jit(solution)/shard_map/ppermute | solution.py:32
  615.2 57.0 %collective-permute-start.52 = (bf16[2,224,1792]{2,1,0:T(8,128)(2,1)}, bf16[2,224,1792]{2,1,0:T(8,128)(2,1)}, u32[]{:S(2)}, u32[]{:S(2)}) collective-permute-start(bf16[2,224,1792]{2,1,0:T(8,128)(2,1)} %fusion.26), channel_id=1, source_target_pairs={{0,16},{16,0},{1,17},{17,1},{2,18},{18,2},{3,19},{19,3},{4,20},{20... | collective-permute-start | bytes 4816904 | tf_op jit(solution)/shard_map/ppermute | solution.py:32
  625.0 47.2 %collective-permute-start.53 = (bf16[224,1280]{1,0:T(8,128)(2,1)}, bf16[224,1280]{1,0:T(8,128)(2,1)}, u32[]{:S(2)}, u32[]{:S(2)}) collective-permute-start(bf16[224,1280]{1,0:T(8,128)(2,1)} %reduce-scatter.4.cloned.1.call-done), channel_id=1, source_target_pairs={{0,0},{8,1},{4,2},{12,3},{1,4},{9,5},{5,6},{13,7},{2,8},{10,9},{6,... | collective-permute-start | bytes 1720328 | tf_op jit(solution)/shard_map/ppermute | solution.py:114
  672.2 16.6 %collective-permute-start.54 = (bf16[4,224,1792]{2,1,0:T(8,128)(2,1)}, bf16[4,224,1792]{2,1,0:T(8,128)(2,1)}, u32[]{:S(2)}, u32[]{:S(2)}) collective-permute-start(bf16[4,224,1792]{2,1,0:T(8,128)(2,1)} %get-tuple-element.352), channel_id=1, source_target_pairs={{0,4},{4,0},{1,5},{5,1},{2,6},{6,2},{3,7},{7,3},{8,12},{12,8},{9,1... | collective-permute-start | bytes 9633800 | tf_op jit(solution)/shard_map/ppermute | solution.py:32
  677.5 46.9 %collective-permute-start.57 = (bf16[224,1792]{1,0:T(8,128)(2,1)}, bf16[224,1792]{1,0:T(8,128)(2,1)}, u32[]{:S(2)}, u32[]{:S(2)}) collective-permute-start(bf16[224,1792]{1,0:T(8,128)(2,1)} %fusion.28), channel_id=1, source_target_pairs={{0,8},{8,0},{1,9},{9,1},{2,10},{10,2},{3,11},{11,3},{4,12},{12,4},... | collective-permute-start | bytes 2408456 | tf_op jit(solution)/shard_map/ppermute | solution.py:32
  680.3 44.1 %collective-permute-start.58 = (bf16[224,1792]{1,0:T(8,128)(2,1)}, bf16[224,1792]{1,0:T(8,128)(2,1)}, u32[]{:S(2)}, u32[]{:S(2)}) collective-permute-start(bf16[224,1792]{1,0:T(8,128)(2,1)} %fusion.27), channel_id=1, source_target_pairs={{0,16},{16,0},{1,17},{17,1},{2,18},{18,2},{3,19},{19,3},{4,20},{20... | collective-permute-start | bytes 2408456 | tf_op jit(solution)/shard_map/ppermute | solution.py:32
  684.1 35.9 %collective-permute-start.59 = (bf16[224,1280]{1,0:T(8,128)(2,1)}, bf16[224,1280]{1,0:T(8,128)(2,1)}, u32[]{:S(2)}, u32[]{:S(2)}) collective-permute-start(bf16[224,1280]{1,0:T(8,128)(2,1)} %reduce-scatter.6.cloned.1.call-done), channel_id=1, source_target_pairs={{0,0},{8,1},{4,2},{12,3},{1,4},{9,5},{5,6},{13,7},{2,8},{10,9},{6,... | collective-permute-start | bytes 1720328 | tf_op jit(solution)/shard_map/ppermute | solution.py:114
  693.5 36.7 %collective-permute-start.55 = (bf16[2,224,1280]{2,1,0:T(8,128)(2,1)}, bf16[2,224,1280]{2,1,0:T(8,128)(2,1)}, u32[]{:S(2)}, u32[]{:S(2)}) collective-permute-start(bf16[2,224,1280]{2,1,0:T(8,128)(2,1)} %fusion.31), channel_id=1, source_target_pairs={{0,16},{16,0},{1,17},{17,1},{2,18},{18,2},{3,19},{19,3},{4,20},{20... | collective-permute-start | bytes 3440648 | tf_op jit(solution)/shard_map/ppermute | solution.py:32
  701.4 24.6 %collective-permute-start.60 = (bf16[224,1280]{1,0:T(8,128)(2,1)}, bf16[224,1280]{1,0:T(8,128)(2,1)S(1)}, u32[]{:S(2)}, u32[]{:S(2)}) collective-permute-start(bf16[224,1280]{1,0:T(8,128)(2,1)} %reduce-scatter.8.cloned.1.call-done), channel_id=1, source_target_pairs={{0,0},{8,1},{4,2},{12,3},{1,4},{9,5},{5,6},{13,7},{2,8},{10,9},{6,... | collective-permute-start | bytes 1720328 | tf_op jit(solution)/shard_map/ppermute | solution.py:114
  737.8 47.4 %collective-permute-start.62 = (bf16[224,1280]{1,0:T(8,128)(2,1)S(1)}, bf16[224,1280]{1,0:T(8,128)(2,1)}, u32[]{:S(2)}, u32[]{:S(2)}) collective-permute-start(bf16[224,1280]{1,0:T(8,128)(2,1)S(1)} %fusion.44), channel_id=1, source_target_pairs={{0,8},{8,0},{1,9},{9,1},{2,10},{10,2},{3,11},{11,3},{4,12},{12,4},... | collective-permute-start | bytes 1720328 | tf_op jit(solution)/shard_map/ppermute | solution.py:32
  742.4 13.3 %collective-permute-start.67 = (f32[2,5,4,56]{3,2,1,0:T(4,128)S(1)}, f32[2,5,4,56]{3,2,1,0:T(4,128)S(1)}, u32[]{:S(2)}, u32[]{:S(2)}) collective-permute-start(f32[2,5,4,56]{3,2,1,0:T(4,128)S(1)} %bitcast_add_fusion.5), channel_id=1, source_target_pairs={{0,16},{16,0},{1,17},{17,1},{2,18},{18,2},{3,19},{19,3},{4,20},{20... | collective-permute-start | bytes 26888 | tf_op jit(solution)/shard_map/ppermute | solution.py:32
  751.6 15.6 %collective-permute-start.64 = (bf16[448,448]{1,0:T(8,128)(2,1)S(1)}, bf16[448,448]{1,0:T(8,128)(2,1)S(1)}, u32[]{:S(2)}, u32[]{:S(2)}) collective-permute-start(bf16[448,448]{1,0:T(8,128)(2,1)S(1)} %get-tuple-element.472), channel_id=1, source_target_pairs={{0,3},{1,0},{2,1},{3,2},{4,7},{5,4},{6,5},{7,6},{8,11},{9,8},{10,9... | collective-permute-start | bytes 1204232 | tf_op jit(solution)/shard_map/ppermute | solution.py:32
  751.9 33.4 %collective-permute-start.65 = (bf16[448,448]{1,0:T(8,128)(2,1)S(1)}, bf16[448,448]{1,0:T(8,128)(2,1)S(1)}, u32[]{:S(2)}, u32[]{:S(2)}) collective-permute-start(bf16[448,448]{1,0:T(8,128)(2,1)S(1)} %get-tuple-element.471), channel_id=1, source_target_pairs={{0,2},{1,3},{2,0},{3,1},{4,6},{5,7},{6,4},{7,5},{8,10},{9,11},{10,... | collective-permute-start | bytes 1204232 | tf_op jit(solution)/shard_map/ppermute | solution.py:32
  751.9 33.3 %collective-permute-start.66 = (bf16[448,448]{1,0:T(8,128)(2,1)S(1)}, bf16[448,448]{1,0:T(8,128)(2,1)S(1)}, u32[]{:S(2)}, u32[]{:S(2)}) collective-permute-start(bf16[448,448]{1,0:T(8,128)(2,1)S(1)} %get-tuple-element.470), channel_id=1, source_target_pairs={{0,1},{1,2},{2,3},{3,0},{4,5},{5,6},{6,7},{7,4},{8,9},{9,10},{10,1... | collective-permute-start | bytes 1204232 | tf_op jit(solution)/shard_map/ppermute | solution.py:32
  790.3 16.5 %collective-permute-start.71 = (bf16[232,448]{1,0:T(8,128)(2,1)S(1)}, bf16[232,448]{1,0:T(8,128)(2,1)S(1)}, u32[]{:S(2)}, u32[]{:S(2)}) collective-permute-start(bf16[232,448]{1,0:T(8,128)(2,1)S(1)} %get-tuple-element.484), channel_id=1, source_target_pairs={{0,1},{1,2},{2,3},{3,0},{4,5},{5,6},{6,7},{7,4},{8,9},{9,10},{10,1... | collective-permute-start | bytes 623624 | tf_op jit(solution)/shard_map/ppermute | solution.py:32
  794.8 26.4 %collective-permute-start.70 = (bf16[232,448]{1,0:T(8,128)(2,1)S(1)}, bf16[232,448]{1,0:T(8,128)(2,1)S(1)}, u32[]{:S(2)}, u32[]{:S(2)}) collective-permute-start(bf16[232,448]{1,0:T(8,128)(2,1)S(1)} %get-tuple-element.485), channel_id=1, source_target_pairs={{0,2},{1,3},{2,0},{3,1},{4,6},{5,7},{6,4},{7,5},{8,10},{9,11},{10,... | collective-permute-start | bytes 623624 | tf_op jit(solution)/shard_map/ppermute | solution.py:32
  801.1 20.1 %collective-permute-start.69 = (bf16[232,448]{1,0:T(8,128)(2,1)S(1)}, bf16[232,448]{1,0:T(8,128)(2,1)S(1)}, u32[]{:S(2)}, u32[]{:S(2)}) collective-permute-start(bf16[232,448]{1,0:T(8,128)(2,1)S(1)} %get-tuple-element.483), channel_id=1, source_target_pairs={{0,3},{1,0},{2,1},{3,2},{4,7},{5,4},{6,5},{7,6},{8,11},{9,8},{10,9... | collective-permute-start | bytes 623624 | tf_op jit(solution)/shard_map/ppermute | solution.py:32
  (117 other events, 980.2 us)
Sparse Core Ops, SparseCore 0:
  50.7 46.0 all-gather.5
  99.5 46.0 all-gather.7
  148.0 55.4 all-gather.9
  494.9 46.3 reduce-scatter.3
  558.9 48.0 reduce-scatter.5
  631.0 55.4 reduce-scatter.7
